TPU v7x, 32 devices: a whole 2x2x4 slice. The times are simulated.
32 devices in a mesh: dp: 8 (over z, core), tensor: 4 (over y, x).
Axes of the slice: x: 2, y: 2, z: 4, core: 2. Of those that a mesh axis runs over, the one named last changes fastest.
Arguments:
- tokens: bfloat16 [32768, 1024], P(('dp', 'tensor')), may hold values from -6 to 6
- lengths: int32 [16], P('dp'), may hold values from 512 to 2048, as said below
- out_grad: bfloat16 [32768, 1024], P(('dp', 'tensor')), may hold values from -6 to 6
- ln1_gain: float32 [1024], replicated, may hold values from 0.5 to 1.5
- ln2_gain: float32 [1024], replicated, may hold values from 0.5 to 1.5
- onorm_gain: float32 [128], replicated, may hold values from 0.5 to 1.5
- a_log: float32 [8], replicated, may hold values from -6 to 0.5
- dt_bias: float32 [8], replicated, may hold values from -4 to 0
- w_query: bfloat16 [1024, 1024], P('dp', 'tensor'), may hold values from -0.1875 to 0.1875
- w_key: bfloat16 [1024, 2048], P('dp', 'tensor'), may hold values from -0.1875 to 0.1875
- w_value: bfloat16 [1024, 2048], P('dp', 'tensor'), may hold values from -0.1875 to 0.1875
- w_rates: bfloat16 [1024, 24], P('dp', 'tensor'), may hold values from -0.1875 to 0.1875
- w_outgate: bfloat16 [1024, 1024], P('dp', 'tensor'), may hold values from -0.1875 to 0.1875
- w_out: bfloat16 [1024, 1024], P('tensor', 'dp'), may hold values from -0.375 to 0.375
- w_gate: bfloat16 [1024, 2816], P('dp', 'tensor'), may hold values from -0.1875 to 0.1875
- w_up: bfloat16 [1024, 2816], P('dp', 'tensor'), may hold values from -0.1875 to 0.1875
- w_down: bfloat16 [2816, 1024], P('tensor', 'dp'), may hold values from -0.21875 to 0.21875
Outputs:
- block_out: bfloat16 [32768, 1024], P(('dp', 'tensor'))
- tokens_grad: bfloat16 [32768, 1024], P(('dp', 'tensor'))
- ln1_gain_grad: float32 [1024], replicated
- ln2_gain_grad: float32 [1024], replicated
- onorm_gain_grad: float32 [128], replicated
- a_log_grad: float32 [8], replicated
- dt_bias_grad: float32 [8], replicated
- w_query_grad: float32 [1024, 1024], P('dp', 'tensor')
- w_key_grad: float32 [1024, 2048], P('dp', 'tensor')
- w_value_grad: float32 [1024, 2048], P('dp', 'tensor')
- w_rates_grad: float32 [1024, 24], P('dp', 'tensor')
- w_outgate_grad: float32 [1024, 1024], P('dp', 'tensor')
- w_out_grad: float32 [1024, 1024], P('tensor', 'dp')
- w_gate_grad: float32 [1024, 2816], P('dp', 'tensor')
- w_up_grad: float32 [1024, 2816], P('dp', 'tensor')
- w_down_grad: float32 [2816, 1024], P('tensor', 'dp')
Inputs may be any that keep to these rules, and one draw needn't show every extreme that they name: `lengths`: valid positions of each sequence; the positions after them are padding; in every draw some sequence has all 2048 positions valid.
All inputs are finite; a program needn't handle non-finite values.
Results may differ from a plain program's by a relative error of at most 0.017.
Values may be sent and summed in bfloat16 or wider, within the bound.
No kernel may reach another device: no remote copies, remote signals or barrier semaphores. Data moves between devices by JAX's collectives and lax.ppermute only.
A program may use at most 448 MiB of HBM per device.

v0:
```python
from functools import partial

import jax
import jax.numpy as jnp
from jax import lax
from jax.sharding import PartitionSpec as P

HEAD = 128
NH = 2
CT = 64
LEN = 2048


HIGH = lax.Precision.HIGHEST
EPS = 1e-06


def project(left, right):
    return jnp.dot(left, right, preferred_element_type=jnp.float32)


def times_trans(left, right):
    return lax.dot_general(
        left, right, (((1,), (1,)), ((), ())), preferred_element_type=jnp.float32
    )


def trans_times(left, right):
    return lax.dot_general(
        left, right, (((0,), (0,)), ((), ())), preferred_element_type=jnp.float32
    )


def rms_parts(values):
    scale = lax.rsqrt(jnp.mean(values * values, axis=-1, keepdims=True) + EPS)
    return (values * scale, scale)


def rms_back(grad_out, values, scale, gain):
    gain_grad = jnp.sum(grad_out * values * scale, axis=0)
    scaled = grad_out * gain
    value_grad = scale * scaled - values * scale * scale * scale * jnp.mean(
        scaled * values, axis=-1, keepdims=True
    )
    return (value_grad, gain_grad)


def unit_rows(values):
    return values * lax.rsqrt(jnp.sum(values * values, axis=-1, keepdims=True) + EPS)


def stretch_mixer(query, keys, values, betas, decays):
    batch, length, heads, width = query.shape
    steps = keys.shape[3]
    vwidth = values.shape[-1]
    span = CT * steps
    nblock = length // CT

    def blocked(array):
        moved = array.reshape((batch, nblock, CT, heads) + array.shape[3:])
        return jnp.moveaxis(jnp.moveaxis(moved, 1, 0), 3, 2)

    queries = blocked(query)
    key_rows = blocked(keys).reshape(nblock, batch, heads, span, width)
    value_rows = blocked(values).reshape(nblock, batch, heads, span, vwidth)
    beta_rows = blocked(betas).reshape(nblock, batch, heads, span)
    log_decay = jnp.concatenate(
        [decays[..., None], jnp.zeros(decays.shape + (steps - 1,), jnp.float32)], axis=-1
    )
    cumul = jnp.cumsum(blocked(log_decay).reshape(nblock, batch, heads, span), axis=-1)
    index = jnp.arange(span)
    strict = index[:, None] > index[None, :]
    apart = cumul[..., :, None] - cumul[..., None, :]
    weights_strict = jnp.where(strict, jnp.exp(jnp.minimum(apart, 0.0)), 0.0)
    intersections = jnp.einsum("nbhid,nbhjd->nbhij", key_rows, key_rows, precision=HIGH)
    lower = (
        jnp.eye(span, dtype=jnp.float32) + weights_strict * intersections * beta_rows[..., None, :]
    )
    growth = jnp.exp(cumul)
    solved = jax.scipy.linalg.solve_triangular(
        lower,
        jnp.concatenate([value_rows, growth[..., None] * key_rows], axis=-1),
        lower=True,
        unit_diagonal=True,
    )
    new_values = solved[..., :vwidth]
    key_mix = solved[..., vwidth:]
    read_at = jnp.arange(CT) * steps + steps - 1
    read_cumul = cumul.reshape(nblock, batch, heads, CT, steps)[..., steps - 1]
    read_apart = read_cumul[..., :, None] - cumul[..., None, :]
    upto = read_at[:, None] >= index[None, :]
    read_weights = jnp.where(upto, jnp.exp(jnp.minimum(read_apart, 0.0)), 0.0)
    scores = (
        jnp.einsum("nbhid,nbhjd->nbhij", queries, key_rows, precision=HIGH)
        * read_weights
        * beta_rows[..., None, :]
    )
    query_decayed = jnp.exp(read_cumul)[..., None] * queries
    tail = cumul[..., span - 1]
    key_out = (jnp.exp(tail[..., None] - cumul) * beta_rows)[..., None] * key_rows

    def advance(carried, block_in):
        new_v, mix_k, score, query_d, key_o, tail_b = block_in
        delta = new_v - jnp.einsum("bhpk,bhkv->bhpv", mix_k, carried, precision=HIGH)
        output = jnp.einsum("bhck,bhkv->bhcv", query_d, carried, precision=HIGH) + jnp.einsum(
            "bhcp,bhpv->bhcv", score, delta, precision=HIGH
        )
        carried = jnp.exp(tail_b)[..., None, None] * carried + jnp.einsum(
            "bhpk,bhpv->bhkv", key_o, delta, precision=HIGH
        )
        return (carried, output)

    initial = jnp.zeros((batch, heads, width, vwidth), jnp.float32)
    last_state, outputs = lax.scan(
        advance, initial, (new_values, key_mix, scores, query_decayed, key_out, tail)
    )
    outputs = jnp.moveaxis(jnp.moveaxis(outputs, 2, 3), 0, 1)
    return outputs.reshape(batch, length, heads, vwidth)


def mixer(query_pre, key_pre, value_pre, rates_pre, outgate_pre, a_here, dt_here, gain, seq_count):
    rows = query_pre.shape[0]
    lead_dims = (seq_count, rows // seq_count)
    heads = a_here.shape[0]
    query = unit_rows(jax.nn.silu(query_pre).reshape(lead_dims + (heads, HEAD)))
    keys = unit_rows(jax.nn.silu(key_pre).reshape(lead_dims + (heads, NH, HEAD)))
    values = jax.nn.silu(value_pre).reshape(lead_dims + (heads, NH, HEAD))
    rates = rates_pre.reshape(lead_dims + (heads, NH + 1))
    betas = jax.nn.sigmoid(rates[..., :NH])
    decays = -jnp.exp(a_here) * jax.nn.softplus(rates[..., NH] + dt_here)
    mixed = stretch_mixer(query, keys, values, betas, decays)
    gate = jax.nn.silu(outgate_pre.reshape(lead_dims + (heads, HEAD)))
    normed = mixed * lax.rsqrt(jnp.mean(mixed * mixed, axis=-1, keepdims=True) + EPS) * gain * gate
    return normed.reshape(rows, heads * HEAD)


def per_device(
    tokens,
    lengths,
    out_grad,
    ln1_gain,
    ln2_gain,
    onorm_gain,
    a_log,
    dt_bias,
    w_query,
    w_key,
    w_value,
    w_rates,
    w_outgate,
    w_out,
    w_gate,
    w_up,
    w_down,
):
    tensor_count = lax.axis_size("tensor")
    tensor_pos = lax.axis_index("tensor")
    tok_dev = tokens.shape[0]
    seq_count = lengths.shape[0]
    heads_here = a_log.shape[0] // tensor_count
    positions = tensor_pos * tok_dev + jnp.arange(tok_dev)
    owners = positions // LEN
    limits = jnp.sum(
        jnp.where(owners[:, None] == jnp.arange(seq_count)[None, :], lengths[None, :], 0), axis=1
    )
    mask = (positions % LEN < limits).astype(jnp.float32)[:, None]
    full_query, full_key, full_value, full_rates, full_outgate, full_out = (
        lax.all_gather(w_query, "dp", axis=0, tiled=True),
        lax.all_gather(w_key, "dp", axis=0, tiled=True),
        lax.all_gather(w_value, "dp", axis=0, tiled=True),
        lax.all_gather(w_rates, "dp", axis=0, tiled=True),
        lax.all_gather(w_outgate, "dp", axis=0, tiled=True),
        lax.all_gather(w_out, "dp", axis=1, tiled=True),
    )
    resid_in = tokens.astype(jnp.float32)
    normed_one, scale_one = rms_parts(resid_in)
    first_all = lax.all_gather(
        (normed_one * ln1_gain).astype(jnp.bfloat16), "tensor", axis=0, tiled=True
    )
    query_pre = project(first_all, full_query)
    key_pre = project(first_all, full_key)
    value_pre = project(first_all, full_value)
    rates_pre = project(first_all, full_rates)
    outgate_pre = project(first_all, full_outgate)
    a_here = lax.dynamic_slice_in_dim(a_log, tensor_pos * heads_here, heads_here)
    dt_here = lax.dynamic_slice_in_dim(dt_bias, tensor_pos * heads_here, heads_here)
    mixed, mixer_back = jax.vjp(
        partial(mixer, seq_count=seq_count),
        query_pre,
        key_pre,
        value_pre,
        rates_pre,
        outgate_pre,
        a_here,
        dt_here,
        onorm_gain,
    )
    mixed_low = mixed.astype(jnp.bfloat16)
    attn_sum = lax.psum_scatter(
        project(mixed_low, full_out), "tensor", scatter_dimension=0, tiled=True
    )
    middle = resid_in + attn_sum
    full_gate, full_up, full_down = (
        lax.all_gather(w_gate, "dp", axis=0, tiled=True),
        lax.all_gather(w_up, "dp", axis=0, tiled=True),
        lax.all_gather(w_down, "dp", axis=1, tiled=True),
    )
    normed_two, scale_two = rms_parts(middle)
    second_all = lax.all_gather(
        (normed_two * ln2_gain).astype(jnp.bfloat16), "tensor", axis=0, tiled=True
    )
    gate_pre = project(second_all, full_gate)
    up_pre = project(second_all, full_up)
    gate_sig = jax.nn.sigmoid(gate_pre)
    gate_act = gate_pre * gate_sig
    hidden = (gate_act * up_pre).astype(jnp.bfloat16)
    mlp_sum = lax.psum_scatter(
        project(hidden, full_down).astype(jnp.bfloat16), "tensor", scatter_dimension=0, tiled=True
    ).astype(jnp.float32)
    block_out = ((middle + mlp_sum) * mask).astype(jnp.bfloat16)
    grad_top = out_grad.astype(jnp.float32) * mask
    grad_all = lax.all_gather(grad_top.astype(jnp.bfloat16), "tensor", axis=0, tiled=True)
    hidden_grad = times_trans(grad_all, full_down)
    down_grad = trans_times(hidden, grad_all)
    up_grad_pre = (hidden_grad * gate_act).astype(jnp.bfloat16)
    gate_grad_pre = (hidden_grad * up_pre * gate_sig * (1.0 + gate_pre * (1.0 - gate_sig))).astype(
        jnp.bfloat16
    )
    gate_grad = trans_times(second_all, gate_grad_pre)
    up_grad = trans_times(second_all, up_grad_pre)
    second_grad = lax.psum_scatter(
        times_trans(gate_grad_pre, full_gate) + times_trans(up_grad_pre, full_up),
        "tensor",
        scatter_dimension=0,
        tiled=True,
    )
    middle_back, ln2_grad = rms_back(second_grad, middle, scale_two, ln2_gain)
    middle_grad = grad_top + middle_back
    middle_low = middle_grad.astype(jnp.bfloat16)
    middle_all = lax.all_gather(middle_low, "tensor", axis=0, tiled=True)
    out_proj_grad = trans_times(mixed_low, middle_all)
    mixed_grad = times_trans(middle_all, full_out)
    pulled = mixer_back(mixed_grad)
    pre_grads = tuple((item.astype(jnp.bfloat16) for item in pulled[:5]))
    weights_full = (full_query, full_key, full_value, full_rates, full_outgate)
    proj_grads = tuple((trans_times(first_all, item) for item in pre_grads))
    first_part = times_trans(pre_grads[0], weights_full[0])
    for which in range(1, 5):
        first_part = first_part + times_trans(pre_grads[which], weights_full[which])
    first_grad = lax.psum_scatter(
        first_part.astype(jnp.bfloat16), "tensor", scatter_dimension=0, tiled=True
    ).astype(jnp.float32)
    input_back, ln1_grad = rms_back(first_grad, resid_in, scale_one, ln1_gain)
    tokens_grad = (middle_grad + input_back).astype(jnp.bfloat16)
    a_grad = lax.dynamic_update_slice_in_dim(
        jnp.zeros_like(a_log), pulled[5], tensor_pos * heads_here, 0
    )
    dt_grad = lax.dynamic_update_slice_in_dim(
        jnp.zeros_like(dt_bias), pulled[6], tensor_pos * heads_here, 0
    )
    small = lax.psum((ln1_grad, ln2_grad, pulled[7], a_grad, dt_grad), ("dp", "tensor"))
    summed = (
        lax.psum_scatter(
            proj_grads[0].astype(jnp.bfloat16), "dp", scatter_dimension=0, tiled=True
        ).astype(jnp.float32),
        lax.psum_scatter(
            proj_grads[1].astype(jnp.bfloat16), "dp", scatter_dimension=0, tiled=True
        ).astype(jnp.float32),
        lax.psum_scatter(
            proj_grads[2].astype(jnp.bfloat16), "dp", scatter_dimension=0, tiled=True
        ).astype(jnp.float32),
        lax.psum_scatter(
            proj_grads[3].astype(jnp.bfloat16), "dp", scatter_dimension=0, tiled=True
        ).astype(jnp.float32),
        lax.psum_scatter(
            proj_grads[4].astype(jnp.bfloat16), "dp", scatter_dimension=0, tiled=True
        ).astype(jnp.float32),
        lax.psum_scatter(
            out_proj_grad.astype(jnp.bfloat16), "dp", scatter_dimension=1, tiled=True
        ).astype(jnp.float32),
        lax.psum_scatter(
            gate_grad.astype(jnp.bfloat16), "dp", scatter_dimension=0, tiled=True
        ).astype(jnp.float32),
        lax.psum_scatter(
            up_grad.astype(jnp.bfloat16), "dp", scatter_dimension=0, tiled=True
        ).astype(jnp.float32),
        lax.psum_scatter(
            down_grad.astype(jnp.bfloat16), "dp", scatter_dimension=1, tiled=True
        ).astype(jnp.float32),
    )
    return (
        block_out,
        tokens_grad,
        small[0],
        small[1],
        small[2],
        small[3],
        small[4],
        summed[0],
        summed[1],
        summed[2],
        summed[3],
        summed[4],
        summed[5],
        summed[6],
        summed[7],
        summed[8],
    )


def solution(mesh):
    in_specs = (
        P(("dp", "tensor"), None),
        P("dp"),
        P(("dp", "tensor"), None),
        P(),
        P(),
        P(),
        P(),
        P(),
        P("dp", "tensor"),
        P("dp", "tensor"),
        P("dp", "tensor"),
        P("dp", "tensor"),
        P("dp", "tensor"),
        P("tensor", "dp"),
        P("dp", "tensor"),
        P("dp", "tensor"),
        P("tensor", "dp"),
    )
    out_specs = (
        P(("dp", "tensor"), None),
        P(("dp", "tensor"), None),
        P(),
        P(),
        P(),
        P(),
        P(),
        P("dp", "tensor"),
        P("dp", "tensor"),
        P("dp", "tensor"),
        P("dp", "tensor"),
        P("dp", "tensor"),
        P("tensor", "dp"),
        P("dp", "tensor"),
        P("dp", "tensor"),
        P("tensor", "dp"),
    )
    return jax.shard_map(
        per_device, mesh=mesh, in_specs=in_specs, out_specs=out_specs, check_vma=False
    )
```

profile of v0, /device:TPU:0, one launch (start us, length us, event | category | flops | bytes accessed | tf_op | source)
XLA Modules:
  0.0 3971.7 jit_solution(5733695194731297895)
XLA Ops:
  15.3 14.4 all_gather.40
  29.8 14.7 all_gather.43
  44.6 15.8 all_gather.44
  60.4 14.7 all_gather.45
  75.1 49.1 %all-gather.10.cloned.1.call-done = bf16[4096,1024]{1,0:T(8,128)(2,1)} async-done(((bf16[1024,1024]{1,0:T(8,128)(2,1)}), bf16[4096,1024]{1,0:T(8,128)(2,1)}) %all-gather.10.cloned.1.call-update) | async-done | bytes 8388624 | tf_op jit(solution)/shard_map/all_gather | solution.py:177
  124.2 15.1 fusion.99
  166.4 15.1 multiply_reduce_fusion.4
  185.7 12.3 multiply_bitcast_fusion
  231.3 15.0 fusion.98
  265.2 21.4 fusion.218
  296.1 1259.2 %custom-call.10 = f32[32,2,2,1,128,128]{4,5,3,2,1,0:T(8,128)} custom-call(f32[32,2,2,1,128,128]{5,4,3,2,1,0:T(8,128)} %add_bitcast_fusion), custom_call_target="InvertDiagBlocksLowerTriangular" | custom-call | tf_op jit(solution)/shard_map/jvp(jit(_solve_triangular))/vmap(vmap(vmap()))/triangular_solve | solution.py:80
  1565.6 23.1 fusion.75
  1588.7 11.6 fusion.215
  1616.0 19.6 fusion.153
  1646.7 263.2 %while.48 = (s32[]{:T(128)}, f32[2,2,128,128]{3,2,1,0:T(8,128)S(1)}, f32[32,2,2,64,128]{4,3,2,1,0:T(8,128)}, f32[32,2,2,128,128]{4,3,2,1,0:T(8,128)}, f32[32,2,2...) while((s32[]{:T(128)}, ...), condition=%wide.region_5.6_spmd.clone, body=%wide.region_4.5_spmd.clone.sunk | while | flops 302481408 | bytes 4070101 | solution.py:114
  1951.8 153.5 %reduce-scatter.24.cloned.1.call-done = f32[1024,1024]{1,0:T(8,128)} async-done(((f32[4096,1024]{1,0:T(8,128)}), f32[1024,1024]{1,0:T(8,128)}) %reduce-scatter.24.cloned.1.call-update) | async-done | bytes 4194320 | tf_op jit(solution)/shard_map/reduce_scatter | solution.py:199
  2115.3 18.0 all-gather.18.cloned.1.call-done
  2133.3 88.6 %all-gather.16.cloned.1.call-done = bf16[4096,1024]{1,0:T(8,128)(2,1)} async-done(((bf16[1024,1024]{1,0:T(8,128)(2,1)}), bf16[4096,1024]{1,0:T(8,128)(2,1)}) %all-gather.16.cloned.1.call-update) | async-done | bytes 8388624 | tf_op jit(solution)/shard_map/all_gather | solution.py:209
  2222.0 12.7 fusion.220
  2234.6 15.5 all-gather.20.cloned.1.call-done
  2250.1 12.4 fusion.221
  2262.5 14.4 all-gather.22.cloned.1.call-done
  2277.0 88.8 %all-gather.24.cloned.1.call-done = bf16[4096,1024]{1,0:T(8,128)(2,1)} async-done(((bf16[1024,1024]{1,0:T(8,128)(2,1)}), bf16[4096,1024]{1,0:T(8,128)(2,1)}) %all-gather.24.cloned.1.call-update) | async-done | bytes 8388624 | tf_op jit(solution)/shard_map/all_gather | solution.py:222
  2365.8 22.4 multiply_convert_fusion
  2388.2 13.6 fusion.222
  2401.8 13.7 convolution_add_fusion.5
  2416.8 11.7 convolution_convert_fusion
  2428.6 140.9 %reduce-scatter.28.cloned.1.call-done = f32[1024,1024]{1,0:T(8,128)} async-done(((f32[4096,1024]{1,0:T(8,128)}), f32[1024,1024]{1,0:T(8,128)}) %reduce-scatter.28.cloned.1.call-update) | async-done | bytes 4194320 | tf_op jit(solution)/shard_map/reduce_scatter | solution.py:231
  2574.6 84.4 %reduce-scatter.26.cloned.1.call-done = bf16[1024,1024]{1,0:T(8,128)(2,1)} async-done(((bf16[4096,1024]{1,0:T(8,128)(2,1)}), bf16[1024,1024]{1,0:T(8,128)(2,1)}) %reduce-scatter.26.cloned.1.call-update) | async-done | bytes 2097168 | tf_op jit(solution)/shard_map/reduce_scatter | solution.py:217
  2698.1 12.3 mul.791
  2733.9 20.0 all-gather.26.cloned.1.call-done
  2753.9 13.3 fusion.119
  2804.5 588.0 %while.49 = (s32[]{:T(128)}, f32[2,2,128,128]{3,2,1,0:T(8,128)S(1)}, f32[32,2,2,128,128]{4,3,2,1,0:T(8,128)}, f32[32,2,2,128,128]{4,3,2,1,0:T(8,128)}, f32[32,2,...) while((s32[]{:T(128)}, ...), condition=%wide.region_16.17_spmd.clone, body=%wide.region_14.16_spmd.clone.sunk | while | flops 604766208 | bytes 6826808 | solution.py:114
  3392.5 23.8 fusion.80
  3416.3 21.4 fusion.79
  3437.7 22.1 fusion.93
  3459.8 17.1 fusion.103
  3476.9 19.7 fusion.105
  3496.6 17.3 multiply_reduce_fusion.1
  3520.5 12.4 add_bitcast_fusion.1
  3558.1 24.3 add_add_fusion.1
  3588.3 14.1 multiply_reduce_fusion.3
  3659.7 11.5 reshape.415
  3687.1 14.6 broadcast_in_dim.170
  3732.0 13.7 fusion.84
  3799.6 25.5 add_convert_fusion
  3841.1 76.0 %reduce-scatter.30.cloned.1.call-done = bf16[1024,1024]{1,0:T(8,128)(2,1)} async-done(((bf16[4096,1024]{1,0:T(8,128)(2,1)}), bf16[1024,1024]{1,0:T(8,128)(2,1)}) %reduce-scatter.30.cloned.1.call-update) | async-done | bytes 2097168 | tf_op jit(solution)/shard_map/reduce_scatter | solution.py:250
  3920.3 39.6 all-reduce.7
  (1067 shorter events, 1362.8 us)
Async XLA Ops:
  7.2 67.9 %all-gather.12.cloned.1.call-start = ((), (), s32[]{:S(2)}) async-start(), calls=%async_computation.14 | async-start | bytes 1179648 | tf_op jit(solution)/shard_map/all_gather | solution.py:169
  8.0 36.6 copy-start.88
  8.0 116.2 %all-gather.10.cloned.1.call-start = ((), (), s32[]{:S(2)}) async-start(), calls=%async_computation.13 | async-start | bytes 10485760 | tf_op jit(solution)/shard_map/all_gather | solution.py:177
  10.1 50.2 %copy-start.89 = (bf16[256,128]{1,0:T(8,128)(2,1)S(1)}, bf16[256,128]{1,0:T(8,128)(2,1)}, u32[]{:S(2)}) copy-start(bf16[256,128]{1,0:T(8,128)(2,1)} %param.34) | copy-start | bytes 196612
  13.6 217.7 %all-gather.14.cloned.1.call-start = ((), (), s32[]{:S(2)}) async-start(), calls=%async_computation.15 | async-start | bytes 1179648 | tf_op jit(solution)/shard_map/all_gather | solution.py:170
  14.4 2090.9 %reduce-scatter.24.cloned.1.call-start = ((), (), s32[]{:S(2)}) async-start(), calls=%async_computation.16 | async-start | bytes 20971520 | tf_op jit(solution)/shard_map/reduce_scatter | solution.py:199
  15.2 182.9 %copy-start.98 = (f32[2]{0:T(128)}, f32[2]{0:T(128)S(1)}, u32[]{:S(2)}) copy-start(f32[2]{0:T(128)S(1)} %fusion.204) | copy-start | bytes 28
  15.3 182.8 %copy-start.101 = (f32[2]{0:T(128)}, f32[2]{0:T(128)S(1)}, u32[]{:S(2)}) copy-start(f32[2]{0:T(128)S(1)} %dynamic_slice.110) | copy-start | bytes 28
  29.6 131.0 %copy-start.85 = (bf16[1024,6]{0,1:T(8,128)(2,1)}, bf16[1024,6]{0,1:T(8,128)(2,1)S(1)}, u32[]{:S(2)}) copy-start(bf16[1024,6]{0,1:T(8,128)(2,1)S(1)} %all_gather.40) | copy-start | bytes 36868
  29.7 256.9 %copy-start.79 = (pred[128,128]{1,0:T(8,128)(4,1)}, pred[128,128]{1,0:T(8,128)(4,1)S(1)}, u32[]{:S(2)}) copy-start(pred[128,128]{1,0:T(8,128)(4,1)S(1)} %get-tuple-element.891) | copy-start | bytes 49156
  29.8 256.9 %copy-start.81 = (pred[128,128]{1,0:T(8,128)(4,1)}, pred[128,128]{1,0:T(8,128)(4,1)S(1)}, u32[]{:S(2)}) copy-start(pred[128,128]{1,0:T(8,128)(4,1)S(1)} %get-tuple-element.892) | copy-start | bytes 49156
  44.5 157.4 %copy-start.44 = (bf16[1024,256]{1,0:T(8,128)(2,1)}, bf16[1024,256]{1,0:T(8,128)(2,1)S(1)}, u32[]{:S(2)}) copy-start(bf16[1024,256]{1,0:T(8,128)(2,1)S(1)} %all_gather.43) | copy-start | bytes 1572868
  44.6 1571.4 %copy-start.83 = (pred[64,128]{1,0:T(8,128)(4,1)}, pred[64,128]{1,0:T(8,128)(4,1)S(1)}, u32[]{:S(2)}) copy-start(pred[64,128]{1,0:T(8,128)(4,1)S(1)} %iota_compare_fusion.4) | copy-start | bytes 24580
  166.4 31.7 copy-start.70
  200.4 30.7 copy-start.40
  201.8 1414.2 %copy-start.30 = (f32[32,2,2,128]{3,2,1,0:T(2,128)}, f32[32,2,2,128]{3,2,1,0:T(2,128)S(1)}, u32[]{:S(2)}) copy-start(f32[32,2,2,128]{3,2,1,0:T(2,128)S(1)} %copy.437) | copy-start | bytes 196612
  201.9 1414.1 %copy-start.28 = (f32[32,2,2,128]{3,2,1,0:T(2,128)}, f32[32,2,2,128]{3,2,1,0:T(2,128)S(1)}, u32[]{:S(2)}) copy-start(f32[32,2,2,128]{3,2,1,0:T(2,128)S(1)} %copy.435) | copy-start | bytes 196612
  222.7 1386.3 %copy-start.50 = (f32[32,2,2,128]{0,3,2,1:T(8,128)}, f32[32,2,2,128]{0,3,2,1:T(8,128)S(1)}, u32[]{:S(2)}) copy-start(f32[32,2,2,128]{0,3,2,1:T(8,128)S(1)} %copy.441) | copy-start | bytes 196612
  231.2 1324.1 %copy-start.56 = (f32[32,2,2,128]{3,2,1,0:T(2,128)}, f32[32,2,2,128]{3,2,1,0:T(2,128)S(1)}, u32[]{:S(2)}) copy-start(f32[32,2,2,128]{3,2,1,0:T(2,128)S(1)} %copy.439) | copy-start | bytes 196612
  231.3 1324.1 %copy-start.58 = (f32[32,2,2,128]{3,2,1,0:T(2,128)}, f32[32,2,2,128]{3,2,1,0:T(2,128)S(1)}, u32[]{:S(2)}) copy-start(f32[32,2,2,128]{3,2,1,0:T(2,128)S(1)} %copy.433) | copy-start | bytes 196612
  1951.2 154.1 %copy-start.7 = (bf16[1024,1024]{1,0:T(8,128)(2,1)S(1)}, bf16[1024,1024]{1,0:T(8,128)(2,1)}, u32[]{:S(2)}) copy-start(bf16[1024,1024]{1,0:T(8,128)(2,1)} %param.21) | copy-start | bytes 6291460
  1951.2 182.1 %all-gather.18.cloned.1.call-start = ((), (), s32[]{:S(2)}) async-start(), calls=%async_computation.18 | async-start | bytes 1622016 | tf_op jit(solution)/shard_map/all_gather | solution.py:204
  1951.8 158.3 %copy-start.93 = (f32[1024]{0:T(1024)S(1)}, f32[1024]{0:T(1024)}, u32[]{:S(2)}) copy-start(f32[1024]{0:T(1024)} %param.25) | copy-start | bytes 12292
  1951.8 270.2 %all-gather.16.cloned.1.call-start = ((), (), s32[]{:S(2)}) async-start(), calls=%async_computation.17 | async-start | bytes 10485760 | tf_op jit(solution)/shard_map/all_gather | solution.py:209
  2111.8 138.3 %all-gather.20.cloned.1.call-start = ((), (), s32[]{:S(2)}) async-start(), calls=%async_computation.19 | async-start | bytes 1622016 | tf_op jit(solution)/shard_map/all_gather | solution.py:205
  2112.6 164.4 %all-gather.22.cloned.1.call-start = ((), (), s32[]{:S(2)}) async-start(), calls=%async_computation.20 | async-start | bytes 1622016 | tf_op jit(solution)/shard_map/all_gather | solution.py:206
  2113.3 252.4 %all-gather.24.cloned.1.call-start = ((), (), s32[]{:S(2)}) async-start(), calls=%async_computation.22 | async-start | bytes 10485760 | tf_op jit(solution)/shard_map/all_gather | solution.py:222
  2115.3 454.2 %reduce-scatter.28.cloned.1.call-start = ((), (), s32[]{:S(2)}) async-start(), calls=%async_computation.23 | async-start | bytes 20971520 | tf_op jit(solution)/shard_map/reduce_scatter | solution.py:231
  2262.5 125.7 %copy-start.111 = (bf16[1024,704]{0,1:T(8,128)(2,1)S(1)}, bf16[1024,704]{0,1:T(8,128)(2,1)}, u32[]{:S(2)}) copy-start(bf16[1024,704]{0,1:T(8,128)(2,1)} %all-gather.18.cloned.1.call-done) | copy-start | bytes 4325380
  2415.5 243.5 %reduce-scatter.26.cloned.1.call-start = ((), (), s32[]{:S(2)}) async-start(), calls=%async_computation.21 | async-start | bytes 10485760 | tf_op jit(solution)/shard_map/reduce_scatter | solution.py:217
  2428.6 325.4 %all-gather.26.cloned.1.call-start = ((), (), s32[]{:S(2)}) async-start(), calls=%async_computation.24 | async-start | bytes 10485760 | tf_op jit(solution)/shard_map/all_gather | solution.py:240
  2666.2 1159.0 %reduce-scatter.44.cloned.1.call-start = ((), (), s32[]{:S(2)}) async-start(), calls=%async_computation.32 | async-start | bytes 1769472
  2678.1 1149.1 %reduce-scatter.46.cloned.1.call-start = ((), (), s32[]{:S(2)}) async-start(), calls=%async_computation.33 | async-start | bytes 1769472
  2690.0 1139.1 %reduce-scatter.48.cloned.1.call-start = ((), (), s32[]{:S(2)}) async-start(), calls=%async_computation.34 | async-start | bytes 1769472
  2733.7 1098.0 %reduce-scatter.40.cloned.1.call-start = ((), (), s32[]{:S(2)}) async-start(), calls=%async_computation.30 | async-start | bytes 294912
  3551.9 36.3 slice-start.2
  3558.1 30.1 slice-start.3
  3615.8 217.4 %reduce-scatter.42.cloned.1.call-start = ((), (), s32[]{:S(2)}) async-start(), calls=%async_computation.31 | async-start | bytes 589824
  3630.7 204.1 %reduce-scatter.32.cloned.1.call-start = ((), (), s32[]{:S(2)}) async-start(), calls=%async_computation.26 | async-start | bytes 589824 | tf_op jit(solution)/shard_map/reduce_scatter | solution.py:263
  3677.8 158.5 %reduce-scatter.38.cloned.1.call-start = ((), (), s32[]{:S(2)}) async-start(), calls=%async_computation.29 | async-start | bytes 589824 | tf_op jit(solution)/shard_map/reduce_scatter | solution.py:275
  3731.9 105.9 %reduce-scatter.34.cloned.1.call-start = ((), (), s32[]{:S(2)}) async-start(), calls=%async_computation.27 | async-start | bytes 1179648 | tf_op jit(solution)/shard_map/reduce_scatter | solution.py:266
  3755.7 83.7 %reduce-scatter.36.cloned.1.call-start = ((), (), s32[]{:S(2)}) async-start(), calls=%async_computation.28 | async-start | bytes 1179648 | tf_op jit(solution)/shard_map/reduce_scatter | solution.py:269
  3780.6 136.4 %reduce-scatter.30.cloned.1.call-start = ((), (), s32[]{:S(2)}) async-start(), calls=%async_computation.25 | async-start | bytes 10485760 | tf_op jit(solution)/shard_map/reduce_scatter | solution.py:250
  3825.1 91.9 %copy-start.8 = (bf16[1024,1024]{1,0:T(8,128)(2,1)S(1)}, bf16[1024,1024]{1,0:T(8,128)(2,1)}, u32[]{:S(2)}) copy-start(bf16[1024,1024]{1,0:T(8,128)(2,1)} %param.21) | copy-start | bytes 6291460
  3825.1 91.9 %copy-start.91 = (f32[1024]{0:T(1024)S(1)}, f32[1024]{0:T(1024)}, u32[]{:S(2)}) copy-start(f32[1024]{0:T(1024)} %copy-done.90) | copy-start | bytes 12292
  3825.2 91.9 %copy-start.94 = (f32[1024]{0:T(1024)S(1)}, f32[1024]{0:T(1024)}, u32[]{:S(2)}) copy-start(f32[1024]{0:T(1024)} %param.24) | copy-start | bytes 12292
  3826.4 93.9 %copy-start.97 = (f32[1024]{0:T(1024)S(1)}, f32[1024]{0:T(1024)}, u32[]{:S(2)}) copy-start(f32[1024]{0:T(1024)} %get-tuple-element.772) | copy-start | bytes 12292
  3826.4 93.9 %copy-start.106 = (f32[128]{0:T(128)S(1)}, f32[128]{0:T(128)}, u32[]{:S(2)}) copy-start(f32[128]{0:T(128)} %get-tuple-element.770) | copy-start | bytes 1540
  (100 other events, 894.7 us)
Sparse Core Ops, SparseCore 0:
  9.6 24.8 all-gather.11
  36.9 87.2 all-gather.9
  125.8 22.0 all-gather.13
  1951.3 153.9 reduce-scatter.23
  2106.7 26.5 all-gather.17
  2135.6 86.3 all-gather.15
  2223.5 26.5 all-gather.19
  2251.7 25.2 all-gather.21
  2279.4 86.3 all-gather.23
  2415.6 153.8 reduce-scatter.27
  2572.6 86.4 reduce-scatter.25
  2666.3 87.5 all-gather.25
  2756.3 34.2 reduce-scatter.43
  2792.9 32.2 reduce-scatter.45
  2827.5 31.9 reduce-scatter.47
  3615.9 30.4 reduce-scatter.39
  3648.4 29.0 reduce-scatter.41
  3679.7 29.1 reduce-scatter.31
  3732.0 30.9 reduce-scatter.37
  3765.3 30.5 reduce-scatter.33
  3798.3 30.6 reduce-scatter.35
  3832.3 84.6 reduce-scatter.29
where the time goes:
time: 3990 us; the launch traced here: 3970 us
  other arithmetic  1550 us (39%)
  matrix products  1230 us (31%)
  waiting for transfers between devices  753 us (19%)
  local copies, waits for them, and re-layouts  322 us (8%)
  blocking collectives  99.2 us (2%)
    another operation x3, other arithmetic, stretch_mixer(): jax.scipy.linalg.solve_triangular(lower, jnp.concatenate([value_rows, gro...  1270 us
    dot_general x96, matrix products, advance(): jnp.einsum('bhcp,bhpv->bhcv', score, delta, precision=HIGH)  207 us
    dot_general x96, matrix products, advance(): jnp.einsum('bhpk,bhkv->bhpv', mix_k, carried, precision=HIGH)  192 us
    dot_general x96, matrix products, advance(): jnp.einsum('bhpk,bhpv->bhkv', key_o, delta, precision=HIGH)  168 us
    dot_general x96, matrix products, advance(): jnp.einsum('bhck,bhkv->bhcv', query_d, carried, precision=HIGH)  163 us
    reduce_scatter x1, waiting for transfers between devices, per_device(): lax.psum_scatter(project(mixed_low, full_out), 'tensor', scatter_dimensio...  153 us
    reduce_scatter x1, waiting for transfers between devices, per_device(): lax.psum_scatter(times_trans(gate_grad_pre, full_gate) + times_trans(up_g...  141 us
    dot_general x9, matrix products, times_trans(): lax.dot_general(left, right, (((1,), (1,)), ((), ())), preferred_element_...  124 us
  transfers between devices with their start and end apart: 22, of which 11 were waited for; matrix products, arithmetic and copies ran while one was open for 33% of the time, Pallas kernels for 0%

commit v1 on v0

v1 whole, which is shorter than its diff:
```python
import functools
import jax
import jax.numpy as jnp
import numpy as np
from jax import lax
from jax.experimental import pallas as pl
from jax.experimental.pallas import tpu as pltpu
from jax.sharding import Mesh
from jax.sharding import PartitionSpec as P

HEAD = 128
NH = 2
CT = 64
ROWS = CT * NH
EPS = 1e-06
HIGH = lax.Precision.HIGHEST
BF = jnp.bfloat16
F32 = jnp.float32


def dot_nn(left, right):
    return jnp.dot(left, right, preferred_element_type=F32)


def dot_nt(left, right):
    return lax.dot_general(left, right, (((1,), (1,)), ((), ())), preferred_element_type=F32)


def dot_tn(left, right):
    return lax.dot_general(left, right, (((0,), (0,)), ((), ())), preferred_element_type=F32)


def mixer_tables():
    row = np.arange(ROWS)
    tok, step = row % CT, row // CT
    order = tok * NH + step
    later = order[:, None] > order[None, :]
    barred = np.where(later, 0.0, -1e30).astype(np.float32)
    levels = []
    for size in (1, 4, 16):
        near = (tok[:, None] // (4 * size)) == (tok[None, :] // (4 * size))
        apart = (tok[:, None] // size) != (tok[None, :] // size)
        levels.append((near & apart).astype(np.float32))
    own = ((tok[:, None] == tok[None, :]) & later).astype(np.float32)
    eye = np.eye(ROWS, dtype=np.float32)
    read = np.zeros((CT, ROWS), np.float32)
    read[np.arange(CT), CT + np.arange(CT)] = 1.0
    sums = (np.arange(CT)[:, None] <= tok[None, :]).astype(np.float32)
    square = np.stack([barred, eye, own] + levels)
    thin = np.stack([read, sums])
    return square, thin


def sigm(values):
    return jax.nn.sigmoid(values)


class Layout:
    def __init__(self, heads):
        self.q = 0
        self.k = heads * HEAD
        self.v = self.k + heads * NH * HEAD
        self.g = self.v + heads * NH * HEAD
        self.r = self.g + heads * HEAD
        self.width = self.r + 128


def piece(ref, s, c, start):
    return ref[s, c * CT : (c + 1) * CT, start : start + HEAD]


def unit_silu(raw):
    sig = sigm(raw)
    act = raw * sig
    norm = lax.rsqrt(jnp.sum(act * act, axis=-1, keepdims=True) + EPS)
    return act * norm, norm, sig


def rates_of(pre_ref, par_ref, thin_ref, s, c, lay):
    raw = pre_ref[s, c * CT : (c + 1) * CT, lay.r : lay.r + 128]
    shifted = raw + par_ref[s, 1:2, :]
    soft = jnp.maximum(shifted, 0.0) + jnp.log1p(jnp.exp(-jnp.abs(shifted)))
    decay = par_ref[s, 0:1, :] * soft
    sums = thin_ref[1]
    cum_col = lax.dot_general(
        sums, decay, (((0,), (0,)), ((), ())), preferred_element_type=F32, precision=HIGH
    )
    cum_row = lax.dot_general(
        decay, sums, (((0,), (0,)), ((), ())), preferred_element_type=F32, precision=HIGH
    )
    return raw, shifted, decay, cum_col, cum_row


def chunk_parts(pre_ref, s, h, c, lay, raw, cum_col, cum_row, square_ref, thin_ref):
    query, nq, sq = unit_silu(piece(pre_ref, s, c, lay.q + h * HEAD))
    key0, nk0, sk0 = unit_silu(piece(pre_ref, s, c, lay.k + (2 * h) * HEAD))
    key1, nk1, sk1 = unit_silu(piece(pre_ref, s, c, lay.k + (2 * h + 1) * HEAD))
    keys = jnp.concatenate([key0, key1], axis=0)
    beta = jnp.concatenate([sigm(raw[:, 3 * h : 3 * h + 1]), sigm(raw[:, 3 * h + 1 : 3 * h + 2])], axis=0)
    scaled = keys * beta
    at = 3 * h + 2
    gcol = cum_col[:, at : at + 1]
    grow = cum_row[at : at + 1, :]
    weights = jnp.exp(gcol - grow + square_ref[0])
    tail = gcol[CT - 1 : CT, :]
    grown = jnp.exp(gcol)
    left = jnp.exp(tail - gcol)
    return dict(
        query=query, keys=keys, beta=beta, scaled=scaled, weights=weights, grown=grown, left=left,
        tail=jnp.exp(tail), nq=nq, sq=sq, nk=(nk0, nk1), sk=(sk0, sk1),
    )


def forward_kernel(lay, nsq, heads, nb, _, pre_ref, par_ref, gain_ref, square_ref, thin_ref,
                   mixed_ref, tinv_ref, state_ref, delta_ref, o_ref, carry):
    @pl.when(pl.program_id(0) == 0)
    def _():
        carry[...] = jnp.zeros_like(carry)

    which = [(c, s, h) for c in range(nb) for s in range(nsq) for h in range(heads)]
    rates = {}
    for c in range(nb):
        for s in range(nsq):
            rates[c, s] = rates_of(pre_ref, par_ref, thin_ref, s, c, lay)
    parts = {}
    for c, s, h in which:
        raw, _, _, cum_col, cum_row = rates[c, s]
        parts[c, s, h] = chunk_parts(pre_ref, s, h, c, lay, raw, cum_col, cum_row, square_ref, thin_ref)
    lam, scores = {}, {}
    for key in which:
        p = parts[key]
        keys_low, scaled_low, query_low = p["keys"].astype(BF), p["scaled"].astype(BF), p["query"].astype(BF)
        both = dot_nt(jnp.concatenate([keys_low, query_low], axis=0), scaled_low)
        lam[key] = both[:ROWS] * p["weights"]
        scores[key] = (both[ROWS:] * (p["weights"][CT:] + thin_ref[0])).astype(BF)
    tinv = {key: square_ref[1] - lam[key] * square_ref[2] for key in which}
    for level in range(3):
        low = {key: tinv[key].astype(BF) for key in which}
        step = {key: dot_nn(low[key], (lam[key] * square_ref[3 + level]).astype(BF)).astype(BF) for key in which}
        twice = {key: dot_nn(step[key], step[key]).astype(BF) for key in which}
        half = {key: tinv[key] - dot_nn(step[key], low[key]) for key in which}
        tinv = {key: half[key] + dot_nn(twice[key], half[key].astype(BF)) for key in which}
    for c in range(nb):
        for s in range(nsq):
            for h in range(heads):
                p = parts[c, s, h]
                at = s * heads + h
                state = carry[at]
                state_low = state.astype(BF)
                t_low = tinv[c, s, h].astype(BF)
                tinv_ref[c, at] = t_low
                state_ref[c, at] = state_low
                kg = (p["keys"] * p["grown"]).astype(BF)
                qg = (p["query"] * p["grown"][:CT]).astype(BF)
                both = dot_nn(jnp.concatenate([kg, qg], axis=0), state_low)
                raw0 = piece(pre_ref, s, c, lay.v + (2 * h) * HEAD)
                raw1 = piece(pre_ref, s, c, lay.v + (2 * h + 1) * HEAD)
                values = jnp.concatenate([raw0 * sigm(raw0), raw1 * sigm(raw1)], axis=0)
                delta = dot_nn(t_low, (values - both[:ROWS]).astype(BF)).astype(BF)
                delta_ref[c, at] = delta
                kout = (p["scaled"] * p["left"]).astype(BF)
                carry[at] = p["tail"] * state + dot_tn(kout, delta)
                out = both[ROWS:] + dot_nn(scores[c, s, h], delta)
                o_ref[s, c * CT : (c + 1) * CT, h * HEAD : (h + 1) * HEAD] = out
                scale = lax.rsqrt(jnp.mean(out * out, axis=-1, keepdims=True) + EPS)
                gate = piece(pre_ref, s, c, lay.g + h * HEAD)
                mixed = out * scale * gain_ref[0:1, :] * (gate * sigm(gate))
                mixed_ref[s, c * CT : (c + 1) * CT, h * HEAD : (h + 1) * HEAD] = mixed.astype(BF)


def silu_slope(raw, sig):
    return sig * (1.0 + raw * (1.0 - sig))


def backward_kernel(lay, nsq, heads, nb, _, pre_ref, par_ref, gain_ref, square_ref, thin_ref,
                    tinv_ref, state_ref, delta_ref, o_ref, dm_ref,
                    dpre_ref, small_ref, carry, acc):
    @pl.when(pl.program_id(0) == 0)
    def _():
        carry[...] = jnp.zeros_like(carry)
        acc[...] = jnp.zeros_like(acc)

    lane = lax.broadcasted_iota(jnp.int32, (CT, 128), 1)
    sub8 = lax.broadcasted_iota(jnp.int32, (8, 128), 0)
    lane_rows = lax.broadcasted_iota(jnp.int32, (ROWS, 128), 1)
    rates = {}
    for c in range(nb):
        for s in range(nsq):
            rates[c, s] = rates_of(pre_ref, par_ref, thin_ref, s, c, lay)
    for c in reversed(range(nb)):
        span = slice(c * CT, (c + 1) * CT)
        for s in range(nsq):
            raw, shifted, decay, cum_col, cum_row = rates[c, s]
            dg_all = jnp.zeros((ROWS, 128), F32)
            dq_all = jnp.zeros((CT, 128), F32)
            dtail_all = jnp.zeros((1, 128), F32)
            dbeta_all = jnp.zeros((CT, 128), F32)
            dcol_all = jnp.zeros((8, 128), F32)
            for h in range(heads):
                at = s * heads + h
                cols = slice(h * HEAD, (h + 1) * HEAD)
                p = chunk_parts(pre_ref, s, h, c, lay, raw, cum_col, cum_row, square_ref, thin_ref)
                out = o_ref[s, span, cols]
                dm = dm_ref[s, span, cols].astype(F32)
                graw = piece(pre_ref, s, c, lay.g + h * HEAD)
                gsig = sigm(graw)
                gate = graw * gsig
                scale = lax.rsqrt(jnp.mean(out * out, axis=-1, keepdims=True) + EPS)
                normed = out * scale
                gain = gain_ref[0:1, :]
                dgate = dm * normed * gain
                dpre_ref[s, span, lay.g + h * HEAD : lay.g + (h + 1) * HEAD] = (
                    dgate * silu_slope(graw, gsig)
                ).astype(BF)
                dn = dm * gate
                acc[0:1, :] += jnp.sum(dn * normed, axis=0, keepdims=True)
                scaled_dn = dn * gain
                dout = scale * (scaled_dn - normed * jnp.mean(scaled_dn * normed, axis=-1, keepdims=True))
                dout_low = dout.astype(BF)
                keys_low, scaled_low, query_low = p["keys"].astype(BF), p["scaled"].astype(BF), p["query"].astype(BF)
                read_w = p["weights"][CT:] + thin_ref[0]
                both_low = jnp.concatenate([keys_low, query_low], axis=0)
                w_all = jnp.concatenate([p["weights"], read_w], axis=0)
                weighted = dot_nt(both_low, scaled_low) * w_all
                scores = weighted[ROWS:].astype(BF)
                dstate = carry[at]
                dstate_low = dstate.astype(BF)
                kout = (p["scaled"] * p["left"]).astype(BF)
                ddelta = dot_tn(scores, dout_low) + dot_nn(kout, dstate_low)
                dpv = dot_tn(tinv_ref[c, at], ddelta.astype(BF))
                kg = (p["keys"] * p["grown"]).astype(BF)
                qg = (p["query"] * p["grown"][:CT]).astype(BF)
                joint = jnp.concatenate([(-dpv).astype(BF), dout_low], axis=0)
                carry[at] = p["tail"] * dstate + dot_tn(jnp.concatenate([kg, qg], axis=0), joint)
                delta = delta_ref[c, at]
                state_low = state_ref[c, at]
                inner = dot_nt(joint, delta)
                inner_low = (inner * w_all).astype(BF)
                pairs = inner * weighted
                grown_all = jnp.concatenate([p["grown"], p["grown"][:CT]], axis=0)
                entered = grown_all * dot_nt(joint, state_low)
                left_out = p["left"] * dot_nt(delta, dstate_low)
                direct = dot_nn(inner_low, scaled_low) + entered
                dscaled = dot_tn(inner_low, both_low) + left_out
                both_rows = jnp.concatenate([p["keys"], p["query"]], axis=0)
                row_part = jnp.sum(pairs + both_rows * entered, axis=-1, keepdims=True)
                col_part = jnp.sum(pairs, axis=0, keepdims=True)
                out_part = jnp.sum(p["scaled"] * left_out, axis=-1, keepdims=True)
                dtail = p["tail"] * jnp.sum(
                    jnp.sum(state_low.astype(F32) * dstate, axis=0, keepdims=True), axis=1, keepdims=True
                ) + jnp.sum(out_part, axis=0, keepdims=True)
                dkeys, dquery = direct[:ROWS], direct[ROWS:]
                dbeta = jnp.sum(p["keys"] * dscaled, axis=-1, keepdims=True)
                kdot = jnp.sum(p["keys"] * dkeys, axis=-1, keepdims=True)
                qdot = jnp.sum(p["query"] * dquery, axis=-1, keepdims=True)
                dg = row_part[:ROWS] - out_part
                kfull = kdot + p["beta"] * dbeta
                here = 3 * h + 2
                dg_all = jnp.where(lane_rows == here, dg, dg_all)
                dq_all = jnp.where(lane == here, row_part[ROWS:], dq_all)
                dcol_all = jnp.where(sub8 == here, col_part, dcol_all)
                dtail_all = jnp.where(lane[0:1] == here, dtail, dtail_all)
                dbp = dbeta * p["beta"] * (1.0 - p["beta"])
                dbeta_all = jnp.where(lane == 3 * h, dbp[:CT], dbeta_all)
                dbeta_all = jnp.where(lane == 3 * h + 1, dbp[CT:], dbeta_all)
                dk = dkeys + p["beta"] * dscaled
                dk = dk - p["keys"] * kfull
                for j in range(NH):
                    part = slice(j * CT, (j + 1) * CT)
                    start = lay.k + (2 * h + j) * HEAD
                    kraw = piece(pre_ref, s, c, start)
                    dpre_ref[s, span, start : start + HEAD] = (
                        dk[part] * p["nk"][j] * silu_slope(kraw, p["sk"][j])
                    ).astype(BF)
                    start = lay.v + (2 * h + j) * HEAD
                    vraw = piece(pre_ref, s, c, start)
                    dpre_ref[s, span, start : start + HEAD] = (
                        dpv[part] * silu_slope(vraw, sigm(vraw))
                    ).astype(BF)
                start = lay.q + h * HEAD
                qraw = piece(pre_ref, s, c, start)
                dq = (dquery - p["query"] * qdot) * p["nq"]
                dpre_ref[s, span, start : start + HEAD] = (dq * silu_slope(qraw, p["sq"])).astype(BF)
            sums = thin_ref[1]
            read_sum = dg_all[:CT] + dg_all[CT:] + dq_all
            col_rows = jnp.concatenate([dcol_all, jnp.zeros((120, 128), F32)], axis=0)
            ddecay = (
                jnp.dot(sums[:, :CT], read_sum, preferred_element_type=F32, precision=HIGH)
                - lax.dot_general(
                    sums, col_rows, (((1,), (1,)), ((), ())), preferred_element_type=F32, precision=HIGH
                )
                + dtail_all
            )
            dshift = ddecay * par_ref[s, 0:1, :] * sigm(shifted)
            acc[1 + s : 2 + s, :] += jnp.sum(dshift, axis=0, keepdims=True)
            acc[1 + nsq + s : 2 + nsq + s, :] += jnp.sum(ddecay * decay, axis=0, keepdims=True)
            dpre_ref[s, span, lay.r : lay.r + 128] = (dshift + dbeta_all).astype(BF)
    small_ref[...] = acc[...]


def shared_specs(square, thin, nsq):
    return [
        pl.BlockSpec((nsq, 2, 128), lambda i, _: (0, 0, 0)),
        pl.BlockSpec((1, HEAD), lambda i, _: (0, 0)),
        pl.BlockSpec(square.shape, lambda i, _: (0, 0, 0)),
        pl.BlockSpec(thin.shape, lambda i, _: (0, 0, 0)),
    ]


def part_chunk(step, place, per_part):
    return ((step // per_part) ^ place[0]) * per_part + step % per_part


def mixer_forward(place, parts, pre, params, gain, heads, nb=2):
    nsq, length, width = pre.shape
    lay = Layout(heads)
    square, thin = mixer_tables()
    nchunk = length // CT
    chains = nsq * heads
    span = nb * CT
    per_part = nchunk // nb // parts
    big = lambda: pl.BlockSpec((nb, chains, ROWS, HEAD), lambda i, _: (i, 0, 0, 0))
    rows = lambda w: pl.BlockSpec((nsq, span, w), lambda i, place: (0, part_chunk(i, place, per_part), 0))
    return pl.pallas_call(
        functools.partial(forward_kernel, lay, nsq, heads, nb),
        grid_spec=pltpu.PrefetchScalarGridSpec(
            num_scalar_prefetch=1,
            grid=(nchunk // nb,),
            in_specs=[rows(width)] + shared_specs(square, thin, nsq),
            out_specs=[rows(heads * HEAD), big(), big(), big(), rows(heads * HEAD)],
            scratch_shapes=[pltpu.VMEM((chains, HEAD, HEAD), F32)],
        ),
        out_shape=[
            jax.ShapeDtypeStruct((nsq, length, heads * HEAD), BF),
            jax.ShapeDtypeStruct((nchunk, chains, ROWS, ROWS), BF),
            jax.ShapeDtypeStruct((nchunk, chains, HEAD, HEAD), BF),
            jax.ShapeDtypeStruct((nchunk, chains, ROWS, HEAD), BF),
            jax.ShapeDtypeStruct((nsq, length, heads * HEAD), F32),
        ],
        compiler_params=pltpu.CompilerParams(vmem_limit_bytes=56 * 1024 * 1024),
        cost_estimate=pl.CostEstimate(
            flops=nchunk * chains * 20 * 2 * ROWS**3,
            bytes_accessed=nsq * length * (4 * width + 6 * heads * HEAD) + nchunk * chains * 6 * ROWS**2,
            transcendentals=0,
        ),
        name="mixer_forward",
    )(place, pre, params, gain, jnp.asarray(square), jnp.asarray(thin))


def mixer_backward(place, parts, pre, params, gain, tinv, states, deltas, outs, dmixed, heads, nb=2):
    nsq, length, width = pre.shape
    lay = Layout(heads)
    square, thin = mixer_tables()
    nchunk = length // CT
    chains = nsq * heads
    span = nb * CT
    per_part = nchunk // nb // parts
    last = nchunk // nb - 1
    big = lambda: pl.BlockSpec((nb, chains, ROWS, HEAD), lambda i, _: (last - i, 0, 0, 0))
    rows = lambda w: pl.BlockSpec(
        (nsq, span, w), lambda i, place: (0, part_chunk(last - i, place, per_part), 0)
    )
    return pl.pallas_call(
        functools.partial(backward_kernel, lay, nsq, heads, nb),
        grid_spec=pltpu.PrefetchScalarGridSpec(
            num_scalar_prefetch=1,
            grid=(nchunk // nb,),
            in_specs=[rows(width)]
            + shared_specs(square, thin, nsq)
            + [big(), big(), big(), rows(heads * HEAD), rows(heads * HEAD)],
            out_specs=[rows(width), pl.BlockSpec((8, 128), lambda i, _: (0, 0))],
            scratch_shapes=[
                pltpu.VMEM((chains, HEAD, HEAD), F32),
                pltpu.VMEM((8, 128), F32),
            ],
        ),
        out_shape=[
            jax.ShapeDtypeStruct((nsq, length, width), BF),
            jax.ShapeDtypeStruct((8, 128), F32),
        ],
        compiler_params=pltpu.CompilerParams(vmem_limit_bytes=56 * 1024 * 1024),
        cost_estimate=pl.CostEstimate(
            flops=nchunk * chains * 26 * 2 * ROWS**3,
            bytes_accessed=nsq * length * (6 * width + 6 * heads * HEAD) + nchunk * chains * 6 * ROWS**2,
            transcendentals=0,
        ),
        name="mixer_backward",
    )(place, pre, params, gain, jnp.asarray(square), jnp.asarray(thin), tinv, states, deltas, outs, dmixed)


def rms_parts(values):
    scale = lax.rsqrt(jnp.mean(values * values, axis=-1, keepdims=True) + EPS)
    return values * scale, scale


def rms_back(grad_out, values, scale, gain):
    gain_grad = jnp.sum(grad_out * values * scale, axis=0)
    scaled = grad_out * gain
    value_grad = scale * scaled - values * scale * scale * scale * jnp.mean(
        scaled * values, axis=-1, keepdims=True
    )
    return value_grad, gain_grad


def swap(values, which, parts):
    return lax.ppermute(values, "sub", [(i, i ^ which) for i in range(parts)])


def pick(options, wanted, keys):
    chosen = options[0]
    for option, key in zip(options[1:], keys[1:]):
        chosen = jnp.where(wanted == key, option, chosen)
    return chosen


def per_device(
    tokens, lengths, out_grad, ln1_gain, ln2_gain, onorm_gain, a_log, dt_bias,
    w_query, w_key, w_value, w_rates, w_outgate, w_out, w_gate, w_up, w_down,
):
    nsq, parts = lax.axis_size("sq"), lax.axis_size("sub")
    which_seq, place = lax.axis_index("sq"), lax.axis_index("sub")
    count = nsq * parts
    tok_dev, model = tokens.shape
    heads = a_log.shape[0] // count
    lay = Layout(heads)
    units = w_gate.shape[1]
    hw = heads * HEAD
    place_arr = place.astype(jnp.int32).reshape(1)

    rates_pad = jnp.zeros((w_rates.shape[0], 128 - w_rates.shape[1]), BF)
    mix_shard = jnp.concatenate([w_query, w_key, w_value, w_outgate, w_rates, rates_pad], axis=1)
    w_mix = lax.all_gather(mix_shard, ("sq", "dp"), axis=0, tiled=True).reshape(nsq, model, lay.width)

    def everywhere(shard):
        full = lax.all_gather(shard, ("sq", "sub", "dp"), axis=0, tiled=True)
        return full.reshape(count, model, shard.shape[1])

    resid_in = tokens.astype(F32)
    normed_one, scale_one = rms_parts(resid_in)
    first = (normed_one * ln1_gain).astype(BF)
    first_seq = jnp.concatenate([first] + [swap(first, r, parts) for r in range(1, parts)], axis=0)

    pre = jnp.stack([dot_nn(first_seq, w_mix[s]) for s in range(nsq)])
    hpos = [(s * parts + place) * heads for s in range(nsq)]
    lanes = 3 * np.arange(heads) + 2

    def spread(values, s):
        mine = lax.dynamic_slice_in_dim(values, hpos[s], heads)
        return jnp.zeros((128,), F32).at[lanes].set(mine)

    params = jnp.stack([jnp.stack([spread(-jnp.exp(a_log), s), spread(dt_bias, s)]) for s in range(nsq)])
    gain = onorm_gain.reshape(1, HEAD)
    mixed, tinv, states, deltas, outs = mixer_forward(place_arr, parts, pre, params, gain, heads)

    w_out_t = everywhere(w_out.T)
    w_gate_f = everywhere(w_gate)
    w_up_f = everywhere(w_up)
    w_down_t = everywhere(w_down.T)

    got = []
    for r in range(parts):
        mine = mixed[:, r * tok_dev : (r + 1) * tok_dev]
        got.append(mine if r == 0 else swap(mine, r, parts))
    keys = [place ^ r for r in range(parts)]
    mixed_of = {}
    for s in range(nsq):
        for j in range(parts):
            mixed_of[s * parts + j] = pick([g[s] for g in got], j, keys)
    attn = dot_nt(mixed_of[0], w_out_t[0])
    for p in range(1, count):
        attn = attn + dot_nt(mixed_of[p], w_out_t[p])

    position = place * tok_dev + jnp.arange(tok_dev)
    limit = jnp.sum(jnp.where(jnp.arange(nsq) == which_seq, lengths, 0))
    mask = (position < limit).astype(F32)[:, None]
    middle = resid_in + attn
    normed_two, scale_two = rms_parts(middle)
    second = (normed_two * ln2_gain).astype(BF)
    grad_low = (out_grad.astype(F32) * mask).astype(BF)
    grad_top = grad_low.astype(F32)
    mlp = None
    second_grad = None
    gate_grads, up_grads, down_grads = [], [], []
    for p in range(count):
        gate_pre = dot_nn(second, w_gate_f[p])
        up_pre = dot_nn(second, w_up_f[p])
        gate_sig = sigm(gate_pre)
        gate_act = gate_pre * gate_sig
        hidden = (gate_act * up_pre).astype(BF)
        part = dot_nt(hidden, w_down_t[p])
        mlp = part if mlp is None else mlp + part
        hidden_grad = dot_nn(grad_low, w_down_t[p])
        down_grads.append(dot_tn(grad_low, hidden))
        up_low = (hidden_grad * gate_act).astype(BF)
        gate_low = (hidden_grad * up_pre * silu_slope(gate_pre, gate_sig)).astype(BF)
        gate_grads.append(dot_tn(second, gate_low))
        up_grads.append(dot_tn(second, up_low))
        part = dot_nt(gate_low, w_gate_f[p]) + dot_nt(up_low, w_up_f[p])
        second_grad = part if second_grad is None else second_grad + part
    block_out = ((middle + mlp) * mask).astype(BF)

    def owned(grads):
        full = jnp.concatenate([g.astype(BF) for g in grads], axis=0)
        return lax.psum_scatter(full, ("sq", "sub", "dp"), scatter_dimension=0, tiled=True).astype(F32)

    gate_own, up_own, down_own = owned(gate_grads), owned(up_grads), owned(down_grads).T

    middle_back, ln2_grad = rms_back(second_grad, middle, scale_two, ln2_gain)
    middle_grad = grad_top + middle_back
    middle_low = middle_grad.astype(BF)
    out_own = owned([dot_tn(middle_low, mixed_of[p]) for p in range(count)]).T
    mixed_grad = [dot_nn(middle_low, w_out_t[p]).astype(BF) for p in range(count)]
    back = []
    for r in range(parts):
        piece_r = jnp.stack(
            [pick([mixed_grad[s * parts + j] for j in range(parts)], place ^ r, list(range(parts))) for s in range(nsq)]
        )
        back.append(piece_r if r == 0 else swap(piece_r, r, parts))
    dmixed = jnp.concatenate(back, axis=1)
    dpre, small = mixer_backward(
        place_arr, parts, pre, params, gain, tinv, states, deltas, outs, dmixed, heads
    )

    mix_grads = jnp.concatenate([dot_tn(first_seq, dpre[s]).astype(BF) for s in range(nsq)], axis=0)
    mix_own = lax.psum_scatter(mix_grads, ("sq", "dp"), scatter_dimension=0, tiled=True).astype(F32)
    first_all = dot_nt(dpre[0], w_mix[0])
    for s in range(1, nsq):
        first_all = first_all + dot_nt(dpre[s], w_mix[s])
    first_low = first_all.astype(BF)
    first_grad = first_all[:tok_dev]
    for r in range(1, parts):
        first_grad = first_grad + swap(first_low[r * tok_dev : (r + 1) * tok_dev], r, parts).astype(F32)
    input_back, ln1_grad = rms_back(first_grad, resid_in, scale_one, ln1_gain)
    tokens_grad = (middle_grad + input_back).astype(BF)

    def gather_heads(rows):
        full = jnp.zeros(a_log.shape, F32)
        for s in range(nsq):
            full = lax.dynamic_update_slice_in_dim(full, rows[s, lanes], hpos[s], 0)
        return full

    a_grad = gather_heads(small[1 + nsq : 1 + 2 * nsq])
    dt_grad = gather_heads(small[1 : 1 + nsq])
    total = lax.psum((ln1_grad, ln2_grad, small[0], a_grad, dt_grad), ("dp", "sq", "sub"))
    return (
        block_out, tokens_grad, total[0], total[1], total[2], total[3], total[4],
        mix_own[:, lay.q : lay.k], mix_own[:, lay.k : lay.v], mix_own[:, lay.v : lay.g],
        mix_own[:, lay.r : lay.r + w_rates.shape[1]], mix_own[:, lay.g : lay.r],
        out_own, gate_own, up_own, down_own,
    )


def solution(mesh):
    dp, tensor = mesh.shape["dp"], mesh.shape["tensor"]

    def run(*args):
        nsq = args[1].shape[0] // dp
        split = Mesh(mesh.devices.reshape(dp, nsq, tensor // nsq), ("dp", "sq", "sub"))
        rows = P(("dp", "sq", "sub"), None)
        down = P("dp", ("sq", "sub"))
        across = P(("sq", "sub"), "dp")
        in_specs = (rows, P("dp"), rows) + (P(),) * 5 + (down,) * 5 + (across, down, down, across)
        out_specs = (rows, rows) + (P(),) * 5 + (down,) * 5 + (across, down, down, across)
        return jax.shard_map(
            per_device, mesh=split, in_specs=in_specs, out_specs=out_specs, check_vma=False
        )(*args)

    return run
```

time: 3990 us -> 1040 us (0.26)
  other arithmetic: 1550 us -> 52.1 us
  matrix products: 1230 us -> 225 us
  waiting for transfers between devices: 753 us -> 429 us
  local copies, waits for them, and re-layouts: 322 us -> 70.7 us
  Pallas kernels: 0 us -> 200 us
  blocking collectives: 99.2 us -> 39.3 us
    another operation x5, other arithmetic: 1270 us -> 15.8 us  [the longest x1 15.1 us: per_device(): pre = jnp.stack([dot_nn(first_seq, w_mix[s]) for s in range(nsq)])]
    dot_general x418 -> x54, matrix products: 1160 us -> 225 us  [the longest x18 94.6 us: dot_nt(): lax.dot_general(left, right, (((1,), (1,)), ((), ())), preferred_element_...]
    reduce_scatter x8 -> x2, waiting for transfers between devices: 455 us -> 89.7 us  [the longest x1 89.7 us: per_device(): lax.psum_scatter(mix_grads, ('sq', 'dp'), scatter_dimension=0, tiled=True)]
    pallas_call x0 -> x2, Pallas kernels: none -> 200 us  [the longest x1 115 us: mixer_backward(): pl.pallas_call(functools.partial(backward_kernel, lay, nsq, heads, nb), g...]
    all_gather x9 -> x5, waiting for transfers between devices: 294 us -> 105 us  [the longest x4 93 us: everywhere(): full = lax.all_gather(shard, ('sq', 'sub', 'dp'), axis=0, tiled=True)]
    ppermute x0 -> x4, waiting for transfers between devices: none -> 118 us  [swap(): return lax.ppermute(values, 'sub', [(i, i ^ which) for i in range(parts)])]
    reduce_sum x45 -> x1, other arithmetic: 118 us -> 0.63 us  [per_device(): limit = jnp.sum(jnp.where(jnp.arange(nsq) == which_seq, lengths, 0))]
    unnamed x27 -> x13, waiting for transfers between devices: 3.59 us -> 116 us
  transfers between devices with their start and end apart: 22 -> 14, of which waited for: 11 -> 9; matrix products, arithmetic and copies ran while one was open for 33% -> 25% of each run, Pallas kernels for 0% -> 19%
where the time goes in v1:
time: 1040 us
  waiting for transfers between devices  429 us (41%)
  matrix products  225 us (22%)
  Pallas kernels  200 us (19%)
  local copies, waits for them, and re-layouts  70.7 us (7%)
  other arithmetic  52.1 us (5%)
  blocking collectives  39.3 us (4%)
  between operations  15.4 us (1%)
    ppermute x4, waiting for transfers between devices, swap(): return lax.ppermute(values, 'sub', [(i, i ^ which) for i in range(parts)])  118 us
    unnamed x13, waiting for transfers between devices  116 us
    pallas_call x1, Pallas kernels, mixer_backward(): pl.pallas_call(functools.partial(backward_kernel, lay, nsq, heads, nb), g...  115 us
    dot_general x18, matrix products, dot_nt(): lax.dot_general(left, right, (((1,), (1,)), ((), ())), preferred_element_...  94.6 us
    all_gather x4, waiting for transfers between devices, everywhere(): full = lax.all_gather(shard, ('sq', 'sub', 'dp'), axis=0, tiled=True)  93 us
    reduce_scatter x1, waiting for transfers between devices, per_device(): lax.psum_scatter(mix_grads, ('sq', 'dp'), scatter_dimension=0, tiled=True)  89.7 us
    pallas_call x1, Pallas kernels, mixer_forward(): pl.pallas_call(functools.partial(forward_kernel, lay, nsq, heads, nb), gr...  84.9 us
    dot_general x18, matrix products, dot_nn(): return jnp.dot(left, right, preferred_element_type=F32)  80.4 us
  transfers between devices with their start and end apart: 14, of which 9 were waited for; matrix products, arithmetic and copies ran while one was open for 25% of the time, Pallas kernels for 19%

profile of v1, /device:TPU:0, one launch (start us, length us, event | category | flops | bytes accessed | tf_op | source)
XLA Modules:
  0.0 1040.1 jit_solution(7409929770589122166)
XLA Ops:
  24.6 42.3 %collective-permute-done = bf16[1024,1024]{0,1:T(8,128)(2,1)} collective-permute-done((bf16[1024,1024]{0,1:T(8,128)(2,1)}, bf16[1024,1024]{0,1:T(8,128)(2,1)}, u32[]{:S(2)}, u32[]{:S(2)}) %collective-permute-start) | collective-permute-done | bytes 2097184 | tf_op jit(solution)/shard_map/ppermute | solution.py:406
  66.9 11.7 %all-gather.6.cloned.1.call-done = bf16[2048,1664]{1,0:T(8,128)(2,1)} async-done(((bf16[128,1664]{1,0:T(8,128)(2,1)}), bf16[2048,1664]{1,0:T(8,128)(2,1)}) %all-gather.6.cloned.1.call-update) | async-done | bytes 6815760 | tf_op jit(solution)/shard_map/all_gather | solution.py:432
  78.6 11.7 %convolution_bitcast_fusion.1 = f32[1,2048,1664]{2,1,0:T(8,128)S(1)} fusion(bf16[2048,1664]{1,0:T(8,128)(2,1)} %all-gather.6.cloned.1.call-done, bf16[1024,1024]{0,1:T(8,128)(2,1)} %collective-permute-done, bf16[1024,1024]{0,1:T(8,128)(2,1)} %fusion.14), kind=kOutput, calls=%fused_computation.10 | convolution fusion | flops 6987710464 | bytes 21233664 | tf_op jit(solution)/shard_map/dot_general | solution.py:22
  90.3 12.6 %convolution_bitcast_fusion = f32[1,2048,1664]{2,1,0:T(8,128)} fusion(bf16[2048,1664]{1,0:T(8,128)(2,1)S(1)} %copy-done.38, bf16[1024,1024]{0,1:T(8,128)(2,1)} %collective-permute-done, bf16[1024,1024]{0,1:T(8,128)(2,1)} %fusion.14), kind=kOutput, calls=%fused_computation.9 | convolution fusion | flops 6987710464 | bytes 21233664 | tf_op jit(solution)/shard_map/dot_general | solution.py:22
  102.9 15.1 %pad_maximum_fusion.pre_ref = f32[2,2048,1664]{2,1,0:T(8,128)} fusion(f32[1,2048,1664]{2,1,0:T(8,128)} %convolution_bitcast_fusion, f32[1,2048,1664]{2,1,0:T(8,128)S(1)} %convolution_bitcast_fusion.1), kind=kLoop, calls=%fused_computation.8 | loop fusion | flops 6815744 | bytes 54525952 | tf_op jit(solution)/shard_map/stack | solution.py:443
  118.0 84.9 %mixer_forward.1 = (bf16[2,2048,256]{2,1,0:T(8,128)(2,1)}, bf16[32,4,128,128]{3,2,1,0:T(8,128)(2,1)}, bf16[32,4,128,128]{3,2,1,0:T(8,128)(2,1)}, bf16[32,4,128,128]{3,2,1,0:T(8,128)(2,1)}, f32[2,2048,256]{2,1,0:T(8,128)}) custom-call(s32[1]{0:T(128)} %bitcast._, f32[2,2048,1664]{2,1,0:T(8,128)} %pad_maximum_fusion.pre_ref, ...), custom_call_target="tpu_custom_call" | custom-call | flops 10737418240 | bytes 46137344 | tf_op jit(solution)/shard_map/mixer_forward/pallas_call | solution.py:324
  206.6 4.1 copy.94
  212.0 20.6 %collective-permute-done.1 = bf16[2,1024,256]{2,1,0:T(8,128)(2,1)S(1)} collective-permute-done((bf16[2,1024,256]{2,1,0:T(8,128)(2,1)}, bf16[2,1024,256]{2,1,0:T(8,128)(2,1)S(1)}, u32[]{:S(2)}, u32[]{:S(2)}) %collective-permute-start.1) | collective-permute-done | bytes 1048608 | tf_op jit(solution)/shard_map/ppermute | solution.py:406
  240.5 5.3 fusion.45
  245.8 4.6 fusion.69
  250.3 39.7 %all-gather.10.cloned.1.call-done = bf16[4096,704]{0,1:T(8,128)(2,1)} async-done(((bf16[128,704]{0,1:T(8,128)(2,1)}), bf16[4096,704]{0,1:T(8,128)(2,1)}) %all-gather.10.cloned.1.call-update) | async-done | bytes 5767184 | tf_op jit(solution)/shard_map/all_gather | solution.py:435
  290.0 4.7 fusion.49
  304.6 3.8 fusion.57
  308.4 5.0 fusion.61
  313.4 53.3 %all-gather.14.cloned.1.call-done = bf16[4096,704]{0,1:T(8,128)(2,1)} async-done(((bf16[128,704]{0,1:T(8,128)(2,1)}), bf16[4096,704]{0,1:T(8,128)(2,1)}) %all-gather.14.cloned.1.call-update) | async-done | bytes 5767184 | tf_op jit(solution)/shard_map/all_gather | solution.py:435
  366.7 6.5 multiply_convert_fusion.3
  374.3 5.5 fusion.47
  379.9 3.8 multiply_convert_fusion.7
  383.7 3.9 fusion.67
  387.7 3.8 fusion.71
  391.5 4.0 multiply_convert_fusion.9
  395.5 3.8 fusion.79
  399.4 3.8 fusion.83
  407.0 3.8 fusion.55
  410.8 4.0 fusion.59
  414.8 15.0 %multiply_reduce_fusion = (f32[1024]{0:T(1024)}, f32[1024]{0:T(1024)S(1)}, f32[1024,1024]{0,1:T(8,128)S(1)}) fusion(f32[1024,1024]{0,1:T(8,128)S(1)} %copy-done.1, f32[1024]{0:T(1024)S(1)} %add_rsqrt_fusion, f32[1024]{0:T(1024)S(1)} %copy-done.25, f32[1024,1024]{0,1:T(8,128)} %fusion.47, bf16[1024,704]{0,1:T(8,128)(2,1)} %get-tuple-element.87, ...), kind=kOutput, calls=%fused_computation.47 | convolution fusion | flops 1490024448 | bytes 40648704 | tf_op jit(solution)/shard_map/dot_general | solution.py:26
  438.1 3.8 convolution_convert_fusion.4
  450.6 8.5 copy.125
  459.1 3.8 convolution_convert_fusion.8
  471.5 8.5 copy.123
  492.1 8.5 copy.127
  508.6 26.1 %collective-permute-done.2 = bf16[2,1024,256]{2,1,0:T(8,128)(2,1)S(1)} collective-permute-done((bf16[2,1024,256]{2,1,0:T(8,128)(2,1)S(1)}, bf16[2,1024,256]{2,1,0:T(8,128)(2,1)S(1)}, u32[]{:S(2)}, u32[]{:S(2)}) %collective-permute-start.2) | collective-permute-done | bytes 1048608 | tf_op jit(solution)/shard_map/ppermute | solution.py:406
  536.1 115.0 %mixer_backward.1 = (bf16[2,2048,1664]{2,1,0:T(8,128)(2,1)}, f32[8,128]{1,0:T(8,128)}) custom-call(s32[1]{0:T(128)} %bitcast._, f32[2,2048,1664]{2,1,0:T(8,128)} %pad_maximum_fusion.pre_ref, f32[2,2,128]{2,1,0:T(2,128)} %pad_maximum_fusion.9.par_ref, f32[1,128]{1,0:T(1,128)} %bitcast.134, f32[6,128,128]{2,1,0:T(8,128)} %constant.46.clone.square_ref, ...), custom_call_target="tpu_custom_call" | custom-call | flops 13958643712 | bytes 59768832 | tf_op jit(solution)/shard_map/mixer_backward/pallas_call | solution.py:363
  651.1 11.7 %fusion.24 = bf16[1024,1664]{1,0:T(8,128)(2,1)S(1)} fusion(bf16[2,2048,1664]{2,1,0:T(8,128)(2,1)} %get-tuple-element.28, bf16[1024,1024]{0,1:T(8,128)(2,1)} %collective-permute-done, bf16[1024,1024]{0,1:T(8,128)(2,1)} %fusion.14), kind=kOutput, calls=%fused_computation.55 | convolution fusion | flops 6989414400 | bytes 14417920 | tf_op jit(solution)/shard_map/dot_general | solution.py:30
  662.9 9.7 fusion.27
  680.4 13.0 %fusion.2 = f32[2048,1024]{0,1:T(8,128)} fusion(bf16[2,2048,1664]{2,1,0:T(8,128)(2,1)} %get-tuple-element.28, bf16[2048,1664]{1,0:T(8,128)(2,1)} %all-gather.6.cloned.1.call-done), kind=kOutput, calls=%fused_computation.19 | convolution fusion | flops 6979321856 | bytes 18612224 | tf_op jit(solution)/shard_map/dot_general | solution.py:26
  693.4 12.2 %fusion.30 = f32[2048,1024]{0,1:T(8,128)S(1)} fusion(f32[2048,1024]{0,1:T(8,128)} %fusion.2, bf16[2,2048,1664]{2,1,0:T(8,128)(2,1)} %get-tuple-element.28, bf16[2048,1664]{1,0:T(8,128)(2,1)} %all-gather.6.cloned.1.call-done), kind=kOutput, calls=%fused_computation.57 | convolution fusion | flops 6981419008 | bytes 27000832 | tf_op jit(solution)/shard_map/dot_general | solution.py:26
  708.9 4.5 fusion.77
  713.4 5.6 fusion.53
  719.0 7.0 multiply_convert_fusion.1
  726.0 4.2 copy.105
  733.6 29.4 %collective-permute-done.3 = bf16[1024,1024]{0,1:T(8,128)(2,1)} collective-permute-done((bf16[1024,1024]{0,1:T(8,128)(2,1)}, bf16[1024,1024]{0,1:T(8,128)(2,1)}, u32[]{:S(2)}, u32[]{:S(2)}) %collective-permute-start.3) | collective-permute-done | bytes 2097184 | tf_op jit(solution)/shard_map/ppermute | solution.py:406
  763.0 4.0 fusion.23
  767.1 6.7 fusion.19
  773.8 4.0 copy.106
  777.8 39.3 %all-reduce.4 = (f32[1024]{0:T(1024)}, f32[1024]{0:T(1024)}, f32[128]{0:T(128)}, f32[8]{0:T(128)}, f32[8]{0:T(128)}) all-reduce(f32[1024]{0:T(1024)S(1)} %get-tuple-element.78, f32[1024]{0:T(1024)S(1)} %copy-done.33, f32[128]{0:T(128)S(1)} %slice_bitcast_fusion, ...), channel_id=1, replica_groups=mesh['dp'=8,'sq'=2,'sub'=2] {'dp','sq','sub'}, use_global_device_ids=true, to_apply=%region_10.11 | all-reduce | flops 2192 | bytes 17536 | tf_op jit(solution)/shard_map/psum | solution.py:544
  822.4 114.3 %reduce-scatter.20.cloned.1.call-done = bf16[128,704]{1,0:T(8,128)(2,1)} async-done(((bf16[4096,704]{1,0:T(8,128)(2,1)}), bf16[128,704]{1,0:T(8,128)(2,1)}) %reduce-scatter.20.cloned.1.call-update) | async-done | bytes 180240
  938.5 89.7 %reduce-scatter.12.cloned.1.call-done = bf16[128,1664]{1,0:T(8,128)(2,1)} async-done(((bf16[2048,1664]{1,0:T(8,128)(2,1)}), bf16[128,1664]{1,0:T(8,128)(2,1)}) %reduce-scatter.12.cloned.1.call-update) | async-done | bytes 426000 | tf_op jit(solution)/shard_map/reduce_scatter | solution.py:525
  (263 shorter events, 118.2 us)
Async XLA Ops:
  7.2 71.4 %all-gather.6.cloned.1.call-start = ((), (), s32[]{:S(2)}) async-start(), calls=%async_computation.5 | async-start | bytes 7241728 | tf_op jit(solution)/shard_map/all_gather | solution.py:432
  9.9 202.1 %all-gather.8.cloned.1.call-start = ((), (), s32[]{:S(2)}) async-start(), calls=%async_computation.6 | async-start | bytes 2162688 | tf_op jit(solution)/shard_map/all_gather | solution.py:435
  10.7 229.8 %all-gather.12.cloned.1.call-start = ((), (), s32[]{:S(2)}) async-start(), calls=%async_computation.8 | async-start | bytes 5947392 | tf_op jit(solution)/shard_map/all_gather | solution.py:435
  11.4 278.6 %all-gather.10.cloned.1.call-start = ((), (), s32[]{:S(2)}) async-start(), calls=%async_computation.7 | async-start | bytes 5947392 | tf_op jit(solution)/shard_map/all_gather | solution.py:435
  12.0 4.2 copy-start.31
  12.0 354.7 %all-gather.14.cloned.1.call-start = ((), (), s32[]{:S(2)}) async-start(), calls=%async_computation.9 | async-start | bytes 5947392 | tf_op jit(solution)/shard_map/all_gather | solution.py:435
  14.9 221.6 %copy-start.4 = (bf16[1024,1024]{0,1:T(8,128)(2,1)}, bf16[1024,1024]{0,1:T(8,128)(2,1)S(1)}, u32[]{:S(2)}) copy-start(bf16[1024,1024]{0,1:T(8,128)(2,1)S(1)} %copy.88) | copy-start | bytes 6291460
  14.9 6.1 copy-start.40
  14.9 6.1 copy-start.36
  18.0 48.9 %collective-permute-start = (bf16[1024,1024]{0,1:T(8,128)(2,1)}, bf16[1024,1024]{0,1:T(8,128)(2,1)}, u32[]{:S(2)}, u32[]{:S(2)}) collective-permute-start(bf16[1024,1024]{0,1:T(8,128)(2,1)} %fusion.14), channel_id=1, source_target_pairs={{0,1},{1,0},{2,3},{3,2},{4,5},{5,4},{6,7},{7,6},{8,9},{9,8},{10,11... | collective-permute-start | bytes 6291464 | tf_op jit(solution)/shard_map/ppermute | solution.py:406
  21.0 796.1 %reduce-scatter.14.cloned.1.call-start = ((), (), s32[]{:S(2)}) async-start(), calls=%async_computation.11 | async-start | bytes 2162688 | tf_op jit(solution)/shard_map/reduce_scatter | solution.py:504
  78.6 11.7 %copy-start.38 = (bf16[2048,1664]{1,0:T(8,128)(2,1)S(1)}, bf16[2048,1664]{1,0:T(8,128)(2,1)}, u32[]{:S(2)}) copy-start(bf16[2048,1664]{1,0:T(8,128)(2,1)} %all-gather.6.cloned.1.call-done) | copy-start | bytes 20447236
  202.9 7.8 copy-start.41
  205.1 27.4 %collective-permute-start.1 = (bf16[2,1024,256]{2,1,0:T(8,128)(2,1)}, bf16[2,1024,256]{2,1,0:T(8,128)(2,1)S(1)}, u32[]{:S(2)}, u32[]{:S(2)}) collective-permute-start(bf16[2,1024,256]{2,1,0:T(8,128)(2,1)} %slice.152), channel_id=1, source_target_pairs={{0,1},{1,0},{2,3},{3,2},{4,5},{5,4},{6,7},{7,6},{8,9},{9,8},{10,11... | collective-permute-start | bytes 3145736 | tf_op jit(solution)/shard_map/ppermute | solution.py:406
  212.0 22.9 %copy-start.12 = (bf16[2,2048,256]{2,1,0:T(8,128)(2,1)S(1)}, bf16[2,2048,256]{2,1,0:T(8,128)(2,1)}, u32[]{:S(2)}) copy-start(bf16[2,2048,256]{2,1,0:T(8,128)(2,1)} %get-tuple-element.23) | copy-start | bytes 6291460
  212.0 22.9 %copy-start.14 = (bf16[4096,256]{0,1:T(8,128)(2,1)S(1)}, bf16[4096,256]{0,1:T(8,128)(2,1)}, u32[]{:S(2)}) copy-start(bf16[4096,256]{0,1:T(8,128)(2,1)} %all-gather.8.cloned.1.call-done) | copy-start | bytes 6291460
  238.0 191.8 %copy-start.23 = (f32[1024]{0:T(1024)}, f32[1024]{0:T(1024)S(1)}, u32[]{:S(2)}) copy-start(f32[1024]{0:T(1024)S(1)} %add_rsqrt_fusion) | copy-start | bytes 12292
  240.4 64.2 %copy-start.16 = (bf16[1024,1024]{0,1:T(8,128)(2,1)}, bf16[1024,1024]{0,1:T(8,128)(2,1)S(1)}, u32[]{:S(2)}) copy-start(bf16[1024,1024]{0,1:T(8,128)(2,1)S(1)} %multiply_convert_fusion.2) | copy-start | bytes 6291460
  290.0 4.7 copy-start.39
  290.0 8.0 slice-start
  308.4 58.3 %copy-start.8 = (bf16[1024,1024]{0,1:T(8,128)(2,1)S(1)}, bf16[1024,1024]{0,1:T(8,128)(2,1)}, u32[]{:S(2)}) copy-start(bf16[1024,1024]{0,1:T(8,128)(2,1)} %copy.94) | copy-start | bytes 6291460
  366.7 13.1 %copy-start.22 = (bf16[4096,704]{0,1:T(8,128)(2,1)S(1)}, bf16[4096,704]{0,1:T(8,128)(2,1)}, u32[]{:S(2)}) copy-start(bf16[4096,704]{0,1:T(8,128)(2,1)} %all-gather.14.cloned.1.call-done) | copy-start | bytes 17301508
  366.7 13.1 %copy-start.47 = (f32[1024,704]{0,1:T(8,128)S(1)}, f32[1024,704]{0,1:T(8,128)}, u32[]{:S(2)}) copy-start(f32[1024,704]{0,1:T(8,128)} %fusion.69) | copy-start | bytes 8650756
  366.7 13.1 %copy-start.48 = (f32[1024,704]{0,1:T(8,128)S(1)}, f32[1024,704]{0,1:T(8,128)}, u32[]{:S(2)}) copy-start(f32[1024,704]{0,1:T(8,128)} %fusion.73) | copy-start | bytes 8650756
  374.3 9.4 slice-start.2
  374.3 13.3 %slice-start.4 = ((s8[5767168]{0:T(1024)(128)(4,1)}), s8[4194304]{0:T(1024)(128)(4,1)S(1)}, s32[]{:S(2)}) async-start(s8[5767168]{0:T(1024)(128)(4,1)} %bitcast.131), calls=%async_computation.19 | async-start | bytes 8388608
  379.9 7.8 slice-start.5
  437.7 381.0 %reduce-scatter.18.cloned.1.call-start = ((), (), s32[]{:S(2)}) async-start(), calls=%async_computation.13 | async-start | bytes 6488064
  459.1 361.5 %reduce-scatter.16.cloned.1.call-start = ((), (), s32[]{:S(2)}) async-start(), calls=%async_computation.12 | async-start | bytes 6488064
  480.0 456.6 %reduce-scatter.20.cloned.1.call-start = ((), (), s32[]{:S(2)}) async-start(), calls=%async_computation.14 | async-start | bytes 6488064
  500.6 527.6 %reduce-scatter.12.cloned.1.call-start = ((), (), s32[]{:S(2)}) async-start(), calls=%async_computation.10 | async-start | bytes 7241728 | tf_op jit(solution)/shard_map/reduce_scatter | solution.py:525
  507.2 27.5 %collective-permute-start.2 = (bf16[2,1024,256]{2,1,0:T(8,128)(2,1)S(1)}, bf16[2,1024,256]{2,1,0:T(8,128)(2,1)S(1)}, u32[]{:S(2)}, u32[]{:S(2)}) collective-permute-start(bf16[2,1024,256]{2,1,0:T(8,128)(2,1)S(1)} %pad_maximum_fusion.8), channel_id=1, source_target_pairs={{0,1},{1,0},{2,3},{3,2},{4,5},{5,4},{6,7},{7,6},{8,9},{9,8},{10,11... | collective-permute-start | bytes 3145736 | tf_op jit(solution)/shard_map/ppermute | solution.py:406
  651.1 11.7 %copy-start.42 = (bf16[2,2048,1664]{2,1,0:T(8,128)(2,1)S(1)}, bf16[2,2048,1664]{2,1,0:T(8,128)(2,1)}, u32[]{:S(2)}) copy-start(bf16[2,2048,1664]{2,1,0:T(8,128)(2,1)} %get-tuple-element.28) | copy-start | bytes 40894468
  705.6 7.7 copy-start.9
  707.3 6.1 copy-start.54
  707.3 55.7 %collective-permute-start.3 = (bf16[1024,1024]{0,1:T(8,128)(2,1)}, bf16[1024,1024]{0,1:T(8,128)(2,1)}, u32[]{:S(2)}, u32[]{:S(2)}) collective-permute-start(bf16[1024,1024]{0,1:T(8,128)(2,1)} %slice.379), channel_id=1, source_target_pairs={{0,1},{1,0},{2,3},{3,2},{4,5},{5,4},{6,7},{7,6},{8,9},{9,8},{10,11... | collective-permute-start | bytes 6291464 | tf_op jit(solution)/shard_map/ppermute | solution.py:406
  713.4 5.6 copy-start.2
  713.4 5.6 copy-start.21
  726.0 4.2 copy-start.35
  726.0 4.9 copy-start.34
  726.0 37.0 %copy-start.5 = (bf16[1024,1024]{0,1:T(8,128)(2,1)S(1)}, bf16[1024,1024]{0,1:T(8,128)(2,1)}, u32[]{:S(2)}) copy-start(bf16[1024,1024]{0,1:T(8,128)(2,1)} %copy-done.4) | copy-start | bytes 6291460
  726.0 37.0 %copy-start.28 = (f32[1024]{0:T(1024)S(1)}, f32[1024]{0:T(1024)}, u32[]{:S(2)}) copy-start(f32[1024]{0:T(1024)} %copy-done.27) | copy-start | bytes 12292
  726.0 37.0 %copy-start.32 = (f32[1024]{0:T(1024)S(1)}, f32[1024]{0:T(1024)}, u32[]{:S(2)}) copy-start(f32[1024]{0:T(1024)} %param.33) | copy-start | bytes 12292
  733.6 33.5 %copy-start.3 = (f32[1024,1024]{0,1:T(8,128)S(1)}, f32[1024,1024]{0,1:T(8,128)}, u32[]{:S(2)}) copy-start(f32[1024,1024]{0,1:T(8,128)} %copy-done) | copy-start | bytes 12582916
  733.6 33.5 %copy-start.7 = (f32[1024,1024]{0,1:T(8,128)S(1)}, f32[1024,1024]{0,1:T(8,128)}, u32[]{:S(2)}) copy-start(f32[1024,1024]{0,1:T(8,128)} %copy-done.6) | copy-start | bytes 12582916
  733.6 33.5 %copy-start.24 = (f32[1024]{0:T(1024)S(1)}, f32[1024]{0:T(1024)}, u32[]{:S(2)}) copy-start(f32[1024]{0:T(1024)} %copy-done.23) | copy-start | bytes 12292
  733.6 33.5 %copy-start.26 = (f32[1024]{0:T(1024)S(1)}, f32[1024]{0:T(1024)}, u32[]{:S(2)}) copy-start(f32[1024]{0:T(1024)} %param.34) | copy-start | bytes 12292
  733.6 33.5 %copy-start.30 = (f32[1024]{0:T(1024)S(1)}, f32[1024]{0:T(1024)}, u32[]{:S(2)}) copy-start(f32[1024]{0:T(1024)} %copy-done.29) | copy-start | bytes 12292
  (40 other events, 119.1 us)
Sparse Core Ops, SparseCore 0:
  10.9 67.6 all-gather.5
  81.5 51.7 all-gather.7
  136.2 74.8 all-gather.11
  213.8 76.1 all-gather.9
  292.7 73.9 all-gather.13
  437.8 135.1 reduce-scatter.13
  579.6 111.2 reduce-scatter.17
  696.5 119.7 reduce-scatter.15
  822.9 113.7 reduce-scatter.19
  940.5 87.6 reduce-scatter.11

commit v2 on v1

--- a/solution.py
+++ b/solution.py
@@ -65,8 +65,8 @@
         self.width = self.r + 128
 
 
-def piece(ref, s, c, start):
-    return ref[s, c * CT : (c + 1) * CT, start : start + HEAD]
+def piece(refs, s, c, start):
+    return refs[s][c * CT : (c + 1) * CT, start : start + HEAD]
 
 
 def unit_silu(raw):
@@ -77,7 +77,7 @@
 
 
 def rates_of(pre_ref, par_ref, thin_ref, s, c, lay):
-    raw = pre_ref[s, c * CT : (c + 1) * CT, lay.r : lay.r + 128]
+    raw = pre_ref[s][c * CT : (c + 1) * CT, lay.r : lay.r + 128]
     shifted = raw + par_ref[s, 1:2, :]
     soft = jnp.maximum(shifted, 0.0) + jnp.log1p(jnp.exp(-jnp.abs(shifted)))
     decay = par_ref[s, 0:1, :] * soft
@@ -111,8 +111,11 @@
     )
 
 
-def forward_kernel(lay, nsq, heads, nb, _, pre_ref, par_ref, gain_ref, square_ref, thin_ref,
-                   mixed_ref, tinv_ref, state_ref, delta_ref, o_ref, carry):
+def forward_kernel(lay, nsq, heads, nb, _, *refs):
+    pre_ref = refs[:nsq]
+    par_ref, gain_ref, square_ref, thin_ref = refs[nsq : nsq + 4]
+    mixed_ref, tinv_ref, state_ref, delta_ref, o_ref, carry = refs[nsq + 4 :]
+
     @pl.when(pl.program_id(0) == 0)
     def _():
         carry[...] = jnp.zeros_like(carry)
@@ -172,9 +175,13 @@
     return sig * (1.0 + raw * (1.0 - sig))
 
 
-def backward_kernel(lay, nsq, heads, nb, _, pre_ref, par_ref, gain_ref, square_ref, thin_ref,
-                    tinv_ref, state_ref, delta_ref, o_ref, dm_ref,
-                    dpre_ref, small_ref, carry, acc):
+def backward_kernel(lay, nsq, heads, nb, _, *refs):
+    pre_ref = refs[:nsq]
+    par_ref, gain_ref, square_ref, thin_ref = refs[nsq : nsq + 4]
+    tinv_ref, state_ref, delta_ref, o_ref, dm_ref = refs[nsq + 4 : nsq + 9]
+    dpre_ref = refs[nsq + 9 : 2 * nsq + 9]
+    small_ref, carry, acc = refs[2 * nsq + 9 :]
+
     @pl.when(pl.program_id(0) == 0)
     def _():
         carry[...] = jnp.zeros_like(carry)
@@ -209,7 +216,7 @@
                 normed = out * scale
                 gain = gain_ref[0:1, :]
                 dgate = dm * normed * gain
-                dpre_ref[s, span, lay.g + h * HEAD : lay.g + (h + 1) * HEAD] = (
+                dpre_ref[s][span, lay.g + h * HEAD : lay.g + (h + 1) * HEAD] = (
                     dgate * silu_slope(graw, gsig)
                 ).astype(BF)
                 dn = dm * gate
@@ -269,18 +276,18 @@
                     part = slice(j * CT, (j + 1) * CT)
                     start = lay.k + (2 * h + j) * HEAD
                     kraw = piece(pre_ref, s, c, start)
-                    dpre_ref[s, span, start : start + HEAD] = (
+                    dpre_ref[s][span, start : start + HEAD] = (
                         dk[part] * p["nk"][j] * silu_slope(kraw, p["sk"][j])
                     ).astype(BF)
                     start = lay.v + (2 * h + j) * HEAD
                     vraw = piece(pre_ref, s, c, start)
-                    dpre_ref[s, span, start : start + HEAD] = (
+                    dpre_ref[s][span, start : start + HEAD] = (
                         dpv[part] * silu_slope(vraw, sigm(vraw))
                     ).astype(BF)
                 start = lay.q + h * HEAD
                 qraw = piece(pre_ref, s, c, start)
                 dq = (dquery - p["query"] * qdot) * p["nq"]
-                dpre_ref[s, span, start : start + HEAD] = (dq * silu_slope(qraw, p["sq"])).astype(BF)
+                dpre_ref[s][span, start : start + HEAD] = (dq * silu_slope(qraw, p["sq"])).astype(BF)
             sums = thin_ref[1]
             read_sum = dg_all[:CT] + dg_all[CT:] + dq_all
             col_rows = jnp.concatenate([dcol_all, jnp.zeros((120, 128), F32)], axis=0)
@@ -294,7 +301,7 @@
             dshift = ddecay * par_ref[s, 0:1, :] * sigm(shifted)
             acc[1 + s : 2 + s, :] += jnp.sum(dshift, axis=0, keepdims=True)
             acc[1 + nsq + s : 2 + nsq + s, :] += jnp.sum(ddecay * decay, axis=0, keepdims=True)
-            dpre_ref[s, span, lay.r : lay.r + 128] = (dshift + dbeta_all).astype(BF)
+            dpre_ref[s][span, lay.r : lay.r + 128] = (dshift + dbeta_all).astype(BF)
     small_ref[...] = acc[...]
 
 
@@ -312,7 +319,7 @@
 
 
 def mixer_forward(place, parts, pre, params, gain, heads, nb=2):
-    nsq, length, width = pre.shape
+    nsq, (length, width) = len(pre), pre[0].shape
     lay = Layout(heads)
     square, thin = mixer_tables()
     nchunk = length // CT
@@ -321,12 +328,13 @@
     per_part = nchunk // nb // parts
     big = lambda: pl.BlockSpec((nb, chains, ROWS, HEAD), lambda i, _: (i, 0, 0, 0))
     rows = lambda w: pl.BlockSpec((nsq, span, w), lambda i, place: (0, part_chunk(i, place, per_part), 0))
+    wide = lambda: pl.BlockSpec((span, width), lambda i, place: (part_chunk(i, place, per_part), 0))
     return pl.pallas_call(
         functools.partial(forward_kernel, lay, nsq, heads, nb),
         grid_spec=pltpu.PrefetchScalarGridSpec(
             num_scalar_prefetch=1,
             grid=(nchunk // nb,),
-            in_specs=[rows(width)] + shared_specs(square, thin, nsq),
+            in_specs=[wide() for _ in pre] + shared_specs(square, thin, nsq),
             out_specs=[rows(heads * HEAD), big(), big(), big(), rows(heads * HEAD)],
             scratch_shapes=[pltpu.VMEM((chains, HEAD, HEAD), F32)],
         ),
@@ -344,11 +352,11 @@
             transcendentals=0,
         ),
         name="mixer_forward",
-    )(place, pre, params, gain, jnp.asarray(square), jnp.asarray(thin))
+    )(place, *pre, params, gain, jnp.asarray(square), jnp.asarray(thin))
 
 
 def mixer_backward(place, parts, pre, params, gain, tinv, states, deltas, outs, dmixed, heads, nb=2):
-    nsq, length, width = pre.shape
+    nsq, (length, width) = len(pre), pre[0].shape
     lay = Layout(heads)
     square, thin = mixer_tables()
     nchunk = length // CT
@@ -360,22 +368,23 @@
     rows = lambda w: pl.BlockSpec(
         (nsq, span, w), lambda i, place: (0, part_chunk(last - i, place, per_part), 0)
     )
+    wide = lambda: pl.BlockSpec((span, width), lambda i, place: (part_chunk(last - i, place, per_part), 0))
     return pl.pallas_call(
         functools.partial(backward_kernel, lay, nsq, heads, nb),
         grid_spec=pltpu.PrefetchScalarGridSpec(
             num_scalar_prefetch=1,
             grid=(nchunk // nb,),
-            in_specs=[rows(width)]
+            in_specs=[wide() for _ in pre]
             + shared_specs(square, thin, nsq)
             + [big(), big(), big(), rows(heads * HEAD), rows(heads * HEAD)],
-            out_specs=[rows(width), pl.BlockSpec((8, 128), lambda i, _: (0, 0))],
+            out_specs=[wide() for _ in pre] + [pl.BlockSpec((8, 128), lambda i, _: (0, 0))],
             scratch_shapes=[
                 pltpu.VMEM((chains, HEAD, HEAD), F32),
                 pltpu.VMEM((8, 128), F32),
             ],
         ),
-        out_shape=[
-            jax.ShapeDtypeStruct((nsq, length, width), BF),
+        out_shape=[jax.ShapeDtypeStruct((length, width), BF) for _ in pre]
+        + [
             jax.ShapeDtypeStruct((8, 128), F32),
         ],
         compiler_params=pltpu.CompilerParams(vmem_limit_bytes=56 * 1024 * 1024),
@@ -385,21 +394,287 @@
             transcendentals=0,
         ),
         name="mixer_backward",
-    )(place, pre, params, gain, jnp.asarray(square), jnp.asarray(thin), tinv, states, deltas, outs, dmixed)
-
-
+    )(place, *pre, params, gain, jnp.asarray(square), jnp.asarray(thin), tinv, states, deltas, outs, dmixed)
+
+
+TILE = 256
+
+
+def token_mask(place, limit, tile, rows, base):
+    position = place * rows + base + lax.broadcasted_iota(jnp.int32, (tile, 1), 0)
+    return position < limit
+
+
+def join_kernel(parts, nsq, tok, scalars, *refs):
+    mixed_refs = refs[:parts]
+    x_ref, og_ref, wout_ref, gain_ref = refs[parts : parts + 4]
+    middle_ref, second_ref, grad_ref = refs[parts + 4 :]
+    place, limit = scalars[0], scalars[1]
+    total = x_ref[...].astype(F32)
+    for r in range(parts):
+        for s in range(nsq):
+            total = total + dot_nt(mixed_refs[r][s], wout_ref[s * parts + (place ^ r)])
+    middle_ref[...] = total
+    scale = lax.rsqrt(jnp.mean(total * total, axis=-1, keepdims=True) + EPS)
+    second_ref[...] = (total * scale * gain_ref[...]).astype(BF)
+    keep = token_mask(place, limit, x_ref.shape[0], tok, pl.program_id(0) * x_ref.shape[0])
+    grad_ref[...] = jnp.where(keep, og_ref[...].astype(F32), 0.0).astype(BF)
+
+
+def join(scalars, mixed_parts, x, out_grad, wall, gain, parts, nsq, hw):
+    tok, model = x.shape
+    count = parts * nsq
+    tile = min(TILE, tok)
+    row = pl.BlockSpec((tile, model), lambda i, _: (i, 0))
+    return pl.pallas_call(
+        functools.partial(join_kernel, parts, nsq, tok),
+        grid_spec=pltpu.PrefetchScalarGridSpec(
+            num_scalar_prefetch=1,
+            grid=(tok // tile,),
+            in_specs=[pl.BlockSpec((nsq, tile, hw), lambda i, _: (0, i, 0)) for _ in mixed_parts]
+            + [row, row, pl.BlockSpec((count, model, hw), lambda i, _: (0, 0, 0)),
+               pl.BlockSpec((1, model), lambda i, _: (0, 0))],
+            out_specs=[row, row, row],
+        ),
+        out_shape=[
+            jax.ShapeDtypeStruct((tok, model), F32),
+            jax.ShapeDtypeStruct((tok, model), BF),
+            jax.ShapeDtypeStruct((tok, model), BF),
+        ],
+        compiler_params=pltpu.CompilerParams(vmem_limit_bytes=40 * 1024 * 1024),
+        cost_estimate=pl.CostEstimate(
+            flops=2 * tok * model * count * hw, bytes_accessed=14 * tok * model, transcendentals=0
+        ),
+        name="join",
+    )(scalars, *mixed_parts, x, out_grad, wall, gain)
+
+
+def ff_kernel(tile, hw, units, sec_ref, grad_ref, w_ref, mlp_ref, sg_ref, dw_ref, hid, both):
+    tok, model = sec_ref.shape
+    mid, end = hw + 2 * units, hw + 3 * units
+
+    @pl.when(pl.program_id(0) == 0)
+    def _():
+        mlp_ref[...] = jnp.zeros_like(mlp_ref)
+        sg_ref[...] = jnp.zeros_like(sg_ref)
+
+    for m in range(tok // tile):
+        rows = slice(m * tile, (m + 1) * tile)
+        pre = dot_nn(sec_ref[rows, :], w_ref[0, :, hw:mid])
+        gate_pre, up_pre = pre[:, :units], pre[:, units:]
+        hidden_grad = dot_nn(grad_ref[rows, :], w_ref[0, :, mid:end])
+        sig = sigm(gate_pre)
+        act = gate_pre * sig
+        hidden = (act * up_pre).astype(BF)
+        hid[rows, :] = hidden
+        gate_low = (hidden_grad * up_pre * (sig + act * (1.0 - sig))).astype(BF)
+        up_low = (hidden_grad * act).astype(BF)
+        both_low = jnp.concatenate([gate_low, up_low], axis=1)
+        both[rows, :] = both_low
+        mlp_ref[rows, :] += dot_nt(hidden, w_ref[0, :, mid:end])
+        sg_ref[rows, :] += dot_nt(both_low, w_ref[0, :, hw:mid])
+    step = min(256, model)
+    for k in range(model // step):
+        cols = slice(k * step, (k + 1) * step)
+        dw_ref[0, cols, hw:mid] = dot_tn(sec_ref[:, cols], both[...]).astype(BF)
+        dw_ref[0, cols, mid:end] = dot_tn(grad_ref[:, cols], hid[...]).astype(BF)
+
+
+def feed_forward(second, grad_low, wall, hw, units):
+    tok, model = second.shape
+    count, _, width = wall.shape
+    whole = pl.BlockSpec((tok, model), lambda p: (0, 0))
+    weight = pl.BlockSpec((1, model, width), lambda p: (p, 0, 0))
+    return pl.pallas_call(
+        functools.partial(ff_kernel, min(TILE, tok), hw, units),
+        grid=(count,),
+        in_specs=[whole, whole, weight],
+        out_specs=[whole, whole, weight],
+        out_shape=[
+            jax.ShapeDtypeStruct((tok, model), F32),
+            jax.ShapeDtypeStruct((tok, model), F32),
+            jax.ShapeDtypeStruct((count, model, width), BF),
+        ],
+        scratch_shapes=[pltpu.VMEM((tok, units), BF), pltpu.VMEM((tok, 2 * units), BF)],
+        compiler_params=pltpu.CompilerParams(vmem_limit_bytes=62 * 1024 * 1024),
+        cost_estimate=pl.CostEstimate(
+            flops=18 * tok * model * units * count,
+            bytes_accessed=count * model * width * 4 + 12 * tok * model,
+            transcendentals=0,
+        ),
+        name="feed_forward",
+    )(second, grad_low, wall)
+
+
+def split_kernel(parts, nsq, tok, scalars, *refs):
+    middle_ref, mlp_ref, sg_ref, grad_ref, wout_ref, gain_ref = refs[:6]
+    out_ref, mg_ref, ml_ref, ln_ref = refs[6:10]
+    back_refs = refs[10:]
+    place, limit = scalars[0], scalars[1]
+    tile = middle_ref.shape[0]
+    middle = middle_ref[...]
+    keep = token_mask(place, limit, tile, tok, pl.program_id(0) * tile)
+    out_ref[...] = jnp.where(keep, middle + mlp_ref[...], 0.0).astype(BF)
+    scale = lax.rsqrt(jnp.mean(middle * middle, axis=-1, keepdims=True) + EPS)
+    normed = middle * scale
+    sg = sg_ref[...]
+
+    @pl.when(pl.program_id(0) == 0)
+    def _():
+        ln_ref[...] = jnp.zeros_like(ln_ref)
+
+    ln_ref[...] += jnp.sum(sg * normed, axis=0, keepdims=True)
+    scaled = sg * gain_ref[...]
+    back = scale * (scaled - normed * jnp.mean(scaled * normed, axis=-1, keepdims=True))
+    total = grad_ref[...].astype(F32) + back
+    mg_ref[...] = total
+    low = total.astype(BF)
+    ml_ref[...] = low
+    for r in range(parts):
+        for s in range(nsq):
+            back_refs[r][s] = dot_nn(low, wout_ref[s * parts + (place ^ r)]).astype(BF)
+
+
+def split(scalars, middle, mlp, second_grad, grad_low, wall, gain, parts, nsq, hw):
+    tok, model = middle.shape
+    count = parts * nsq
+    tile = min(TILE, tok)
+    row = pl.BlockSpec((tile, model), lambda i, _: (i, 0))
+    line = pl.BlockSpec((1, model), lambda i, _: (0, 0))
+    return pl.pallas_call(
+        functools.partial(split_kernel, parts, nsq, tok),
+        grid_spec=pltpu.PrefetchScalarGridSpec(
+            num_scalar_prefetch=1,
+            grid=(tok // tile,),
+            in_specs=[row, row, row, row, pl.BlockSpec((count, model, hw), lambda i, _: (0, 0, 0)), line],
+            out_specs=[row, row, row, line]
+            + [pl.BlockSpec((nsq, tile, hw), lambda i, _: (0, i, 0)) for _ in range(parts)],
+        ),
+        out_shape=[
+            jax.ShapeDtypeStruct((tok, model), BF),
+            jax.ShapeDtypeStruct((tok, model), F32),
+            jax.ShapeDtypeStruct((tok, model), BF),
+            jax.ShapeDtypeStruct((1, model), F32),
+        ]
+        + [jax.ShapeDtypeStruct((nsq, tok, hw), BF) for _ in range(parts)],
+        compiler_params=pltpu.CompilerParams(vmem_limit_bytes=40 * 1024 * 1024),
+        cost_estimate=pl.CostEstimate(
+            flops=2 * tok * model * count * hw, bytes_accessed=26 * tok * model, transcendentals=0
+        ),
+        name="split",
+    )(scalars, middle, mlp, second_grad, grad_low, wall, gain)
+
+
+def out_grad_kernel(scalars, ml_ref, mixed_ref, full_ref, dw_ref):
+    model = ml_ref.shape[1]
+    step = min(256, model)
+    for k in range(model // step):
+        cols = slice(k * step, (k + 1) * step)
+        dw_ref[0, cols, :] = dot_tn(ml_ref[:, cols], mixed_ref[0]).astype(BF)
+
+
+def out_proj_grad(scalars, middle_low, mixed_part, full, r, parts, nsq, hw):
+    tok, model = middle_low.shape
+    return pl.pallas_call(
+        out_grad_kernel,
+        grid_spec=pltpu.PrefetchScalarGridSpec(
+            num_scalar_prefetch=1,
+            grid=(nsq,),
+            in_specs=[
+                pl.BlockSpec((tok, model), lambda s, _: (0, 0)),
+                pl.BlockSpec((1, tok, hw), lambda s, _: (s, 0, 0)),
+                pl.BlockSpec(memory_space=pl.ANY),
+            ],
+            out_specs=pl.BlockSpec((1, model, hw), lambda s, sc: (s * parts + (sc[0] ^ r), 0, 0)),
+        ),
+        out_shape=jax.ShapeDtypeStruct(full.shape, BF),
+        input_output_aliases={3: 0},
+        compiler_params=pltpu.CompilerParams(vmem_limit_bytes=40 * 1024 * 1024),
+        cost_estimate=pl.CostEstimate(
+            flops=2 * tok * model * nsq * hw, bytes_accessed=2 * tok * model * 2, transcendentals=0
+        ),
+        name="out_proj_grad",
+    )(scalars, middle_low, mixed_part, full)
+
+
+def pack_kernel(lay, q_ref, k_ref, v_ref, r_ref, g_ref, out_ref, gate_ref, up_ref, down_ref, mix_ref, all_ref):
+    mix_ref[:, lay.q : lay.k] = q_ref[...]
+    mix_ref[:, lay.k : lay.v] = k_ref[...]
+    mix_ref[:, lay.v : lay.g] = v_ref[...]
+    mix_ref[:, lay.g : lay.r] = g_ref[...]
+    mix_ref[:, lay.r : lay.width] = jnp.zeros((mix_ref.shape[0], 128), BF)
+    mix_ref[:, lay.r : lay.r + r_ref.shape[1]] = r_ref[...]
+    hw, units = out_ref.shape[0], gate_ref.shape[1]
+    all_ref[:, 0:hw] = out_ref[...].astype(F32).T.astype(BF)
+    all_ref[:, hw : hw + units] = gate_ref[...]
+    all_ref[:, hw + units : hw + 2 * units] = up_ref[...]
+    all_ref[:, hw + 2 * units : hw + 3 * units] = down_ref[...].astype(F32).T.astype(BF)
+
+
+def pack(lay, w_query, w_key, w_value, w_rates, w_outgate, w_out, w_gate, w_up, w_down):
+    rows = w_query.shape[0]
+    return pl.pallas_call(
+        functools.partial(pack_kernel, lay),
+        out_shape=[
+            jax.ShapeDtypeStruct((rows, lay.width), BF),
+            jax.ShapeDtypeStruct((rows, w_out.shape[0] + 3 * w_gate.shape[1]), BF),
+        ],
+        name="pack",
+    )(w_query, w_key, w_value, w_rates, w_outgate, w_out, w_gate, w_up, w_down)
 def rms_parts(values):
     scale = lax.rsqrt(jnp.mean(values * values, axis=-1, keepdims=True) + EPS)
     return values * scale, scale
 
 
-def rms_back(grad_out, values, scale, gain):
-    gain_grad = jnp.sum(grad_out * values * scale, axis=0)
-    scaled = grad_out * gain
-    value_grad = scale * scaled - values * scale * scale * scale * jnp.mean(
-        scaled * values, axis=-1, keepdims=True
-    )
-    return value_grad, gain_grad
+def bits(axis):
+    return [1 << k for k in range((lax.axis_size(axis) - 1).bit_length())]
+
+
+def trade(values, axis, bit):
+    return lax.ppermute(values, axis, [(i, i ^ bit) for i in range(lax.axis_size(axis))])
+
+
+def everyone(values):
+    for axis in ("sub", "sq", "dp"):
+        for bit in bits(axis):
+            values = values + trade(values, axis, bit)
+    return values
+
+
+def plus(left, right):
+    return (left.astype(F32) + right.astype(F32)).astype(BF)
+
+
+def scatter_mix(grads, which_seq):
+    dp = lax.axis_size("dp")
+    me = lax.axis_index("dp")
+    nbits = len(bits("dp"))
+    width = grads[0].shape[1]
+    shaped = [g.reshape((2,) * nbits + (-1, width)) for g in grads]
+
+    def halves(values, k):
+        axis, mine = nbits - 1 - k, (me >> k) & 1
+        part = lambda i: lax.dynamic_index_in_dim(values, i, axis, keepdims=True)
+        return part(mine), part(1 - mine)
+
+    kept = []
+    for g in shaped:
+        keep, send = halves(g, 0)
+        kept.append(plus(keep, trade(send, "dp", 1)))
+    if len(kept) == 2:
+        keep = jnp.where(which_seq == 0, kept[0], kept[1])
+        send = jnp.where(which_seq == 0, kept[1], kept[0])
+        keep_near, keep_far = halves(keep, 1)
+        send_near, send_far = halves(send, 1)
+        far = plus(keep_far, trade(send_far, "sq", 1))
+        near = plus(keep_near, trade(send_near, "sq", 1))
+    else:
+        near, far = halves(kept[0], 1)
+    value = plus(near, trade(far, "dp", 2))
+    for k in range(2, nbits):
+        keep, send = halves(value, k)
+        value = plus(keep, trade(send, "dp", 1 << k))
+    return value.reshape(-1, width)
 
 
 def swap(values, which, parts):
@@ -427,20 +702,19 @@
     hw = heads * HEAD
     place_arr = place.astype(jnp.int32).reshape(1)
 
-    rates_pad = jnp.zeros((w_rates.shape[0], 128 - w_rates.shape[1]), BF)
-    mix_shard = jnp.concatenate([w_query, w_key, w_value, w_outgate, w_rates, rates_pad], axis=1)
+    mix_shard, all_shard = pack(
+        lay, w_query, w_key, w_value, w_rates, w_outgate, w_out, w_gate, w_up, w_down
+    )
     w_mix = lax.all_gather(mix_shard, ("sq", "dp"), axis=0, tiled=True).reshape(nsq, model, lay.width)
-
-    def everywhere(shard):
-        full = lax.all_gather(shard, ("sq", "sub", "dp"), axis=0, tiled=True)
-        return full.reshape(count, model, shard.shape[1])
+    wall = lax.all_gather(all_shard, ("sq", "sub", "dp"), axis=0, tiled=True)
+    wall = wall.reshape(count, model, all_shard.shape[1])
 
     resid_in = tokens.astype(F32)
     normed_one, scale_one = rms_parts(resid_in)
     first = (normed_one * ln1_gain).astype(BF)
     first_seq = jnp.concatenate([first] + [swap(first, r, parts) for r in range(1, parts)], axis=0)
 
-    pre = jnp.stack([dot_nn(first_seq, w_mix[s]) for s in range(nsq)])
+    pre = [dot_nn(first_seq, w_mix[s]) for s in range(nsq)]
     hpos = [(s * parts + place) * heads for s in range(nsq)]
     lanes = 3 * np.arange(heads) + 2
 
@@ -452,85 +726,42 @@
     gain = onorm_gain.reshape(1, HEAD)
     mixed, tinv, states, deltas, outs = mixer_forward(place_arr, parts, pre, params, gain, heads)
 
-    w_out_t = everywhere(w_out.T)
-    w_gate_f = everywhere(w_gate)
-    w_up_f = everywhere(w_up)
-    w_down_t = everywhere(w_down.T)
-
-    got = []
+    got = [mixed] + [swap(mixed[:, r * tok_dev : (r + 1) * tok_dev], r, parts) for r in range(1, parts)]
+
+    limit = jnp.sum(jnp.where(jnp.arange(nsq) == which_seq, lengths, 0)).astype(jnp.int32)
+    scalars = jnp.stack([place.astype(jnp.int32), limit])
+    middle, second, grad_low = join(
+        scalars, got, tokens, out_grad, wall, ln2_gain.reshape(1, model), parts, nsq, hw
+    )
+    mlp, second_grad, grads = feed_forward(second, grad_low, wall, hw, units)
+    block_out, middle_grad, middle_low, ln2_grad, *back = split(
+        scalars, middle, mlp, second_grad, grad_low, wall, ln2_gain.reshape(1, model), parts, nsq, hw
+    )
     for r in range(parts):
-        mine = mixed[:, r * tok_dev : (r + 1) * tok_dev]
-        got.append(mine if r == 0 else swap(mine, r, parts))
-    keys = [place ^ r for r in range(parts)]
-    mixed_of = {}
-    for s in range(nsq):
-        for j in range(parts):
-            mixed_of[s * parts + j] = pick([g[s] for g in got], j, keys)
-    attn = dot_nt(mixed_of[0], w_out_t[0])
-    for p in range(1, count):
-        attn = attn + dot_nt(mixed_of[p], w_out_t[p])
-
-    position = place * tok_dev + jnp.arange(tok_dev)
-    limit = jnp.sum(jnp.where(jnp.arange(nsq) == which_seq, lengths, 0))
-    mask = (position < limit).astype(F32)[:, None]
-    middle = resid_in + attn
-    normed_two, scale_two = rms_parts(middle)
-    second = (normed_two * ln2_gain).astype(BF)
-    grad_low = (out_grad.astype(F32) * mask).astype(BF)
-    grad_top = grad_low.astype(F32)
-    mlp = None
-    second_grad = None
-    gate_grads, up_grads, down_grads = [], [], []
-    for p in range(count):
-        gate_pre = dot_nn(second, w_gate_f[p])
-        up_pre = dot_nn(second, w_up_f[p])
-        gate_sig = sigm(gate_pre)
-        gate_act = gate_pre * gate_sig
-        hidden = (gate_act * up_pre).astype(BF)
-        part = dot_nt(hidden, w_down_t[p])
-        mlp = part if mlp is None else mlp + part
-        hidden_grad = dot_nn(grad_low, w_down_t[p])
-        down_grads.append(dot_tn(grad_low, hidden))
-        up_low = (hidden_grad * gate_act).astype(BF)
-        gate_low = (hidden_grad * up_pre * silu_slope(gate_pre, gate_sig)).astype(BF)
-        gate_grads.append(dot_tn(second, gate_low))
-        up_grads.append(dot_tn(second, up_low))
-        part = dot_nt(gate_low, w_gate_f[p]) + dot_nt(up_low, w_up_f[p])
-        second_grad = part if second_grad is None else second_grad + part
-    block_out = ((middle + mlp) * mask).astype(BF)
-
-    def owned(grads):
-        full = jnp.concatenate([g.astype(BF) for g in grads], axis=0)
-        return lax.psum_scatter(full, ("sq", "sub", "dp"), scatter_dimension=0, tiled=True).astype(F32)
-
-    gate_own, up_own, down_own = owned(gate_grads), owned(up_grads), owned(down_grads).T
-
-    middle_back, ln2_grad = rms_back(second_grad, middle, scale_two, ln2_gain)
-    middle_grad = grad_top + middle_back
-    middle_low = middle_grad.astype(BF)
-    out_own = owned([dot_tn(middle_low, mixed_of[p]) for p in range(count)]).T
-    mixed_grad = [dot_nn(middle_low, w_out_t[p]).astype(BF) for p in range(count)]
-    back = []
-    for r in range(parts):
-        piece_r = jnp.stack(
-            [pick([mixed_grad[s * parts + j] for j in range(parts)], place ^ r, list(range(parts))) for s in range(nsq)]
-        )
-        back.append(piece_r if r == 0 else swap(piece_r, r, parts))
-    dmixed = jnp.concatenate(back, axis=1)
-    dpre, small = mixer_backward(
+        grads = out_proj_grad(scalars, middle_low, got[r], grads, r, parts, nsq, hw)
+    dmixed = jnp.concatenate([back[0]] + [swap(back[r], r, parts) for r in range(1, parts)], axis=1)
+    dmixed, grads = lax.optimization_barrier((dmixed, grads))
+    own = lax.psum_scatter(
+        grads.reshape(count * model, -1), ("sq", "sub", "dp"), scatter_dimension=0, tiled=True
+    ).astype(F32)
+    own_out, own_gate = own[:, :hw].T, own[:, hw : hw + units]
+    own_up, own_down = own[:, hw + units : hw + 2 * units], own[:, hw + 2 * units :].T
+
+    *dpre, small = mixer_backward(
         place_arr, parts, pre, params, gain, tinv, states, deltas, outs, dmixed, heads
     )
 
-    mix_grads = jnp.concatenate([dot_tn(first_seq, dpre[s]).astype(BF) for s in range(nsq)], axis=0)
-    mix_own = lax.psum_scatter(mix_grads, ("sq", "dp"), scatter_dimension=0, tiled=True).astype(F32)
+    mix_own = scatter_mix([dot_tn(first_seq, dpre[s]).astype(BF) for s in range(nsq)], which_seq).astype(F32)
     first_all = dot_nt(dpre[0], w_mix[0])
     for s in range(1, nsq):
         first_all = first_all + dot_nt(dpre[s], w_mix[s])
     first_low = first_all.astype(BF)
+    ln1_grad = jnp.sum(first_all * first_seq.astype(F32), axis=0) / ln1_gain
     first_grad = first_all[:tok_dev]
     for r in range(1, parts):
         first_grad = first_grad + swap(first_low[r * tok_dev : (r + 1) * tok_dev], r, parts).astype(F32)
-    input_back, ln1_grad = rms_back(first_grad, resid_in, scale_one, ln1_gain)
+    scaled = first_grad * ln1_gain
+    input_back = scale_one * (scaled - normed_one * jnp.mean(scaled * normed_one, axis=-1, keepdims=True))
     tokens_grad = (middle_grad + input_back).astype(BF)
 
     def gather_heads(rows):
@@ -541,12 +772,13 @@
 
     a_grad = gather_heads(small[1 + nsq : 1 + 2 * nsq])
     dt_grad = gather_heads(small[1 : 1 + nsq])
-    total = lax.psum((ln1_grad, ln2_grad, small[0], a_grad, dt_grad), ("dp", "sq", "sub"))
+    total = everyone(jnp.concatenate([ln1_grad, ln2_grad[0], small[0], a_grad, dt_grad]))
+    marks = np.cumsum([0, model, model, HEAD, a_log.shape[0], a_log.shape[0]])
     return (
-        block_out, tokens_grad, total[0], total[1], total[2], total[3], total[4],
+        block_out, tokens_grad, *[total[i:j] for i, j in zip(marks[:-1], marks[1:])],
         mix_own[:, lay.q : lay.k], mix_own[:, lay.k : lay.v], mix_own[:, lay.v : lay.g],
         mix_own[:, lay.r : lay.r + w_rates.shape[1]], mix_own[:, lay.g : lay.r],
-        out_own, gate_own, up_own, down_own,
+        own_out, own_gate, own_up, own_down,
     )
 
 

time: 1040 us -> 652 us (0.63)
  waiting for transfers between devices: 429 us -> 195 us
  matrix products: 225 us -> 78.3 us
  Pallas kernels: 200 us -> 295 us
  blocking collectives: 39.3 us -> 0 us
  local copies, waits for them, and re-layouts: 70.7 us -> 33.5 us
  other arithmetic: 52.1 us -> 20.5 us
    unnamed x13 -> x4, waiting for transfers between devices: 116 us -> 0.73 us
    ppermute x0 -> x11, waiting for transfers between devices: none -> 96.7 us  [trade(): lax.ppermute(values, axis, [(i, i ^ bit) for i in range(lax.axis_size(axi...]
    pallas_call x0 -> x6, Pallas kernels: none -> 94.9 us  [the longest x1 68.9 us: feed_forward(): pl.pallas_call(functools.partial(ff_kernel, min(TILE, tok), hw, units), g...]
    all_gather x4 -> x1, waiting for transfers between devices: 93 us -> 0.01 us  [per_device(): wall = lax.all_gather(all_shard, ('sq', 'sub', 'dp'), axis=0, tiled=True)]
    reduce_scatter x2 -> x0, waiting for transfers between devices: 89.7 us -> none  [the longest x1 89.7 us: per_device(): lax.psum_scatter(mix_grads, ('sq', 'dp'), scatter_dimension=0, tiled=True)]
    dot_general x18 -> x2, matrix products: 94.6 us -> 28.8 us  [dot_nt(): lax.dot_general(left, right, (((1,), (1,)), ((), ())), preferred_element_...]
    dot_general x18 -> x2, matrix products: 80.4 us -> 27.3 us  [dot_nn(): return jnp.dot(left, right, preferred_element_type=F32)]
    unnamed x161 -> x61, local copies, waits for them, and re-layouts: 54.5 us -> 14.6 us
  transfers between devices with their start and end apart: 14 -> 18, of which waited for: 9 -> 12; matrix products, arithmetic and copies ran while one was open for 25% -> 18% of each run, Pallas kernels for 19% -> 32%
where the time goes in v2:
time: 652 us; the launch traced here: 649 us
  Pallas kernels  295 us (45%)
  waiting for transfers between devices  195 us (30%)
  matrix products  78.3 us (12%)
  local copies, waits for them, and re-layouts  33.5 us (5%)
  other arithmetic  20.5 us (3%)
  between operations  14.3 us (2%)
  starting transfers between devices  12.7 us (2%)
    pallas_call x1, Pallas kernels, mixer_backward(): pl.pallas_call(functools.partial(backward_kernel, lay, nsq, heads, nb), g...  115 us
    ppermute x11, waiting for transfers between devices, trade(): lax.ppermute(values, axis, [(i, i ^ bit) for i in range(lax.axis_size(axi...  96.7 us
    pallas_call x1, Pallas kernels, mixer_forward(): pl.pallas_call(functools.partial(forward_kernel, lay, nsq, heads, nb), gr...  85 us
    ppermute x4, waiting for transfers between devices, swap(): return lax.ppermute(values, 'sub', [(i, i ^ which) for i in range(parts)])  81.8 us
    pallas_call x1, Pallas kernels, feed_forward(): pl.pallas_call(functools.partial(ff_kernel, min(TILE, tok), hw, units), g...  68.9 us
    dot_general x2, matrix products, dot_nt(): lax.dot_general(left, right, (((1,), (1,)), ((), ())), preferred_element_...  28.8 us
    dot_general x2, matrix products, dot_nn(): return jnp.dot(left, right, preferred_element_type=F32)  27.3 us
    dot_general x2, matrix products, dot_tn(): lax.dot_general(left, right, (((0,), (0,)), ((), ())), preferred_element_...  22.3 us
  transfers between devices with their start and end apart: 18, of which 12 were waited for; matrix products, arithmetic and copies ran while one was open for 18% of the time, Pallas kernels for 32%

profile of v2, /device:TPU:0, one launch (start us, length us, event | category | flops | bytes accessed | tf_op | source)
XLA Modules:
  0.0 648.9 jit_solution(10999317029172859314)
XLA Ops:
  7.2 1.9 copy.59.gate_ref
  9.1 1.7 copy.60.up_ref
  10.9 1.4 copy.58.r_ref
  12.3 2.5 pack.1
  16.1 1.9 fusion.3
  18.0 2.9 collective-permute-start
  24.6 42.2 %collective-permute-done = bf16[1024,1024]{1,0:T(8,128)(2,1)} collective-permute-done((bf16[1024,1024]{1,0:T(8,128)(2,1)}, bf16[1024,1024]{1,0:T(8,128)(2,1)}, u32[]{:S(2)}, u32[]{:S(2)}) %collective-permute-start) | collective-permute-done | bytes 2097184 | tf_op jit(solution)/shard_map/ppermute | solution.py:681
  66.8 15.8 %all-gather.3.cloned.1.call-done = bf16[2048,1664]{1,0:T(8,128)(2,1)} async-done(((bf16[128,1664]{1,0:T(8,128)(2,1)}), bf16[2048,1664]{1,0:T(8,128)(2,1)}) %all-gather.3.cloned.1.call-update) | async-done | bytes 6815760 | tf_op jit(solution)/shard_map/all_gather | solution.py:708
  82.6 14.2 %fusion.12.refs_1_ = f32[2048,1664]{1,0:T(8,128)} fusion(bf16[2048,1664]{1,0:T(8,128)(2,1)} %all-gather.3.cloned.1.call-done, bf16[1024,1024]{1,0:T(8,128)(2,1)} %collective-permute-done, bf16[1024,1024]{1,0:T(8,128)(2,1)} %fusion.3), kind=kOutput, calls=%fused_computation.31 | convolution fusion | flops 6987710464 | bytes 21233664 | tf_op jit(solution)/shard_map/dot_general | solution.py:22
  96.8 13.1 %fusion.16.refs_0_ = f32[2048,1664]{1,0:T(8,128)} fusion(bf16[2048,1664]{1,0:T(8,128)(2,1)S(1)} %copy-done.22, bf16[1024,1024]{1,0:T(8,128)(2,1)} %collective-permute-done, bf16[1024,1024]{1,0:T(8,128)(2,1)} %fusion.3), kind=kOutput, calls=%fused_computation.35 | convolution fusion | flops 6987710464 | bytes 21233664 | tf_op jit(solution)/shard_map/dot_general | solution.py:22
  109.9 85.0 %mixer_forward.1 = (bf16[2,2048,256]{2,1,0:T(8,128)(2,1)}, bf16[32,4,128,128]{3,2,1,0:T(8,128)(2,1)}, bf16[32,4,128,128]{3,2,1,0:T(8,128)(2,1)}, bf16[32,4,128,128]{3,2,1,0:T(8,128)(2,1)}, f32[2,2048,256]{2,1,0:T(8,128)}) custom-call(s32[1]{0:T(128)} %bitcast._, f32[2048,1664]{1,0:T(8,128)} %fusion.16.refs_0_, f32[2048,1664]{1,0:T(8,128)} %fusion.12.refs_1_, ...), custom_call_target="tpu_custom_call" | custom-call | flops 10737418240 | bytes 46137344 | tf_op jit(solution)/shard_map/mixer_forward/pallas_call | solution.py:332
  194.9 2.3 slice.72
  197.2 1.5 collective-permute-start.1
  200.0 22.7 %collective-permute-done.1.refs_1_.mixed_ref = bf16[2,1024,256]{2,1,0:T(8,128)(2,1)S(1)} collective-permute-done((bf16[2,1024,256]{2,1,0:T(8,128)(2,1)}, bf16[2,1024,256]{2,1,0:T(8,128)(2,1)S(1)}, u32[]{:S(2)}, u32[]{:S(2)}) %collective-permute-start.1) | collective-permute-done | bytes 1048608 | tf_op jit(solution)/shard_map/ppermute | solution.py:681
  222.7 1.6 copy-done.2
  224.3 1.6 copy-done.6
  225.9 7.4 %join.1 = (f32[1024,1024]{1,0:T(8,128)}, bf16[1024,1024]{1,0:T(8,128)(2,1)S(1)}, bf16[1024,1024]{1,0:T(8,128)(2,1)S(1)}) custom-call(s32[2]{0:T(128)S(1)} %pad_add_fusion.scalars, bf16[2,2048,256]{2,1,0:T(8,128)(2,1)S(1)} %copy-done.2, bf16[2,1024,256]{2,1,0:T(8,128)(2,1)S(1)} %collective-permute-done.1.refs_1_.mixed_ref, bf16[1024,1024]{1,0:T(8,128)(2,1)S(1)} %copy-done, ...), custom_call_target="tpu_custom_call" | custom-call | flops 2147483648 | bytes 14680064 | tf_op jit(solution)/shard_map/join/pallas_call | solution.py:429
  233.3 1.3 copy-done.7
  234.6 1.3 copy-done.10
  236.0 68.9 %feed_forward.1 = (f32[1024,1024]{1,0:T(8,128)}, f32[1024,1024]{1,0:T(8,128)}, bf16[4,1024,2368]{2,1,0:T(8,128)(2,1)}) custom-call(bf16[1024,1024]{1,0:T(8,128)(2,1)} %copy-done.10, bf16[1024,1024]{1,0:T(8,128)(2,1)} %copy-done.7, bf16[4,1024,2368]{2,1,0:T(8,128)(2,1)} %bitcast.38), custom_call_target="tpu_custom_call" | custom-call | flops 53150220288 | bytes 51380224 | tf_op jit(solution)/shard_map/feed_forward/pallas_call | solution.py:488
  304.9 1.6 copy-done.8
  306.5 10.1 %split.1 = (bf16[1024,1024]{1,0:T(8,128)(2,1)}, f32[1024,1024]{1,0:T(8,128)S(1)}, bf16[1024,1024]{1,0:T(8,128)(2,1)S(1)}, f32[1,1024]{1,0:T(1,128)S(1)}, bf16[2,...) custom-call(s32[2]{0:T(128)S(1)} %pad_add_fusion.scalars, f32[1024,1024]{1,0:T(8,128)} %get-tuple-element.43.refs_0_, ...), custom_call_target="tpu_custom_call" | custom-call | flops 2147483648 | bytes 27262976 | tf_op jit(solution)/shard_map/split/pallas_call | solution.py:544
  316.5 1.5 collective-permute-start.2
  318.1 3.0 out_proj_grad.2.full_ref
  321.0 3.1 out_proj_grad.3
  324.1 16.9 %collective-permute-done.2 = bf16[2,1024,256]{2,1,0:T(8,128)(2,1)S(1)} collective-permute-done((bf16[2,1024,256]{2,1,0:T(8,128)(2,1)S(1)}, bf16[2,1024,256]{2,1,0:T(8,128)(2,1)S(1)}, u32[]{:S(2)}, u32[]{:S(2)}) %collective-permute-start.2) | collective-permute-done | bytes 1048608 | tf_op jit(solution)/shard_map/ppermute | solution.py:681
  341.1 1.5 pad_maximum_fusion.1.refs_10_
  342.6 114.6 %mixer_backward.1 = (bf16[2048,1664]{1,0:T(8,128)(2,1)}, bf16[2048,1664]{1,0:T(8,128)(2,1)}, f32[8,128]{1,0:T(8,128)}) custom-call(s32[1]{0:T(128)} %bitcast._, f32[2048,1664]{1,0:T(8,128)} %fusion.16.refs_0_, f32[2048,1664]{1,0:T(8,128)} %fusion.12.refs_1_, f32[2,2,128]{2,1,0:T(2,128)} %pad_maximum_fusion.2.refs_2_, f32[1,128]{1,0:T(1,128)} %bitcast.51, ...), custom_call_target="tpu_custom_call" | custom-call | flops 13958643712 | bytes 59768832 | tf_op jit(solution)/shard_map/mixer_backward/pallas_call | solution.py:372
  457.2 12.1 %convolution_convert_fusion = bf16[1024,1664]{1,0:T(8,128)(2,1)S(1)} fusion(bf16[2048,1664]{1,0:T(8,128)(2,1)} %get-tuple-element.60, bf16[1024,1024]{1,0:T(8,128)(2,1)} %collective-permute-done, bf16[1024,1024]{1,0:T(8,128)(2,1)} %fusion.3), kind=kOutput, calls=%fused_computation.25 | convolution fusion | flops 6989414400 | bytes 14417920 | tf_op jit(solution)/shard_map/dot_general | solution.py:30
  469.5 10.2 %convolution_convert_fusion.1 = bf16[1024,1664]{1,0:T(8,128)(2,1)S(1)} fusion(bf16[2048,1664]{1,0:T(8,128)(2,1)S(1)} %copy-done.25, bf16[1024,1024]{1,0:T(8,128)(2,1)} %collective-permute-done, bf16[1024,1024]{1,0:T(8,128)(2,1)} %fusion.3), kind=kOutput, calls=%fused_computation.26 | convolution fusion | flops 6989414400 | bytes 14417920 | tf_op jit(solution)/shard_map/dot_general | solution.py:30
  479.8 1.3 constant_dynamic-slice_fusion.3
  481.4 10.6 %fusion.14 = f32[2048,1024]{1,0:T(8,128)} fusion(bf16[2048,1664]{1,0:T(8,128)(2,1)S(1)} %copy-done.25, bf16[2048,1664]{1,0:T(8,128)(2,1)S(1)} %bitcast.49), kind=kOutput, calls=%fused_computation.33 | convolution fusion | flops 6979321856 | bytes 18612224 | tf_op jit(solution)/shard_map/dot_general | solution.py:26
  491.9 18.2 %multiply_reduce_fusion = (f32[1024]{0:T(1024)S(1)}, f32[2048,1024]{1,0:T(8,128)S(1)}) fusion(bf16[1024,1024]{1,0:T(8,128)(2,1)} %collective-permute-done, bf16[1024,1024]{1,0:T(8,128)(2,1)} %fusion.3, f32[2048,1024]{1,0:T(8,128)} %fusion.14, bf16[2048,1664]{1,0:T(8,128)(2,1)} %get-tuple-element.60, bf16[2048,1664]{1,0:T(8,128)(2,1)} %all-gather.3.cloned.1.call-done), kind=kOutput, calls=%fused_computation.8 | convolution fusion | flops 6994000896 | bytes 31199232 | tf_op jit(solution)/shard_map/dot_general | solution.py:26
  510.2 1.9 slice.137
  512.1 1.6 collective-permute-start.3
  513.6 4.4 broadcast_select_fusion.1
  523.3 1.6 collective-permute-start.4
  524.9 57.2 %collective-permute-done.4 = f32[2192]{0:T(1024)S(1)} collective-permute-done((f32[2192]{0:T(1024)S(1)}, f32[2192]{0:T(1024)S(1)}, u32[]{:S(2)}, u32[]{:S(2)}) %collective-permute-start.4) | collective-permute-done | bytes 8800 | tf_op jit(solution)/shard_map/ppermute | solution.py:634
  583.1 2.7 collective-permute-done.5
  587.0 3.7 collective-permute-done.7
  590.7 4.6 collective-permute-done.8
  596.9 1.7 add_convert_fusion.3
  599.8 4.1 fusion.4
  604.0 10.6 %collective-permute-done.11 = bf16[2,1,1,128,1664]{4,3,2,1,0:T(8,128)(2,1)S(1)} collective-permute-done((bf16[2,1,1,128,1664]{4,3,2,1,0:T(8,128)(2,1)S(1)}, bf16[2,1,1,128,1664]{4,3,2,1,0:T(8,128)(2,1)S(1)}, u32[]{:S(2)}, u32[]{:S(2)}) %collective-permute-start.11) | collective-permute-done | bytes 852000 | tf_op jit(solution)/shard_map/ppermute | solution.py:634
  614.6 2.5 collective-permute-done.13
  617.8 3.9 fusion.8
  621.7 14.2 %collective-permute-done.14 = bf16[1,1,1,128,1664]{4,3,2,1,0:T(8,128)(2,1)S(1)} collective-permute-done((bf16[1,1,1,128,1664]{4,3,2,1,0:T(8,128)(2,1)S(1)}, bf16[1,1,1,128,1664]{4,3,2,1,0:T(8,128)(2,1)S(1)}, u32[]{:S(2)}, u32[]{:S(2)}) %collective-permute-start.14) | collective-permute-done | bytes 426016 | tf_op jit(solution)/shard_map/ppermute | solution.py:634
  638.3 1.4 copy.64
  (124 shorter events, 22.6 us)
Async XLA Ops:
  7.2 8.4 %copy-start = (bf16[1024,1024]{1,0:T(8,128)(2,1)S(1)}, bf16[1024,1024]{1,0:T(8,128)(2,1)}, u32[]{:S(2)}) copy-start(bf16[1024,1024]{1,0:T(8,128)(2,1)} %refs_2_.1) | copy-start | bytes 6291460
  7.2 8.9 %copy-start.14 = (f32[1024]{0:T(1024)S(1)}, f32[1024]{0:T(1024)}, u32[]{:S(2)}) copy-start(f32[1024]{0:T(1024)} %param.33) | copy-start | bytes 12292
  7.2 75.4 %all-gather.3.cloned.1.call-start = ((), (), s32[]{:S(2)}) async-start(), calls=%async_computation.1 | async-start | bytes 7241728 | tf_op jit(solution)/shard_map/all_gather | solution.py:708
  12.3 8.6 %copy-start.23 = (f32[8]{0:T(128)S(1)}, f32[8]{0:T(128)}, u32[]{:S(2)}) copy-start(f32[8]{0:T(128)} %param.36) | copy-start | bytes 100
  12.3 8.6 %copy-start.20 = (f32[8]{0:T(128)S(1)}, f32[8]{0:T(128)}, u32[]{:S(2)}) copy-start(f32[8]{0:T(128)} %param.37) | copy-start | bytes 100
  14.8 207.9 %all-gather.5.cloned.1.call-start = ((), (), s32[]{:S(2)}) async-start(), calls=%async_computation.2 | async-start | bytes 20545536 | tf_op jit(solution)/shard_map/all_gather | solution.py:709
  15.5 622.8 %reduce-scatter.4.cloned.1.call-start = ((), (), s32[]{:S(2)}) async-start(), calls=%async_computation.3 | async-start | bytes 20545536
  16.1 1.9 copy-start.16
  18.0 48.9 %collective-permute-start = (bf16[1024,1024]{1,0:T(8,128)(2,1)}, bf16[1024,1024]{1,0:T(8,128)(2,1)}, u32[]{:S(2)}, u32[]{:S(2)}) collective-permute-start(bf16[1024,1024]{1,0:T(8,128)(2,1)} %fusion.3), channel_id=1, source_target_pairs={{0,1},{1,0},{2,3},{3,2},{4,5},{5,4},{6,7},{7,6},{8,9},{9,8},{10,11... | collective-permute-start | bytes 6291464 | tf_op jit(solution)/shard_map/ppermute | solution.py:681
  82.6 14.2 %copy-start.22 = (bf16[2048,1664]{1,0:T(8,128)(2,1)S(1)}, bf16[2048,1664]{1,0:T(8,128)(2,1)}, u32[]{:S(2)}) copy-start(bf16[2048,1664]{1,0:T(8,128)(2,1)} %all-gather.3.cloned.1.call-done) | copy-start | bytes 20447236
  109.9 88.8 %copy-start.24 = (s32[2]{0:T(128)S(1)}, s32[2]{0:T(128)}, u32[]{:S(2)}) copy-start(s32[2]{0:T(128)} %param.31) | copy-start | bytes 28
  109.9 112.8 %copy-start.9 = (f32[1024]{0:T(1024)S(1)}, f32[1024]{0:T(1024)}, u32[]{:S(2)}) copy-start(f32[1024]{0:T(1024)} %param.34) | copy-start | bytes 12292
  197.2 25.5 %collective-permute-start.1 = (bf16[2,1024,256]{2,1,0:T(8,128)(2,1)}, bf16[2,1024,256]{2,1,0:T(8,128)(2,1)S(1)}, u32[]{:S(2)}, u32[]{:S(2)}) collective-permute-start(bf16[2,1024,256]{2,1,0:T(8,128)(2,1)} %slice.72), channel_id=1, source_target_pairs={{0,1},{1,0},{2,3},{3,2},{4,5},{5,4},{6,7},{7,6},{8,9},{9,8},{10,11... | collective-permute-start | bytes 3145736 | tf_op jit(solution)/shard_map/ppermute | solution.py:681
  222.7 1.6 copy-start.2
  224.3 1.6 copy-start.6
  233.3 1.3 copy-start.7
  234.6 1.3 copy-start.10
  304.9 1.6 copy-start.8
  306.5 11.6 %copy-start.3 = (bf16[2,2048,256]{2,1,0:T(8,128)(2,1)S(1)}, bf16[2,2048,256]{2,1,0:T(8,128)(2,1)}, u32[]{:S(2)}) copy-start(bf16[2,2048,256]{2,1,0:T(8,128)(2,1)} %get-tuple-element.41.refs_0_.mixed_ref) | copy-start | bytes 6291460
  316.5 4.5 copy-start.4
  316.5 24.5 %collective-permute-start.2 = (bf16[2,1024,256]{2,1,0:T(8,128)(2,1)S(1)}, bf16[2,1024,256]{2,1,0:T(8,128)(2,1)S(1)}, u32[]{:S(2)}, u32[]{:S(2)}) collective-permute-start(bf16[2,1024,256]{2,1,0:T(8,128)(2,1)S(1)} %get-tuple-element.55), channel_id=1, source_target_pairs={{0,1},{1,0},{2,3},{3,2},{4,5},{5,4},{6,7},{7,6},{8,9},{9,8},{10,11... | collective-permute-start | bytes 3145736 | tf_op jit(solution)/shard_map/ppermute | solution.py:681
  457.2 12.3 %copy-start.25 = (bf16[2048,1664]{1,0:T(8,128)(2,1)S(1)}, bf16[2048,1664]{1,0:T(8,128)(2,1)}, u32[]{:S(2)}) copy-start(bf16[2048,1664]{1,0:T(8,128)(2,1)} %get-tuple-element.59) | copy-start | bytes 20447236
  457.2 24.2 %slice-start = ((s8[6815744]{0:T(1024)(128)(4,1)}), s8[4194304]{0:T(1024)(128)(4,1)S(1)}, s32[]{:S(2)}) async-start(s8[6815744]{0:T(1024)(128)(4,1)} %bitcast.48), calls=%async_computation.4 | async-start | bytes 8388608
  469.4 11.9 %slice-start.1 = ((s8[6815744]{0:T(1024)(128)(4,1)}), s8[2621440]{0:T(1024)(128)(4,1)S(1)}, s32[]{:S(2)}) async-start(s8[6815744]{0:T(1024)(128)(4,1)} %bitcast.48), calls=%async_computation.5 | async-start | bytes 5242880
  469.5 44.2 %collective-permute-start.10 = (bf16[2,2,1,128,1664]{4,3,2,1,0:T(8,128)(2,1)S(1)}, bf16[2,2,1,128,1664]{4,3,2,1,0:T(8,128)(2,1)}, u32[]{:S(2)}, u32[]{:S(2)}) collective-permute-start(bf16[2,2,1,128,1664]{4,3,2,1,0:T(8,128)(2,1)S(1)} %constant_dynamic-slice_fusion.2), channel_id=1, source_target_pairs={{0,4},{4,0},{8,12},{12,8},{16,20},{20,16},{24,28},{28,24},{1,5},{5... | collective-permute-start | bytes 5111816 | tf_op jit(solution)/shard_map/ppermute | solution.py:634
  481.1 32.5 %collective-permute-start.9 = (bf16[2,2,1,128,1664]{4,3,2,1,0:T(8,128)(2,1)}, bf16[2,2,1,128,1664]{4,3,2,1,0:T(8,128)(2,1)}, u32[]{:S(2)}, u32[]{:S(2)}) collective-permute-start(bf16[2,2,1,128,1664]{4,3,2,1,0:T(8,128)(2,1)} %constant_dynamic-slice_fusion.3), channel_id=1, source_target_pairs={{0,4},{4,0},{8,12},{12,8},{16,20},{20,16},{24,28},{28,24},{1,5},{5... | collective-permute-start | bytes 5111816 | tf_op jit(solution)/shard_map/ppermute | solution.py:634
  510.2 7.9 %copy-start.11 = (f32[2048,1024]{1,0:T(8,128)}, f32[2048,1024]{1,0:T(8,128)S(1)}, u32[]{:S(2)}) copy-start(f32[2048,1024]{1,0:T(8,128)S(1)} %get-tuple-element.133) | copy-start | bytes 25165828
  512.0 7.7 %copy-start.21 = (f32[8,128]{1,0:T(8,128)S(1)}, f32[8,128]{1,0:T(8,128)}, u32[]{:S(2)}) copy-start(f32[8,128]{1,0:T(8,128)} %get-tuple-element.62) | copy-start | bytes 12292
  512.0 7.7 %copy-start.19 = (s32[2]{0:T(128)S(1)}, s32[2]{0:T(128)}, u32[]{:S(2)}) copy-start(s32[2]{0:T(128)} %constant.152) | copy-start | bytes 28
  512.1 8.4 %copy-start.18 = (s32[2]{0:T(128)S(1)}, s32[2]{0:T(128)}, u32[]{:S(2)}) copy-start(s32[2]{0:T(128)} %constant.160) | copy-start | bytes 28
  512.1 87.7 %collective-permute-start.3 = (bf16[1024,1024]{1,0:T(8,128)(2,1)}, bf16[1024,1024]{1,0:T(8,128)(2,1)}, u32[]{:S(2)}, u32[]{:S(2)}) collective-permute-start(bf16[1024,1024]{1,0:T(8,128)(2,1)} %slice.137), channel_id=1, source_target_pairs={{0,1},{1,0},{2,3},{3,2},{4,5},{5,4},{6,7},{7,6},{8,9},{9,8},{10,11... | collective-permute-start | bytes 6291464 | tf_op jit(solution)/shard_map/ppermute | solution.py:681
  518.0 4.3 copy-start.15
  518.0 81.8 %copy-start.1 = (bf16[1024,1024]{1,0:T(8,128)(2,1)S(1)}, bf16[1024,1024]{1,0:T(8,128)(2,1)}, u32[]{:S(2)}) copy-start(bf16[1024,1024]{1,0:T(8,128)(2,1)} %refs_2_.1) | copy-start | bytes 6291460
  518.0 81.8 %copy-start.17 = (f32[1024]{0:T(1024)S(1)}, f32[1024]{0:T(1024)}, u32[]{:S(2)}) copy-start(f32[1024]{0:T(1024)} %copy-done.16) | copy-start | bytes 12292
  519.2 77.7 %collective-permute-start.12 = (bf16[2,1,1,128,1664]{4,3,2,1,0:T(8,128)(2,1)}, bf16[2,1,1,128,1664]{4,3,2,1,0:T(8,128)(2,1)}, u32[]{:S(2)}, u32[]{:S(2)}) collective-permute-start(bf16[2,1,1,128,1664]{4,3,2,1,0:T(8,128)(2,1)} %get-tuple-element.115), channel_id=1, source_target_pairs={{0,2},{2,0},{1,3},{3,1},{4,6},{6,4},{5,7},{7,5},{8,10},{10,8},{9,1... | collective-permute-start | bytes 2555912 | tf_op jit(solution)/shard_map/ppermute | solution.py:634
  523.3 58.8 %collective-permute-start.4 = (f32[2192]{0:T(1024)S(1)}, f32[2192]{0:T(1024)S(1)}, u32[]{:S(2)}, u32[]{:S(2)}) collective-permute-start(f32[2192]{0:T(1024)S(1)} %concatenate.27), channel_id=1, source_target_pairs={{0,1},{1,0},{2,3},{3,2},{4,5},{5,4},{6,7},{7,6},{8,9},{9,8},{10,11... | collective-permute-start | bytes 26312 | tf_op jit(solution)/shard_map/ppermute | solution.py:634
  582.1 3.7 collective-permute-start.5
  585.8 1.2 collective-permute-start.6
  587.0 3.7 collective-permute-start.7
  590.7 4.6 collective-permute-start.8
  595.9 18.7 %collective-permute-start.11 = (bf16[2,1,1,128,1664]{4,3,2,1,0:T(8,128)(2,1)S(1)}, bf16[2,1,1,128,1664]{4,3,2,1,0:T(8,128)(2,1)S(1)}, u32[]{:S(2)}, u32[]{:S(2)}) collective-permute-start(bf16[2,1,1,128,1664]{4,3,2,1,0:T(8,128)(2,1)S(1)} %get-tuple-element.114), channel_id=1, source_target_pairs={{0,2},{2,0},{1,3},{3,1},{4,6},{6,4},{5,7},{7,5},{8,10},{10,8},{9,1... | collective-permute-start | bytes 2555912 | tf_op jit(solution)/shard_map/ppermute | solution.py:634
  596.9 20.2 %copy-start.13 = (bf16[2,2,1,128,1664]{4,3,2,1,0:T(8,128)(2,1)S(1)}, bf16[2,2,1,128,1664]{4,3,2,1,0:T(8,128)(2,1)}, u32[]{:S(2)}) copy-start(bf16[2,2,1,128,1664]{4,3,2,1,0:T(8,128)(2,1)} %get-tuple-element.112) | copy-start | bytes 5111812
  598.6 18.5 %collective-permute-start.13 = (bf16[2,1,1,128,1664]{4,3,2,1,0:T(8,128)(2,1)S(1)}, bf16[2,1,1,128,1664]{4,3,2,1,0:T(8,128)(2,1)S(1)}, u32[]{:S(2)}, u32[]{:S(2)}) collective-permute-start(bf16[2,1,1,128,1664]{4,3,2,1,0:T(8,128)(2,1)S(1)} %add_convert_fusion.3), channel_id=1, source_target_pairs={{0,8},{4,12},{8,0},{12,4},{16,24},{20,28},{24,16},{28,20},{1,9},{5... | collective-permute-start | bytes 2555912 | tf_op jit(solution)/shard_map/ppermute | solution.py:634
  599.8 18.0 %copy-start.12 = (f32[2048,1024]{1,0:T(8,128)S(1)}, f32[2048,1024]{1,0:T(8,128)}, u32[]{:S(2)}) copy-start(f32[2048,1024]{1,0:T(8,128)} %copy-done.11) | copy-start | bytes 25165828
  603.9 13.9 %copy-start.5 = (f32[1024,1024]{1,0:T(8,128)S(1)}, f32[1024,1024]{1,0:T(8,128)}, u32[]{:S(2)}) copy-start(f32[1024,1024]{1,0:T(8,128)} %copy-done.4) | copy-start | bytes 12582916
  617.5 18.5 %collective-permute-start.14 = (bf16[1,1,1,128,1664]{4,3,2,1,0:T(8,128)(2,1)S(1)}, bf16[1,1,1,128,1664]{4,3,2,1,0:T(8,128)(2,1)S(1)}, u32[]{:S(2)}, u32[]{:S(2)}) collective-permute-start(bf16[1,1,1,128,1664]{4,3,2,1,0:T(8,128)(2,1)S(1)} %constant_dynamic-slice_fusion.4), channel_id=1, source_target_pairs={{0,16},{4,20},{8,24},{12,28},{16,0},{20,4},{24,8},{28,12},{1,17},{... | collective-permute-start | bytes 1277960 | tf_op jit(solution)/shard_map/ppermute | solution.py:634
Sparse Core Ops, SparseCore 0:
  14.9 67.6 all-gather.2
  85.5 128.0 all-gather.4
  342.7 217.9 reduce-scatter.3

commit v3 on v2

v3 whole, which is shorter than its diff:
```python
import functools
import jax
import jax.numpy as jnp
import numpy as np
from jax import lax
from jax.experimental import pallas as pl
from jax.experimental.pallas import tpu as pltpu
from jax.sharding import Mesh
from jax.sharding import PartitionSpec as P

HEAD = 128
NH = 2
CT = 64
ROWS = CT * NH
EPS = 1e-06
HIGH = lax.Precision.HIGHEST
BF = jnp.bfloat16
F32 = jnp.float32


def dot_nn(left, right):
    return jnp.dot(left, right, preferred_element_type=F32)


def dot_nt(left, right):
    return lax.dot_general(left, right, (((1,), (1,)), ((), ())), preferred_element_type=F32)


def dot_tn(left, right):
    return lax.dot_general(left, right, (((0,), (0,)), ((), ())), preferred_element_type=F32)


def mixer_tables():
    row = np.arange(ROWS)
    tok, step = row % CT, row // CT
    order = tok * NH + step
    later = order[:, None] > order[None, :]
    barred = np.where(later, 0.0, -1e30).astype(np.float32)
    levels = []
    for size in (1, 4, 16):
        near = (tok[:, None] // (4 * size)) == (tok[None, :] // (4 * size))
        apart = (tok[:, None] // size) != (tok[None, :] // size)
        levels.append((near & apart).astype(np.float32))
    own = ((tok[:, None] == tok[None, :]) & later).astype(np.float32)
    eye = np.eye(ROWS, dtype=np.float32)
    read = np.zeros((CT, ROWS), np.float32)
    read[np.arange(CT), CT + np.arange(CT)] = 1.0
    sums = (np.arange(CT)[:, None] <= tok[None, :]).astype(np.float32)
    square = np.stack([barred, eye, own] + levels)
    thin = np.stack([read, sums])
    return square, thin, np.concatenate([sums] * 3, axis=0)


def sigm(values):
    return jax.nn.sigmoid(values)


class Layout:
    def __init__(self, heads):
        self.q = 0
        self.k = heads * HEAD
        self.v = self.k + heads * NH * HEAD
        self.g = self.v + heads * NH * HEAD
        self.r = self.g + heads * HEAD
        self.width = self.r + 128


def piece(refs, s, c, start):
    return refs[s][c * CT : (c + 1) * CT, start : start + HEAD]


def unit_silu(raw):
    sig = sigm(raw)
    act = raw * sig
    norm = lax.rsqrt(jnp.sum(act * act, axis=-1, keepdims=True) + EPS)
    return act * norm, norm, sig


def thirds(values):
    high = values.astype(BF)
    rest = values - high.astype(F32)
    middle = rest.astype(BF)
    return high, middle, (rest - middle.astype(F32)).astype(BF)


def rates_of(pre_ref, par_ref, sums_ref, nb, nsq, lay):
    raw = None
    for c in range(nb):
        for s in range(nsq):
            here = pre_ref[s][c * CT : (c + 1) * CT, lay.r : lay.r + 128]
            if c + s > 0:
                here = pltpu.roll(here, 8 * (c * nsq + s), axis=1)
            raw = here if raw is None else raw + here
    shifted = raw + par_ref[1:2, :]
    soft = jnp.maximum(shifted, 0.0) + jnp.log1p(jnp.exp(-jnp.abs(shifted)))
    decay = par_ref[0:1, :] * soft
    stacked = jnp.concatenate(thirds(decay), axis=0)
    sums = sums_ref[...]
    return sigm(raw), shifted, decay, dot_tn(sums, stacked), dot_tn(stacked, sums)


def chunk_parts(pre_ref, s, h, c, nsq, lay, betas, cum_col, cum_row, square_ref):
    query, nq, sq = unit_silu(piece(pre_ref, s, c, lay.q + h * HEAD))
    key0, nk0, sk0 = unit_silu(piece(pre_ref, s, c, lay.k + (2 * h) * HEAD))
    key1, nk1, sk1 = unit_silu(piece(pre_ref, s, c, lay.k + (2 * h + 1) * HEAD))
    keys = jnp.concatenate([key0, key1], axis=0)
    base = 8 * (c * nsq + s) + 3 * h
    wide = lambda column: jnp.broadcast_to(column, (CT, HEAD))
    beta = jnp.concatenate([wide(betas[:, base : base + 1]), wide(betas[:, base + 1 : base + 2])], axis=0)
    scaled = keys * beta
    g = wide(cum_col[:CT, base + 2 : base + 3])
    grow = cum_row[base + 2 : base + 3, :]
    weights = jnp.exp(jnp.concatenate([g, g], axis=0) - grow + square_ref[0])
    tail = g[CT - 1 : CT, :]
    grown, left = jnp.exp(g), jnp.exp(tail - g)
    return dict(
        query=query, keys=keys, beta=beta, scaled=scaled, weights=weights, grown=jnp.concatenate([grown, grown], axis=0),
        left=jnp.concatenate([left, left], axis=0), tail=jnp.exp(tail), nq=nq, sq=sq, nk=(nk0, nk1), sk=(sk0, sk1),
    )


def forward_kernel(lay, nsq, heads, nb, _, *refs):
    pre_ref = refs[:nsq]
    par_ref, gain_ref, square_ref, thin_ref, sums_ref = refs[nsq : nsq + 5]
    mixed_ref, tinv_ref, wk_ref, state_ref, delta_ref, o_ref, carry = refs[nsq + 5 :]

    @pl.when(pl.program_id(0) == 0)
    def _():
        carry[...] = jnp.zeros_like(carry)

    which = [(c, s, h) for c in range(nb) for s in range(nsq) for h in range(heads)]
    betas, _, _, cum_col, cum_row = rates_of(pre_ref, par_ref, sums_ref, nb, nsq, lay)
    parts = {}
    for c, s, h in which:
        parts[c, s, h] = chunk_parts(pre_ref, s, h, c, nsq, lay, betas, cum_col, cum_row, square_ref)
    lam, scores = {}, {}
    for key in which:
        p = parts[key]
        keys_low, scaled_low, query_low = p["keys"].astype(BF), p["scaled"].astype(BF), p["query"].astype(BF)
        both = dot_nt(jnp.concatenate([keys_low, query_low], axis=0), scaled_low)
        lam[key] = both[:ROWS] * p["weights"]
        scores[key] = (both[ROWS:] * (p["weights"][CT:] + thin_ref[0])).astype(BF)
    tinv = {key: square_ref[1] - lam[key] * square_ref[2] for key in which}
    for level in range(3):
        low = {key: tinv[key].astype(BF) for key in which}
        step = {key: dot_nn(low[key], (lam[key] * square_ref[3 + level]).astype(BF)).astype(BF) for key in which}
        twice = {key: dot_nn(step[key], step[key]).astype(BF) for key in which}
        half = {key: tinv[key] - dot_nn(step[key], low[key]) for key in which}
        tinv = {key: half[key] + dot_nn(twice[key], half[key].astype(BF)) for key in which}
    chains = [(s, h) for s in range(nsq) for h in range(heads)]
    mixed_in = {}
    for key in which:
        c, s, h = key
        p = parts[key]
        t_low = tinv[key].astype(BF)
        tinv_ref[c, s * heads + h] = t_low
        raw0 = piece(pre_ref, s, c, lay.v + (2 * h) * HEAD)
        raw1 = piece(pre_ref, s, c, lay.v + (2 * h + 1) * HEAD)
        values = jnp.concatenate([raw0 * sigm(raw0), raw1 * sigm(raw1)], axis=0)
        kg = p["keys"] * p["grown"]
        solved = dot_nn(t_low, jnp.concatenate([values, kg], axis=1).astype(BF))
        wk = solved[:, HEAD:].astype(BF)
        wk_ref[c, s * heads + h] = wk
        qg = (p["query"] * p["grown"][:CT]).astype(BF)
        mixed_in[key] = (solved[:, :HEAD], jnp.concatenate([wk, qg], axis=0), (p["scaled"] * p["left"]).astype(BF))
    state = {k: carry[k[0] * heads + k[1]] for k in chains}
    read, deltas = {}, {}
    for c in range(nb):
        low = {k: state[k].astype(BF) for k in chains}
        for s, h in chains:
            state_ref[c, s * heads + h] = low[s, h]
        seen = {k: dot_nn(mixed_in[(c,) + k][1], low[k]) for k in chains}
        delta = {k: (mixed_in[(c,) + k][0] - seen[k][:ROWS]).astype(BF) for k in chains}
        state = {k: parts[(c,) + k]["tail"] * state[k] + dot_tn(mixed_in[(c,) + k][2], delta[k]) for k in chains}
        for k in chains:
            read[(c,) + k] = seen[k][ROWS:]
            deltas[(c,) + k] = delta[k]
    for s, h in chains:
        carry[s * heads + h] = state[s, h]
    for key in which:
        c, s, h = key
        delta_ref[c, s * heads + h] = deltas[key]
        out = read[key] + dot_nn(scores[key], deltas[key])
        o_ref[s, c * CT : (c + 1) * CT, h * HEAD : (h + 1) * HEAD] = out
        scale = lax.rsqrt(jnp.mean(out * out, axis=-1, keepdims=True) + EPS)
        gate = piece(pre_ref, s, c, lay.g + h * HEAD)
        mixed = out * scale * gain_ref[0:1, :] * (gate * sigm(gate))
        mixed_ref[s, c * CT : (c + 1) * CT, h * HEAD : (h + 1) * HEAD] = mixed.astype(BF)


def silu_slope(raw, sig):
    return sig * (1.0 + raw * (1.0 - sig))


def backward_kernel(lay, nsq, heads, nb, _, *refs):
    pre_ref = refs[:nsq]
    par_ref, gain_ref, square_ref, thin_ref, sums_ref = refs[nsq : nsq + 5]
    tinv_ref, wk_ref, state_ref, delta_ref, o_ref, dm_ref = refs[nsq + 5 : nsq + 11]
    carry_in, small_in = refs[nsq + 11 : nsq + 13]
    dpre_ref = refs[-nsq - 3 : -3]
    carry, acc, carried = refs[-3:]

    @pl.when(pl.program_id(0) == 0)
    def _():
        carried[...] = carry_in[...]
        acc[...] = small_in[...]

    lane = lax.broadcasted_iota(jnp.int32, (CT, 128), 1)
    sub8 = lax.broadcasted_iota(jnp.int32, (8, 128), 0)
    chains = [(s, h) for s in range(nsq) for h in range(heads)]
    spans = [slice(c * CT, (c + 1) * CT) for c in range(nb)]
    gain = gain_ref[0:1, :]
    gain_sum = jnp.zeros((1, HEAD), F32)
    work = {}
    betas, shifted, decay, cum_col, cum_row = rates_of(pre_ref, par_ref, sums_ref, nb, nsq, lay)
    for c in reversed(range(nb)):
        for s, h in chains:
            cols = slice(h * HEAD, (h + 1) * HEAD)
            p = chunk_parts(pre_ref, s, h, c, nsq, lay, betas, cum_col, cum_row, square_ref)
            out = o_ref[s, spans[c], cols]
            dm = dm_ref[s, spans[c], cols].astype(F32)
            graw = piece(pre_ref, s, c, lay.g + h * HEAD)
            gsig = sigm(graw)
            gate = graw * gsig
            scale = lax.rsqrt(jnp.mean(out * out, axis=-1, keepdims=True) + EPS)
            normed = out * scale
            dpre_ref[s][spans[c], lay.g + h * HEAD : lay.g + (h + 1) * HEAD] = (
                dm * normed * gain * (gsig + gate * (1.0 - gsig))
            ).astype(BF)
            dn = dm * gate
            gain_sum = gain_sum + jnp.sum(dn * normed, axis=0, keepdims=True)
            scaled_dn = dn * gain
            dout = scale * (scaled_dn - normed * jnp.mean(scaled_dn * normed, axis=-1, keepdims=True))
            dout_low = dout.astype(BF)
            keys_low, query_low = p["keys"].astype(BF), p["query"].astype(BF)
            scaled_low = p["scaled"].astype(BF)
            both_low = jnp.concatenate([keys_low, query_low], axis=0)
            w_all = jnp.concatenate([p["weights"], p["weights"][CT:] + thin_ref[0]], axis=0)
            weighted = dot_nt(both_low, scaled_low) * w_all
            p["w_all"], p["weighted"], p["both_low"], p["scaled_low"] = w_all, weighted, both_low, scaled_low
            p["dout_low"] = dout_low
            p["from_out"] = dot_tn(weighted[ROWS:].astype(BF), dout_low)
            qg = (p["query"] * p["grown"][:CT]).astype(BF)
            p["to_state"] = dot_tn(qg, dout_low)
            p["kout"] = (p["scaled"] * p["left"]).astype(BF)
            work[c, s, h] = p
    dstate = {k: carried[k[0] * heads + k[1]] for k in chains}
    for c in reversed(range(nb)):
        low = {k: dstate[k].astype(BF) for k in chains}
        ddelta = {
            k: (work[(c,) + k]["from_out"] + dot_nn(work[(c,) + k]["kout"], low[k])).astype(BF) for k in chains
        }
        for k in chains:
            p = work[(c,) + k]
            p["ddelta"], p["dstate"], p["dstate_low"] = ddelta[k], dstate[k], low[k]
        dstate = {
            k: work[(c,) + k]["tail"] * dstate[k]
            + work[(c,) + k]["to_state"]
            - dot_tn(wk_ref[c, k[0] * heads + k[1]], ddelta[k])
            for k in chains
        }
    for s, h in chains:
        carried[s * heads + h] = dstate[s, h]
        carry[s * heads + h] = dstate[s, h]
    read_all = jnp.zeros((CT, 128), F32)
    dtail_all = jnp.zeros((1, 128), F32)
    dbeta_all = jnp.zeros((CT, 128), F32)
    col_rows = {}
    for c in reversed(range(nb)):
        span = spans[c]
        for s in range(nsq):
            dcol_all = jnp.zeros((8, 128), F32)
            for h in range(heads):
                at = s * heads + h
                p = work[c, s, h]
                dpv = dot_tn(tinv_ref[c, at], p["ddelta"])
                joint = jnp.concatenate([(-dpv).astype(BF), p["dout_low"]], axis=0)
                delta = delta_ref[c, at]
                state_low = state_ref[c, at]
                inner = dot_nt(joint, delta)
                inner_low = (inner * p["w_all"]).astype(BF)
                pairs = inner * p["weighted"]
                grown_all = jnp.concatenate([p["grown"], p["grown"][:CT]], axis=0)
                base = 8 * (c * nsq + s) + 3 * h
                entered = grown_all * dot_nt(joint, state_low)
                left_out = p["left"] * dot_nt(delta, p["dstate_low"])
                direct = dot_nn(inner_low, p["scaled_low"]) + entered
                dscaled = dot_tn(inner_low, p["both_low"]) + left_out
                both_rows = jnp.concatenate([p["keys"], p["query"]], axis=0)
                row_part = jnp.sum(pairs + both_rows * entered, axis=-1, keepdims=True)
                col_part = jnp.sum(pairs, axis=0, keepdims=True)
                out_part = jnp.sum(p["scaled"] * left_out, axis=-1, keepdims=True)
                dtail = p["tail"] * jnp.sum(
                    jnp.sum(state_low.astype(F32) * p["dstate"], axis=0, keepdims=True), axis=1, keepdims=True
                ) + jnp.sum(out_part, axis=0, keepdims=True)
                dkeys, dquery = direct[:ROWS], direct[ROWS:]
                dbeta = jnp.sum(p["keys"] * dscaled, axis=-1, keepdims=True)
                kdot = jnp.sum(p["keys"] * dkeys, axis=-1, keepdims=True)
                qdot = jnp.sum(p["query"] * dquery, axis=-1, keepdims=True)
                kfull = kdot + p["beta"] * dbeta
                tokens = row_part[:CT] + row_part[CT:ROWS] + row_part[ROWS:] - out_part[:CT] - out_part[CT:]
                read_all = jnp.where(lane == base + 2, tokens, read_all)
                dcol_all = jnp.where(sub8 == 3 * h + 2, col_part, dcol_all)
                dtail_all = jnp.where(lane[0:1] == base + 2, dtail, dtail_all)
                dbeta_all = jnp.where(lane == base, dbeta[:CT], dbeta_all)
                dbeta_all = jnp.where(lane == base + 1, dbeta[CT:], dbeta_all)
                dk = dkeys + p["beta"] * dscaled
                dk = dk - p["keys"] * kfull
                for j in range(NH):
                    part = slice(j * CT, (j + 1) * CT)
                    start = lay.k + (2 * h + j) * HEAD
                    kraw = piece(pre_ref, s, c, start)
                    dpre_ref[s][span, start : start + HEAD] = (
                        dk[part] * p["nk"][j] * silu_slope(kraw, p["sk"][j])
                    ).astype(BF)
                    start = lay.v + (2 * h + j) * HEAD
                    vraw = piece(pre_ref, s, c, start)
                    dpre_ref[s][span, start : start + HEAD] = (
                        dpv[part] * silu_slope(vraw, sigm(vraw))
                    ).astype(BF)
                start = lay.q + h * HEAD
                qraw = piece(pre_ref, s, c, start)
                dq = (dquery - p["query"] * qdot) * p["nq"]
                dpre_ref[s][span, start : start + HEAD] = (dq * silu_slope(qraw, p["sq"])).astype(BF)
            col_rows[c * nsq + s] = dcol_all
    sums = sums_ref[0:CT, :]
    reads = jnp.concatenate(thirds(read_all), axis=0)
    padding = [jnp.zeros((128 - 8 * len(col_rows), 128), F32)] if len(col_rows) < 16 else []
    columns = jnp.concatenate([col_rows[k] for k in range(len(col_rows))] + padding, axis=0)
    ddecay = dot_nn(jnp.concatenate([sums[:, :CT]] * 3, axis=1), reads) + dtail_all
    for term in thirds(columns):
        ddecay = ddecay - dot_nt(sums, term)
    dshift = ddecay * par_ref[0:1, :] * sigm(shifted)
    acc[1:2, :] += jnp.sum(dshift, axis=0, keepdims=True)
    acc[2:3, :] += jnp.sum(ddecay * decay, axis=0, keepdims=True)
    drates = dshift + dbeta_all * betas * (1.0 - betas)
    for c in range(nb):
        for s in range(nsq):
            shift = 8 * (c * nsq + s)
            here = pltpu.roll(drates, 128 - shift, axis=1) if shift else drates
            dpre_ref[s][spans[c], lay.r : lay.r + 128] = jnp.where(lane < 8, here, 0.0).astype(BF)
    acc[0:1, :] += gain_sum


def shared_specs(square, thin, sums):
    return [
        pl.BlockSpec((2, 128), lambda i, _: (0, 0)),
        pl.BlockSpec((1, HEAD), lambda i, _: (0, 0)),
        pl.BlockSpec(square.shape, lambda i, _: (0, 0, 0)),
        pl.BlockSpec(thin.shape, lambda i, _: (0, 0, 0)),
        pl.BlockSpec(sums.shape, lambda i, _: (0, 0)),
    ]


def part_chunk(step, place, per_part):
    return ((step // per_part) ^ place[0]) * per_part + step % per_part


def mixer_forward(place, parts, pre, params, gain, heads, nb=2):
    nsq, (length, width) = len(pre), pre[0].shape
    lay = Layout(heads)
    square, thin, sums3 = mixer_tables()
    nchunk = length // CT
    chains = nsq * heads
    span = nb * CT
    per_part = nchunk // nb // parts
    big = lambda: pl.BlockSpec((nb, chains, ROWS, HEAD), lambda i, _: (i, 0, 0, 0))
    rows = lambda w: pl.BlockSpec((nsq, span, w), lambda i, place: (0, part_chunk(i, place, per_part), 0))
    wide = lambda: pl.BlockSpec((span, width), lambda i, place: (part_chunk(i, place, per_part), 0))
    return pl.pallas_call(
        functools.partial(forward_kernel, lay, nsq, heads, nb),
        grid_spec=pltpu.PrefetchScalarGridSpec(
            num_scalar_prefetch=1,
            grid=(nchunk // nb,),
            in_specs=[wide() for _ in pre] + shared_specs(square, thin, sums3),
            out_specs=[rows(heads * HEAD), big(), big(), big(), big(), rows(heads * HEAD)],
            scratch_shapes=[pltpu.VMEM((chains, HEAD, HEAD), F32)],
        ),
        out_shape=[
            jax.ShapeDtypeStruct((nsq, length, heads * HEAD), BF),
            jax.ShapeDtypeStruct((nchunk, chains, ROWS, ROWS), BF),
            jax.ShapeDtypeStruct((nchunk, chains, ROWS, HEAD), BF),
            jax.ShapeDtypeStruct((nchunk, chains, HEAD, HEAD), BF),
            jax.ShapeDtypeStruct((nchunk, chains, ROWS, HEAD), BF),
            jax.ShapeDtypeStruct((nsq, length, heads * HEAD), F32),
        ],
        compiler_params=pltpu.CompilerParams(vmem_limit_bytes=56 * 1024 * 1024),
        cost_estimate=pl.CostEstimate(
            flops=nchunk * chains * 20 * 2 * ROWS**3,
            bytes_accessed=nsq * length * (4 * width + 6 * heads * HEAD) + nchunk * chains * 6 * ROWS**2,
            transcendentals=0,
        ),
        name="mixer_forward",
    )(place, *pre, params, gain, jnp.asarray(square), jnp.asarray(thin), jnp.asarray(sums3, BF))


def mixer_backward(place, parts, pre, params, gain, tinv, wks, states, deltas, outs, dmixed, heads, nb, at, earlier):
    nsq, (length, width) = len(pre), pre[0].shape
    lay = Layout(heads)
    square, thin, sums3 = mixer_tables()
    nchunk = length // CT
    chains = nsq * heads
    span = nb * CT
    per_part = nchunk // nb // parts
    last = nchunk // nb - 1 - at * per_part
    big = lambda: pl.BlockSpec((nb, chains, ROWS, HEAD), lambda i, _: (last - i, 0, 0, 0))
    rows = lambda w: pl.BlockSpec(
        (nsq, span, w), lambda i, place: (0, part_chunk(last - i, place, per_part), 0)
    )
    wide = lambda: pl.BlockSpec((span, width), lambda i, place: (part_chunk(last - i, place, per_part), 0))
    held = pl.BlockSpec((chains, HEAD, HEAD), lambda i, _: (0, 0, 0))
    sums = pl.BlockSpec((8, 128), lambda i, _: (0, 0))
    carry, small, *done = earlier
    first_done = nsq + 14
    return pl.pallas_call(
        functools.partial(backward_kernel, lay, nsq, heads, nb),
        grid_spec=pltpu.PrefetchScalarGridSpec(
            num_scalar_prefetch=1,
            grid=(per_part,),
            in_specs=[wide() for _ in pre]
            + shared_specs(square, thin, sums3)
            + [big(), big(), big(), big(), rows(heads * HEAD), rows(heads * HEAD), held, sums]
            + [pl.BlockSpec(memory_space=pl.ANY) for _ in done],
            out_specs=[wide() for _ in pre] + [held, sums],
            scratch_shapes=[pltpu.VMEM((chains, HEAD, HEAD), F32)],
        ),
        out_shape=[jax.ShapeDtypeStruct((length, width), BF) for _ in pre]
        + [jax.ShapeDtypeStruct((chains, HEAD, HEAD), F32), jax.ShapeDtypeStruct((8, 128), F32)],
        input_output_aliases={first_done + k: k for k in range(len(done))},
        compiler_params=pltpu.CompilerParams(vmem_limit_bytes=56 * 1024 * 1024),
        cost_estimate=pl.CostEstimate(
            flops=nchunk // parts * chains * 26 * 2 * ROWS**3,
            bytes_accessed=(nsq * length * (6 * width + 6 * heads * HEAD) + nchunk * chains * 8 * ROWS**2) // parts,
            transcendentals=0,
        ),
        name="mixer_backward",
    )(
        place, *pre, params, gain, jnp.asarray(square), jnp.asarray(thin), jnp.asarray(sums3, BF),
        tinv, wks, states, deltas, outs, dmixed, carry, small, *done,
    )


TILE = 256


def token_mask(place, limit, tile, rows, base):
    position = place * rows + base + lax.broadcasted_iota(jnp.int32, (tile, 1), 0)
    return position < limit


def join_kernel(parts, nsq, tok, scalars, *refs):
    mixed_refs = refs[:parts]
    x_ref, og_ref, wout_ref, gain_ref = refs[parts : parts + 4]
    middle_ref, second_ref, grad_ref = refs[parts + 4 :]
    place, limit = scalars[0], scalars[1]
    total = x_ref[...].astype(F32)
    for r in range(parts):
        for s in range(nsq):
            total = total + dot_nt(mixed_refs[r][s], wout_ref[s * parts + (place ^ r)])
    middle_ref[...] = total
    scale = lax.rsqrt(jnp.mean(total * total, axis=-1, keepdims=True) + EPS)
    second_ref[...] = (total * scale * gain_ref[...]).astype(BF)
    keep = token_mask(place, limit, x_ref.shape[0], tok, pl.program_id(0) * x_ref.shape[0])
    grad_ref[...] = jnp.where(keep, og_ref[...].astype(F32), 0.0).astype(BF)


def join(scalars, mixed_parts, x, out_grad, wall, gain, parts, nsq, hw):
    tok, model = x.shape
    count = parts * nsq
    tile = min(TILE, tok)
    row = pl.BlockSpec((tile, model), lambda i, _: (i, 0))
    return pl.pallas_call(
        functools.partial(join_kernel, parts, nsq, tok),
        grid_spec=pltpu.PrefetchScalarGridSpec(
            num_scalar_prefetch=1,
            grid=(tok // tile,),
            in_specs=[pl.BlockSpec((nsq, tile, hw), lambda i, _: (0, i, 0)) for _ in mixed_parts]
            + [row, row, pl.BlockSpec((count, model, hw), lambda i, _: (0, 0, 0)),
               pl.BlockSpec((1, model), lambda i, _: (0, 0))],
            out_specs=[row, row, row],
        ),
        out_shape=[
            jax.ShapeDtypeStruct((tok, model), F32),
            jax.ShapeDtypeStruct((tok, model), BF),
            jax.ShapeDtypeStruct((tok, model), BF),
        ],
        compiler_params=pltpu.CompilerParams(vmem_limit_bytes=40 * 1024 * 1024),
        cost_estimate=pl.CostEstimate(
            flops=2 * tok * model * count * hw, bytes_accessed=14 * tok * model, transcendentals=0
        ),
        name="join",
    )(scalars, *mixed_parts, x, out_grad, wall, gain)


def core_halves(core, block, value):
    count = value.shape[0] // block
    pieces = [value[j * block : (j + 1) * block] for j in range(count)]
    join_all = lambda items: items[0] if len(items) == 1 else jnp.concatenate(items, axis=0)
    even, odd = join_all(pieces[0::2]), join_all(pieces[1::2])
    return jnp.where(core == 0, even, odd), jnp.where(core == 0, odd, even)


def ff_kernel(
    tile, block, lead, lead_out, units, scalars, sec_ref, grad_ref, w_ref, mlp_ref, sg_ref, keep_ref, send_ref, hid, both
):
    tok, model = sec_ref.shape
    mid, end = lead + 2 * units, lead + 3 * units
    mid_out, end_out = lead_out + 2 * units, lead_out + 3 * units

    @pl.when(pl.program_id(0) == 0)
    def _():
        mlp_ref[...] = jnp.zeros_like(mlp_ref)
        sg_ref[...] = jnp.zeros_like(sg_ref)

    for m in range(tok // tile):
        rows = slice(m * tile, (m + 1) * tile)
        pre = dot_nn(sec_ref[rows, :], w_ref[0, :, lead:mid])
        gate_pre, up_pre = pre[:, :units], pre[:, units:]
        hidden_grad = dot_nn(grad_ref[rows, :], w_ref[0, :, mid:end])
        sig = sigm(gate_pre)
        act = gate_pre * sig
        hidden = (act * up_pre).astype(BF)
        hid[rows, :] = hidden
        gate_low = (hidden_grad * up_pre * (sig + act * (1.0 - sig))).astype(BF)
        up_low = (hidden_grad * act).astype(BF)
        both_low = jnp.concatenate([gate_low, up_low], axis=1)
        both[rows, :] = both_low
        mlp_ref[rows, :] += dot_nt(hidden, w_ref[0, :, mid:end])
        sg_ref[rows, :] += dot_nt(both_low, w_ref[0, :, lead:mid])
    step = min(256, model)
    for k in range(model // step):
        cols = slice(k * step, (k + 1) * step)
        rows = slice(k * step // 2, (k + 1) * step // 2)
        value = core_halves(scalars[2], block, dot_tn(sec_ref[:, cols], both[...]))
        keep_ref[0, rows, lead_out:mid_out] = value[0].astype(BF)
        send_ref[0, rows, lead_out:mid_out] = value[1].astype(BF)
        value = core_halves(scalars[2], block, dot_tn(grad_ref[:, cols], hid[...]))
        keep_ref[0, rows, mid_out:end_out] = value[0].astype(BF)
        send_ref[0, rows, mid_out:end_out] = value[1].astype(BF)


def feed_forward(scalars, second, grad_low, wall, lead, lead_out, width_out, units, block):
    tok, model = second.shape
    count, _, width = wall.shape
    whole = pl.BlockSpec((tok, model), lambda p, _: (0, 0))
    weight = pl.BlockSpec((1, model, width), lambda p, _: (p, 0, 0))
    half = pl.BlockSpec((1, model // 2, width_out), lambda p, _: (p, 0, 0))
    return pl.pallas_call(
        functools.partial(ff_kernel, min(TILE, tok), block, lead, lead_out, units),
        grid_spec=pltpu.PrefetchScalarGridSpec(
            num_scalar_prefetch=1,
            grid=(count,),
            in_specs=[whole, whole, weight],
            out_specs=[whole, whole, half, half],
            scratch_shapes=[pltpu.VMEM((tok, units), BF), pltpu.VMEM((tok, 2 * units), BF)],
        ),
        out_shape=[
            jax.ShapeDtypeStruct((tok, model), F32),
            jax.ShapeDtypeStruct((tok, model), F32),
            jax.ShapeDtypeStruct((count, model // 2, width_out), BF),
            jax.ShapeDtypeStruct((count, model // 2, width_out), BF),
        ],
        compiler_params=pltpu.CompilerParams(vmem_limit_bytes=62 * 1024 * 1024),
        cost_estimate=pl.CostEstimate(
            flops=18 * tok * model * units * count,
            bytes_accessed=count * model * width * 4 + 12 * tok * model,
            transcendentals=0,
        ),
        name="feed_forward",
    )(scalars, second, grad_low, wall)


def split_kernel(parts, nsq, tok, scalars, *refs):
    middle_ref, mlp_ref, mlp2_ref, sg_ref, sg2_ref, grad_ref, wout_ref, gain_ref = refs[:8]
    out_ref, mg_ref, ml_ref, ln_ref = refs[8:12]
    back_refs = refs[12:]
    place, limit = scalars[0], scalars[1]
    tile = middle_ref.shape[0]
    middle = middle_ref[...]
    keep = token_mask(place, limit, tile, tok, pl.program_id(0) * tile)
    out_ref[...] = jnp.where(keep, middle + (mlp_ref[...] + mlp2_ref[...]), 0.0).astype(BF)
    scale = lax.rsqrt(jnp.mean(middle * middle, axis=-1, keepdims=True) + EPS)
    normed = middle * scale
    sg = sg_ref[...] + sg2_ref[...]

    @pl.when(pl.program_id(0) == 0)
    def _():
        ln_ref[...] = jnp.zeros_like(ln_ref)

    ln_ref[...] += jnp.sum(sg * normed, axis=0, keepdims=True)
    scaled = sg * gain_ref[...]
    back = scale * (scaled - normed * jnp.mean(scaled * normed, axis=-1, keepdims=True))
    total = grad_ref[...].astype(F32) + back
    mg_ref[...] = total
    low = total.astype(BF)
    ml_ref[...] = low
    for r in range(parts):
        for s in range(nsq):
            back_refs[r][s] = dot_nn(low, wout_ref[s * parts + (place ^ r)]).astype(BF)


def split(scalars, middle, mlps, second_grads, grad_low, wall, gain, parts, nsq, hw):
    tok, model = middle.shape
    count = parts * nsq
    tile = min(TILE, tok)
    row = pl.BlockSpec((tile, model), lambda i, _: (i, 0))
    line = pl.BlockSpec((1, model), lambda i, _: (0, 0))
    return pl.pallas_call(
        functools.partial(split_kernel, parts, nsq, tok),
        grid_spec=pltpu.PrefetchScalarGridSpec(
            num_scalar_prefetch=1,
            grid=(tok // tile,),
            in_specs=[row] * 6 + [pl.BlockSpec((count, model, hw), lambda i, _: (0, 0, 0)), line],
            out_specs=[row, row, row, line]
            + [pl.BlockSpec((nsq, tile, hw), lambda i, _: (0, i, 0)) for _ in range(parts)],
        ),
        out_shape=[
            jax.ShapeDtypeStruct((tok, model), BF),
            jax.ShapeDtypeStruct((tok, model), F32),
            jax.ShapeDtypeStruct((tok, model), BF),
            jax.ShapeDtypeStruct((1, model), F32),
        ]
        + [jax.ShapeDtypeStruct((nsq, tok, hw), BF) for _ in range(parts)],
        compiler_params=pltpu.CompilerParams(vmem_limit_bytes=40 * 1024 * 1024),
        cost_estimate=pl.CostEstimate(
            flops=2 * tok * model * count * hw, bytes_accessed=26 * tok * model, transcendentals=0
        ),
        name="split",
    )(scalars, middle, *mlps, *second_grads, grad_low, wall, gain)


def out_grad_kernel(block, scalars, ml_ref, mixed_ref, _, __, keep_ref, send_ref):
    model = ml_ref.shape[1]
    step = min(256, model)
    for k in range(model // step):
        rows = slice(k * step // 2, (k + 1) * step // 2)
        value = dot_tn(ml_ref[:, k * step : (k + 1) * step], mixed_ref[0])
        value = core_halves(scalars[2], block, value)
        keep_ref[0, rows, :] = value[0].astype(BF)
        send_ref[0, rows, :] = value[1].astype(BF)


def out_proj_grad(scalars, middle_low, mixed_part, halves, r, parts, nsq, hw, block):
    tok, model = middle_low.shape
    shape = halves[0].shape
    half = pl.BlockSpec((1, model // 2, hw), lambda s, sc: (s * parts + (sc[0] ^ r), 0, 0))
    return pl.pallas_call(
        functools.partial(out_grad_kernel, block),
        grid_spec=pltpu.PrefetchScalarGridSpec(
            num_scalar_prefetch=1,
            grid=(nsq,),
            in_specs=[
                pl.BlockSpec((tok, model), lambda s, _: (0, 0)),
                pl.BlockSpec((1, tok, hw), lambda s, _: (s, 0, 0)),
                pl.BlockSpec(memory_space=pl.ANY),
                pl.BlockSpec(memory_space=pl.ANY),
            ],
            out_specs=[half, half],
        ),
        out_shape=[jax.ShapeDtypeStruct(shape, BF)] * 2,
        input_output_aliases={3: 0, 4: 1},
        compiler_params=pltpu.CompilerParams(vmem_limit_bytes=40 * 1024 * 1024),
        cost_estimate=pl.CostEstimate(
            flops=2 * tok * model * nsq * hw, bytes_accessed=2 * tok * model * 2, transcendentals=0
        ),
        name="out_proj_grad",
    )(scalars, middle_low, mixed_part, *halves)


def rounded(size):
    return size + -size % 128


def unit_halves(units):
    first = rounded(units * 7 // 10)
    return first, units - first


def pack_kernel(lay, q_ref, k_ref, v_ref, r_ref, g_ref, out_ref, gate_ref, up_ref, down_ref, mix_ref, *all_refs):
    mix_ref[:, lay.q : lay.k] = q_ref[...]
    mix_ref[:, lay.k : lay.v] = k_ref[...]
    mix_ref[:, lay.v : lay.g] = v_ref[...]
    mix_ref[:, lay.g : lay.r] = g_ref[...]
    mix_ref[:, lay.r : lay.width] = jnp.zeros((mix_ref.shape[0], 128), BF)
    mix_ref[:, lay.r : lay.r + r_ref.shape[1]] = r_ref[...]
    hw, units = out_ref.shape[0], gate_ref.shape[1]
    all_refs[0][:, 0:hw] = out_ref[...].astype(F32).T.astype(BF)
    down = down_ref[...].astype(F32).T.astype(BF)
    start, lead = 0, hw
    for ref, size in zip(all_refs, unit_halves(units)):
        cols = slice(start, start + size)
        end = lead + 3 * size
        ref[:, lead : lead + size] = gate_ref[:, cols]
        ref[:, lead + size : lead + 2 * size] = up_ref[:, cols]
        ref[:, lead + 2 * size : end] = down[:, cols]
        if end < ref.shape[1]:
            ref[:, end:] = jnp.zeros((ref.shape[0], ref.shape[1] - end), BF)
        start, lead = start + size, 0


def pack(lay, w_query, w_key, w_value, w_rates, w_outgate, w_out, w_gate, w_up, w_down):
    rows = w_query.shape[0]
    one, two = unit_halves(w_gate.shape[1])
    return pl.pallas_call(
        functools.partial(pack_kernel, lay),
        out_shape=[
            jax.ShapeDtypeStruct((rows, lay.width), BF),
            jax.ShapeDtypeStruct((rows, rounded(w_out.shape[0] + 3 * one)), BF),
            jax.ShapeDtypeStruct((rows, rounded(3 * two)), BF),
        ],
        name="pack",
    )(w_query, w_key, w_value, w_rates, w_outgate, w_out, w_gate, w_up, w_down)


def unpack_kernel(hw, one, two, a_ref, b_ref, out_ref, gate_ref, up_ref, down_ref):
    a, b = a_ref[...].astype(F32), b_ref[...].astype(F32)
    out_ref[...] = b[:, :hw].T
    gate_ref[:, 0:one] = a[:, :one]
    gate_ref[:, one:] = b[:, hw : hw + two]
    up_ref[:, 0:one] = a[:, one : 2 * one]
    up_ref[:, one:] = b[:, hw + two : hw + 2 * two]
    down_ref[0:one, :] = a[:, 2 * one : 3 * one].T
    down_ref[one:, :] = b[:, hw + 2 * two : hw + 3 * two].T


def unpack(own_a, own_b, hw, units):
    one, two = unit_halves(units)
    rows = own_a.shape[0]
    shapes = [(hw, rows), (rows, units), (rows, units), (units, rows)]
    return pl.pallas_call(
        functools.partial(unpack_kernel, hw, one, two),
        out_shape=[jax.ShapeDtypeStruct(shape, F32) for shape in shapes],
        name="unpack",
    )(own_a, own_b)


def unpack_mix_kernel(lay, nrates, own_ref, q_ref, k_ref, v_ref, r_ref, g_ref):
    own = own_ref[...].astype(F32)
    q_ref[...] = own[:, lay.q : lay.k]
    k_ref[...] = own[:, lay.k : lay.v]
    v_ref[...] = own[:, lay.v : lay.g]
    r_ref[...] = own[:, lay.r : lay.r + nrates]
    g_ref[...] = own[:, lay.g : lay.r]


def unpack_mix(own, lay, nrates):
    rows = own.shape[0]
    widths = (lay.k - lay.q, lay.v - lay.k, lay.g - lay.v, nrates, lay.r - lay.g)
    return pl.pallas_call(
        functools.partial(unpack_mix_kernel, lay, nrates),
        out_shape=[jax.ShapeDtypeStruct((rows, width), F32) for width in widths],
        name="unpack_mix",
    )(own)
STEP = 4


def rms_parts(values):
    scale = lax.rsqrt(jnp.mean(values * values, axis=-1, keepdims=True) + EPS)
    return values * scale, scale


def bits(axis):
    return [1 << k for k in range((lax.axis_size(axis) - 1).bit_length())]


def trade(values, axis, bit):
    return lax.ppermute(values, axis, [(i, i ^ bit) for i in range(lax.axis_size(axis))])


def everyone(values):
    for axis in ("core", "dz", "sq", "sub"):
        for bit in bits(axis):
            values = values + trade(values, axis, bit)
    return values


def plus(left, right):
    return (left.astype(F32) + right.astype(F32)).astype(BF)


def swap(values, which, parts):
    return lax.ppermute(values, "sub", [(i, i ^ which) for i in range(parts)])


def per_device(
    tokens, lengths, out_grad, ln1_gain, ln2_gain, onorm_gain, a_log, dt_bias,
    w_query, w_key, w_value, w_rates, w_outgate, w_out, w_gate, w_up, w_down,
):
    nsq, parts = lax.axis_size("sq"), lax.axis_size("sub")
    which_seq, place = lax.axis_index("sq"), lax.axis_index("sub")
    count = nsq * parts
    tok_dev, model = tokens.shape
    heads = a_log.shape[0] // count
    lay = Layout(heads)
    units = w_gate.shape[1]
    hw = heads * HEAD
    place_arr = place.astype(jnp.int32).reshape(1)

    mix_shard, *ff_shards = pack(
        lay, w_query, w_key, w_value, w_rates, w_outgate, w_out, w_gate, w_up, w_down
    )
    w_mix = lax.all_gather(mix_shard, ("sq", "dz", "core"), axis=0, tiled=True)
    w_mix = w_mix.reshape(nsq, model, lay.width)
    walls = [
        lax.all_gather(shard, ("sq", "sub", "dz", "core"), axis=0, tiled=True).reshape(count, model, -1)
        for shard in ff_shards
    ]
    one, two = unit_halves(units)

    resid_in = tokens.astype(F32)
    normed_one, scale_one = rms_parts(resid_in)
    first = (normed_one * ln1_gain).astype(BF)
    first_seq = jnp.concatenate([first] + [swap(first, r, parts) for r in range(1, parts)], axis=0)

    pre = [dot_nn(first_seq, w_mix[s]) for s in range(nsq)]
    hpos = [(s * parts + place) * heads for s in range(nsq)]
    lanes = np.stack([8 * (c * nsq + s) + 3 * np.arange(heads) + 2 for c in range(STEP) for s in range(nsq)])

    def spread(values):
        mine = jnp.stack([lax.dynamic_slice_in_dim(values, hpos[s], heads) for s in range(nsq)])
        return jnp.zeros((128,), F32).at[lanes.ravel()].set(jnp.tile(mine.ravel(), STEP))

    params = jnp.stack([spread(-jnp.exp(a_log)), spread(dt_bias)])
    gain = onorm_gain.reshape(1, HEAD)
    mixed, *kept = mixer_forward(place_arr, parts, pre, params, gain, heads, STEP)

    got = [mixed] + [swap(mixed[:, r * tok_dev : (r + 1) * tok_dev], r, parts) for r in range(1, parts)]

    limit = jnp.sum(jnp.where(jnp.arange(nsq) == which_seq, lengths, 0)).astype(jnp.int32)
    scalars = jnp.stack([place.astype(jnp.int32), limit, lax.axis_index("core").astype(jnp.int32)])
    block = w_gate.shape[0]
    middle, second, grad_low = join(
        scalars, got, tokens, out_grad, walls[0], ln2_gain.reshape(1, model), parts, nsq, hw
    )
    def chips(pair):
        total = plus(pair[0], trade(pair[1], "core", 1))
        return total.reshape(count * model // 2, -1)

    def plane(values):
        return lax.psum_scatter(values, ("sq", "sub"), scatter_dimension=0, tiled=True)

    def column(values):
        return lax.psum_scatter(values, "dz", scatter_dimension=0, tiled=True)

    mlp_a, sg_a, *grads_a = feed_forward(
        scalars, second, grad_low, walls[0], hw, 0, rounded(3 * one), one, block
    )
    grads_a, wall_b = lax.optimization_barrier((chips(grads_a), walls[1]))
    grads_a = plane(grads_a)
    mlp_b, sg_b, *grads_b = feed_forward(
        scalars, second, grad_low, wall_b, 0, hw, hw + rounded(3 * two), two, block
    )
    block_out, middle_grad, middle_low, ln2_grad, *back = split(
        scalars, middle, (mlp_a, mlp_b), (sg_a, sg_b), grad_low, walls[0],
        ln2_gain.reshape(1, model), parts, nsq, hw,
    )
    for r in range(parts):
        grads_b = out_proj_grad(scalars, middle_low, got[r], grads_b, r, parts, nsq, hw, block)

    dmixed = jnp.concatenate([back[0]] + [swap(back[r], r, parts) for r in range(1, parts)], axis=1)
    dmixed, grads_b, grads_a = lax.optimization_barrier((dmixed, chips(grads_b), grads_a))
    own_a = column(grads_a)
    grads_b = plane(grads_b)
    chains = nsq * heads
    dpre = (jnp.zeros((chains, HEAD, HEAD), F32), jnp.zeros((8, 128), F32))
    for at in range(parts):
        *dpre, carry, small = mixer_backward(
            place_arr, parts, pre, params, gain, *kept, dmixed, heads, STEP, at, dpre
        )
        if at == 0:
            carry, grads_b = lax.optimization_barrier((carry, grads_b))
            own_b = column(grads_b)
        if at < parts - 1:
            dpre = (carry, small, *dpre)
    own_out, own_gate, own_up, own_down = unpack(own_a, own_b, hw, units)

    def back_rows(values, r):
        rows = slice(r * tok_dev, (r + 1) * tok_dev)
        total = dot_nt(values[0][rows], w_mix[0])
        for s in range(1, nsq):
            total = total + dot_nt(values[s][rows], w_mix[s])
        return total, jnp.sum(total * first_seq[rows].astype(F32), axis=0)

    mix_grads = jnp.concatenate([dot_tn(first_seq, dpre[s]).astype(BF) for s in range(nsq)], axis=0)
    dpre, mix_grads = lax.optimization_barrier((dpre, mix_grads))
    mix_own = lax.psum_scatter(mix_grads, ("sq", "dz", "core"), scatter_dimension=0, tiled=True)
    leaving = [back_rows(dpre, r) for r in range(1, parts)]
    arriving = [swap(leaving[r - 1][0].astype(BF), r, parts) for r in range(1, parts)]
    first_grad, ln1_grad = back_rows(dpre, 0)
    for r in range(1, parts):
        ln1_grad = ln1_grad + leaving[r - 1][1]
    ln1_grad = ln1_grad / ln1_gain
    first_grad, ln1_grad = lax.optimization_barrier((first_grad, ln1_grad))
    for r in range(1, parts):
        first_grad = first_grad + arriving[r - 1].astype(F32)
    scaled = first_grad * ln1_gain
    input_back = scale_one * (scaled - normed_one * jnp.mean(scaled * normed_one, axis=-1, keepdims=True))
    tokens_grad = (middle_grad + input_back).astype(BF)

    def gather_heads(row):
        mine = jnp.sum(row[lanes].reshape(STEP, nsq, heads), axis=0)
        full = jnp.zeros(a_log.shape, F32)
        for s in range(nsq):
            full = lax.dynamic_update_slice_in_dim(full, mine[s], hpos[s], 0)
        return full

    a_grad, dt_grad = gather_heads(small[2]), gather_heads(small[1])
    total = everyone(jnp.concatenate([ln1_grad, ln2_grad[0], small[0], a_grad, dt_grad]))
    marks = np.cumsum([0, model, model, HEAD, a_log.shape[0], a_log.shape[0]])
    return (
        block_out, tokens_grad, *[total[i:j] for i, j in zip(marks[:-1], marks[1:])],
        *unpack_mix(mix_own, lay, w_rates.shape[1]),
        own_out, own_gate, own_up, own_down,
    )


def solution(mesh):
    dp, tensor = mesh.shape["dp"], mesh.shape["tensor"]

    def run(*args):
        nsq = args[1].shape[0] // dp
        split = Mesh(
            mesh.devices.reshape(dp // 2, 2, nsq, tensor // nsq), ("dz", "core", "sq", "sub")
        )
        rows = P(("dz", "core", "sq", "sub"), None)
        down = P(("dz", "core"), ("sq", "sub"))
        across = P(("sq", "sub"), ("dz", "core"))
        in_specs = (rows, P(("dz", "core")), rows) + (P(),) * 5 + (down,) * 5 + (across, down, down, across)
        out_specs = (rows, rows) + (P(),) * 5 + (down,) * 5 + (across, down, down, across)
        return jax.shard_map(
            per_device, mesh=split, in_specs=in_specs, out_specs=out_specs, check_vma=False
        )(*args)

    return run
```

time: 652 us -> 596 us (0.914); the launches traced: 649 us -> 585 us
  Pallas kernels: 295 us -> 244 us
  waiting for transfers between devices: 195 us -> 181 us
  other arithmetic: 20.5 us -> 30.6 us
    ppermute x11 -> x7, waiting for transfers between devices: 96.7 us -> 42 us  [trade(): lax.ppermute(values, axis, [(i, i ^ bit) for i in range(lax.axis_size(axi...]
    pallas_call x1, Pallas kernels: 85 us -> 51.7 us  [mixer_forward(): pl.pallas_call(functools.partial(forward_kernel, lay, nsq, heads, nb), gr...]
    pallas_call x1 -> x2, Pallas kernels: 115 us -> 82.6 us  [mixer_backward(): pl.pallas_call(functools.partial(backward_kernel, lay, nsq, heads, nb), g...]
    ppermute x4, waiting for transfers between devices: 81.8 us -> 111 us  [swap(): return lax.ppermute(values, 'sub', [(i, i ^ which) for i in range(parts)])]
    reduce_scatter x0 -> x5, waiting for transfers between devices: none -> 13.6 us  [the longest x1 8.2 us: per_device(): lax.psum_scatter(mix_grads, ('sq', 'dz', 'core'), scatter_dimension=0, ti...]
    pallas_call x3 -> x6, Pallas kernels: 74.9 us -> 87 us  [the longest x2 78.4 us: feed_forward(): pl.pallas_call(functools.partial(ff_kernel, min(TILE, tok), block, lead,...]
    convert_element_type x2, other arithmetic: 2.05 us -> 11.8 us  [plus(): return (left.astype(F32) + right.astype(F32)).astype(BF)]
    unnamed x61 -> x70, local copies, waits for them, and re-layouts: 14.6 us -> 20.2 us
  transfers between devices with their start and end apart: 18 -> 19, of which waited for: 12 -> 12; matrix products, arithmetic and copies ran while one was open for 18% -> 20% of each run, Pallas kernels for 32% -> 41%
where the time goes in v3:
time: 596 us; the launch traced here: 585 us
  Pallas kernels  244 us (41%)
  waiting for transfers between devices  181 us (30%)
  matrix products  75.3 us (13%)
  other arithmetic  30.6 us (5%)
  local copies, waits for them, and re-layouts  30.3 us (5%)
  between operations  14.8 us (2%)
  starting transfers between devices  8.78 us (1%)
    ppermute x4, waiting for transfers between devices, swap(): return lax.ppermute(values, 'sub', [(i, i ^ which) for i in range(parts)])  111 us
    pallas_call x2, Pallas kernels, mixer_backward(): pl.pallas_call(functools.partial(backward_kernel, lay, nsq, heads, nb), g...  82.6 us
    pallas_call x2, Pallas kernels, feed_forward(): pl.pallas_call(functools.partial(ff_kernel, min(TILE, tok), block, lead,...  78.4 us
    pallas_call x1, Pallas kernels, mixer_forward(): pl.pallas_call(functools.partial(forward_kernel, lay, nsq, heads, nb), gr...  51.7 us
    ppermute x7, waiting for transfers between devices, trade(): lax.ppermute(values, axis, [(i, i ^ bit) for i in range(lax.axis_size(axi...  42 us
    dot_general x2, matrix products, dot_nn(): return jnp.dot(left, right, preferred_element_type=F32)  27.3 us
    dot_general x4, matrix products, dot_nt(): lax.dot_general(left, right, (((1,), (1,)), ((), ())), preferred_element_...  26.1 us
    dot_general x2, matrix products, dot_tn(): lax.dot_general(left, right, (((0,), (0,)), ((), ())), preferred_element_...  21.9 us
  transfers between devices with their start and end apart: 19, of which 12 were waited for; matrix products, arithmetic and copies ran while one was open for 20% of the time, Pallas kernels for 41%

profile of v3, /device:TPU:0, one launch (start us, length us, event | category | flops | bytes accessed | tf_op | source)
XLA Modules:
  0.0 585.3 jit_solution(12757575423520671721)
XLA Ops:
  7.3 1.5 copy.61.r_ref
  8.8 1.7 copy.62.gate_ref
  10.5 1.7 copy.63.up_ref
  12.3 2.4 pack.1
  15.5 2.1 fusion.9
  18.2 1.9 fusion.3
  20.1 2.9 collective-permute-start
  25.6 43.4 %collective-permute-done = bf16[1024,1024]{1,0:T(8,128)(2,1)} collective-permute-done((bf16[1024,1024]{1,0:T(8,128)(2,1)}, bf16[1024,1024]{1,0:T(8,128)(2,1)}, u32[]{:S(2)}, u32[]{:S(2)}) %collective-permute-start) | collective-permute-done | bytes 2097184 | tf_op jit(solution)/shard_map/ppermute | solution.py:782
  69.0 13.6 %all-gather.4.cloned.1.call-done = bf16[2048,1664]{1,0:T(8,128)(2,1)} async-done(((bf16[128,1664]{1,0:T(8,128)(2,1)}), bf16[2048,1664]{1,0:T(8,128)(2,1)}) %all-gather.4.cloned.1.call-update) | async-done | bytes 6815760 | tf_op jit(solution)/shard_map/all_gather | solution.py:802
  82.6 14.2 %fusion.20.refs_1_ = f32[2048,1664]{1,0:T(8,128)} fusion(bf16[2048,1664]{1,0:T(8,128)(2,1)} %all-gather.4.cloned.1.call-done, bf16[1024,1024]{1,0:T(8,128)(2,1)} %collective-permute-done, bf16[1024,1024]{1,0:T(8,128)(2,1)} %fusion.3), kind=kOutput, calls=%fused_computation.35 | convolution fusion | flops 6987710464 | bytes 21233664 | tf_op jit(solution)/shard_map/dot_general | solution.py:22
  96.7 13.1 %fusion.24.refs_0_ = f32[2048,1664]{1,0:T(8,128)} fusion(bf16[2048,1664]{1,0:T(8,128)(2,1)S(1)} %copy-done.23, bf16[1024,1024]{1,0:T(8,128)(2,1)} %collective-permute-done, bf16[1024,1024]{1,0:T(8,128)(2,1)} %fusion.3), kind=kOutput, calls=%fused_computation.39 | convolution fusion | flops 6987710464 | bytes 21233664 | tf_op jit(solution)/shard_map/dot_general | solution.py:22
  109.8 51.7 %mixer_forward.1 = (bf16[2,2048,256]{2,1,0:T(8,128)(2,1)}, bf16[32,4,128,128]{3,2,1,0:T(8,128)(2,1)}, bf16[32,4,128,128]{3,2,1,0:T(8,128)(2,1)}, bf16[32,4,128,1...) custom-call(s32[1]{0:T(128)} %bitcast._, f32[2048,1664]{1,0:T(8,128)} %fusion.24.refs_0_, ...), custom_call_target="tpu_custom_call" | custom-call | flops 10737418240 | bytes 46137344 | tf_op jit(solution)/shard_map/mixer_forward/pallas_call | solution.py:370
  161.5 2.3 slice.65
  166.7 25.8 %collective-permute-done.1.refs_1_.mixed_ref = bf16[2,1024,256]{2,1,0:T(8,128)(2,1)S(1)} collective-permute-done((bf16[2,1024,256]{2,1,0:T(8,128)(2,1)}, bf16[2,1024,256]{2,1,0:T(8,128)(2,1)S(1)}, u32[]{:S(2)}, u32[]{:S(2)}) %collective-permute-start.1) | collective-permute-done | bytes 1048608 | tf_op jit(solution)/shard_map/ppermute | solution.py:782
  192.5 1.6 copy-done.4
  194.1 1.6 copy-done.8
  195.7 7.4 %join.1 = (f32[1024,1024]{1,0:T(8,128)}, bf16[1024,1024]{1,0:T(8,128)(2,1)S(1)}, bf16[1024,1024]{1,0:T(8,128)(2,1)S(1)}) custom-call(s32[3]{0:T(128)S(1)} %pad_add_fusion.scalars, bf16[2,2048,256]{2,1,0:T(8,128)(2,1)S(1)} %copy-done.4, bf16[2,1024,256]{2,1,0:T(8,128)(2,1)S(1)} %collective-permute-done.1.refs_1_.mixed_ref, bf16[1024,1024]{1,0:T(8,128)(2,1)S(1)} %copy-done, ...), custom_call_target="tpu_custom_call" | custom-call | flops 2147483648 | bytes 14680064 | tf_op jit(solution)/shard_map/join/pallas_call | solution.py:472
  205.7 48.6 %feed_forward.2 = (f32[1024,1024]{1,0:T(8,128)}, f32[1024,1024]{1,0:T(8,128)}, bf16[4,512,1536]{2,1,0:T(8,128)(2,1)}, bf16[4,512,1536]{2,1,0:T(8,128)(2,1)}) custom-call(s32[3]{0:T(128)} %copy-done.12, bf16[1024,1024]{1,0:T(8,128)(2,1)} %copy-done.14, bf16[1024,1024]{1,0:T(8,128)(2,1)} %copy-done.9, bf16[4,1024,1792]{2,1,0:T(8,128)(2,1)} %bitcast.42), custom_call_target="tpu_custom_call" | custom-call | flops 38654705664 | bytes 41943040 | tf_op jit(solution)/shard_map/feed_forward/pallas_call | solution.py:548
  254.5 12.0 %collective-permute-done.2 = bf16[4,512,1536]{2,1,0:T(8,128)(2,1)} collective-permute-done((bf16[4,512,1536]{2,1,0:T(8,128)(2,1)}, bf16[4,512,1536]{2,1,0:T(8,128)(2,1)}, u32[]{:S(2)}, u32[]{:S(2)}) %collective-permute-start.2) | collective-permute-done | bytes 6291488 | tf_op jit(solution)/shard_map/ppermute | solution.py:767
  266.5 9.0 %add_convert_fusion = bf16[4,512,1536]{2,1,0:T(8,128)(2,1)} fusion(bf16[4,512,1536]{2,1,0:T(8,128)(2,1)} %collective-permute-done.2, bf16[4,512,1536]{2,1,0:T(8,128)(2,1)} %get-tuple-element.81), kind=kLoop, calls=%fused_computation.4 | loop fusion | flops 12582912 | bytes 18874368 | tf_op jit(solution)/shard_map/convert_element_type | solution.py:778
  275.6 29.7 %feed_forward.3 = (f32[1024,1024]{1,0:T(8,128)}, f32[1024,1024]{1,0:T(8,128)}, bf16[4,512,896]{2,1,0:T(8,128)(2,1)}, bf16[4,512,896]{2,1,0:T(8,128)(2,1)}) custom-call(s32[3]{0:T(128)} %copy-done.12, bf16[1024,1024]{1,0:T(8,128)(2,1)} %copy-done.14, bf16[1024,1024]{1,0:T(8,128)(2,1)} %copy-done.9, bf16[4,1024,640]{2,1,0:T(8,128)(2,1)} %bitcast.57), custom_call_target="tpu_custom_call" | custom-call | flops 14495514624 | bytes 23068672 | tf_op jit(solution)/shard_map/feed_forward/pallas_call | solution.py:548
  305.4 1.6 copy-done.10
  307.0 13.1 %split.1 = (bf16[1024,1024]{1,0:T(8,128)(2,1)}, f32[1024,1024]{1,0:T(8,128)S(1)}, bf16[1024,1024]{1,0:T(8,128)(2,1)S(1)}, f32[1,1024]{1,0:T(1,128)S(1)}, bf16[2,...) custom-call(s32[3]{0:T(128)S(1)} %copy-done.13, f32[1024,1024]{1,0:T(8,128)} %get-tuple-element.77.refs_0_, ...), custom_call_target="tpu_custom_call" | custom-call | flops 2147483648 | bytes 27262976 | tf_op jit(solution)/shard_map/split/pallas_call | solution.py:608
  320.1 2.3 out_proj_grad.2
  322.4 2.3 out_proj_grad.3
  324.8 41.7 %collective-permute-done.3 = bf16[2,1024,256]{2,1,0:T(8,128)(2,1)S(1)} collective-permute-done((bf16[2,1024,256]{2,1,0:T(8,128)(2,1)S(1)}, bf16[2,1024,256]{2,1,0:T(8,128)(2,1)S(1)}, u32[]{:S(2)}, u32[]{:S(2)}) %collective-permute-start.3) | collective-permute-done | bytes 1048608 | tf_op jit(solution)/shard_map/ppermute | solution.py:782
  368.0 2.8 add_convert_fusion.1
  372.8 41.2 %mixer_backward.2 = (bf16[2048,1664]{1,0:T(8,128)(2,1)}, bf16[2048,1664]{1,0:T(8,128)(2,1)}, f32[4,128,128]{2,1,0:T(8,128)}, f32[8,128]{1,0:T(8,128)}) custom-call(s32[1]{0:T(128)} %bitcast._, f32[2048,1664]{1,0:T(8,128)} %fusion.24.refs_0_, f32[2048,1664]{1,0:T(8,128)} %fusion.20.refs_1_, f32[2,128]{1,0:T(2,128)} %pad_maximum_fusion.5.refs_2_, ...), custom_call_target="tpu_custom_call" | custom-call | flops 6979321856 | bytes 31981568 | tf_op jit(solution)/shard_map/mixer_backward/pallas_call | solution.py:415
  413.9 5.4 reduce-scatter.8.cloned.1.call-done
  419.4 41.4 %mixer_backward.3 = (bf16[2048,1664]{1,0:T(8,128)(2,1)}, bf16[2048,1664]{1,0:T(8,128)(2,1)}, f32[4,128,128]{2,1,0:T(8,128)}, f32[8,128]{1,0:T(8,128)}) custom-call(s32[1]{0:T(128)} %bitcast._, f32[2048,1664]{1,0:T(8,128)} %fusion.24.refs_0_, f32[2048,1664]{1,0:T(8,128)} %fusion.20.refs_1_, ...), custom_call_target="tpu_custom_call", output_to_operand_aliasing={{0}: (16, {}), {1}: (17, {})} | custom-call | flops 6979321856 | bytes 31981568 | tf_op jit(solution)/shard_map/mixer_backward/pallas_call | solution.py:415
  460.8 12.0 %convolution_convert_fusion.1 = bf16[1024,1664]{1,0:T(8,128)(2,1)S(1)} fusion(bf16[2048,1664]{1,0:T(8,128)(2,1)} %get-tuple-element.114, bf16[1024,1024]{1,0:T(8,128)(2,1)} %collective-permute-done, bf16[1024,1024]{1,0:T(8,128)(2,1)} %fusion.3), kind=kOutput, calls=%fused_computation.24 | convolution fusion | flops 6989414400 | bytes 14417920 | tf_op jit(solution)/shard_map/dot_general | solution.py:30
  472.8 10.0 %convolution_convert_fusion = bf16[1024,1664]{1,0:T(8,128)(2,1)S(1)} fusion(bf16[2048,1664]{1,0:T(8,128)(2,1)S(1)} %copy-done.16, bf16[1024,1024]{1,0:T(8,128)(2,1)} %collective-permute-done, bf16[1024,1024]{1,0:T(8,128)(2,1)} %fusion.3), kind=kOutput, calls=%fused_computation.23 | convolution fusion | flops 6989414400 | bytes 14417920 | tf_op jit(solution)/shard_map/dot_general | solution.py:30
  482.8 3.3 pad_maximum_fusion
  486.7 7.1 %fusion.10 = f32[1024,1024]{1,0:T(8,128)S(1)} fusion(bf16[2048,1664]{1,0:T(8,128)(2,1)} %get-tuple-element.115, bf16[2048,1664]{1,0:T(8,128)(2,1)} %all-gather.4.cloned.1.call-done), kind=kOutput, calls=%fused_computation.25 | convolution fusion | flops 3489660928 | bytes 11010048 | tf_op jit(solution)/shard_map/dot_general | solution.py:26
  493.9 8.1 %fusion.41 = (bf16[1024,1024]{1,0:T(8,128)(2,1)}, f32[1024]{0:T(1024)S(1)}) fusion(bf16[1024,1024]{1,0:T(8,128)(2,1)} %collective-permute-done, f32[1024,1024]{1,0:T(8,128)S(1)} %fusion.10, bf16[2048,1664]{1,0:T(8,128)(2,1)} %all-gather.4.cloned.1.call-done, bf16[2048,1664]{1,0:T(8,128)(2,1)S(1)} %bitcast.47), kind=kOutput, calls=%fused_computation.70 | convolution fusion | flops 3494902784 | bytes 15208448 | tf_op jit(solution)/shard_map/dot_general | solution.py:26
  503.2 4.0 fusion.14
  507.2 6.9 %multiply_reduce_fusion.1 = (f32[1024]{0:T(1024)S(1)}, f32[1024,1024]{1,0:T(8,128)}) fusion(bf16[1024,1024]{1,0:T(8,128)(2,1)} %fusion.3, f32[1024,1024]{1,0:T(8,128)S(1)} %fusion.14, bf16[2048,1664]{1,0:T(8,128)(2,1)S(1)} %bitcast.56, bf16[2048,1664]{1,0:T(8,128)(2,1)S(1)} %bitcast.47), kind=kOutput, calls=%fused_computation.22 | convolution fusion | flops 3493854208 | bytes 17305600 | tf_op jit(solution)/shard_map/dot_general | solution.py:26
  519.8 3.8 collective-permute-done.7
  524.7 5.0 collective-permute-done.8
  529.7 3.9 collective-permute-done.9
  533.6 16.1 %collective-permute-done.10 = f32[2192]{0:T(1024)S(1)} collective-permute-done((f32[2192]{0:T(1024)S(1)}, f32[2192]{0:T(1024)S(1)}, u32[]{:S(2)}, u32[]{:S(2)}) %collective-permute-start.10) | collective-permute-done | bytes 8800 | tf_op jit(solution)/shard_map/ppermute | solution.py:767
  551.4 2.2 unpack.1
  553.6 1.9 copy.65
  555.5 1.9 copy.66
  557.4 4.1 fusion.4
  562.7 3.9 fusion.8
  566.6 8.2 %reduce-scatter.10.cloned.1.call-done.own_ref = bf16[128,1664]{1,0:T(8,128)(2,1)} async-done(((bf16[2048,1664]{1,0:T(8,128)(2,1)}), bf16[128,1664]{1,0:T(8,128)(2,1)}) %reduce-scatter.10.cloned.1.call-update) | async-done | bytes 426000 | tf_op jit(solution)/shard_map/reduce_scatter | solution.py:886
  574.8 1.9 unpack_mix.1
  (143 shorter events, 26.4 us)
Async XLA Ops:
  7.2 11.0 %copy-start = (bf16[1024,1024]{1,0:T(8,128)(2,1)S(1)}, bf16[1024,1024]{1,0:T(8,128)(2,1)}, u32[]{:S(2)}) copy-start(bf16[1024,1024]{1,0:T(8,128)(2,1)} %refs_2_.1) | copy-start | bytes 6291460
  7.2 11.0 %copy-start.19 = (f32[1024]{0:T(1024)S(1)}, f32[1024]{0:T(1024)}, u32[]{:S(2)}) copy-start(f32[1024]{0:T(1024)} %param.36) | copy-start | bytes 12292
  7.2 75.4 %all-gather.4.cloned.1.call-start = ((), (), s32[]{:S(2)}) async-start(), calls=%async_computation.5 | async-start | bytes 7241728 | tf_op jit(solution)/shard_map/all_gather | solution.py:802
  12.3 10.7 %copy-start.24 = (f32[8]{0:T(128)S(1)}, f32[8]{0:T(128)}, u32[]{:S(2)}) copy-start(f32[8]{0:T(128)} %param.39) | copy-start | bytes 100
  12.3 10.8 %copy-start.21 = (f32[8]{0:T(128)S(1)}, f32[8]{0:T(128)}, u32[]{:S(2)}) copy-start(f32[8]{0:T(128)} %param.40) | copy-start | bytes 100
  14.7 177.8 %all-gather.6.cloned.1.call-start = ((), (), s32[]{:S(2)}) async-start(), calls=%async_computation.6 | async-start | bytes 15138816 | tf_op jit(solution)/shard_map/all_gather | solution.py:805
  15.5 260.1 %all-gather.8.cloned.1.call-start = ((), (), s32[]{:S(2)}) async-start(), calls=%async_computation.7 | async-start | bytes 5406720 | tf_op jit(solution)/shard_map/all_gather | solution.py:805
  20.1 48.9 %collective-permute-start = (bf16[1024,1024]{1,0:T(8,128)(2,1)}, bf16[1024,1024]{1,0:T(8,128)(2,1)}, u32[]{:S(2)}, u32[]{:S(2)}) collective-permute-start(bf16[1024,1024]{1,0:T(8,128)(2,1)} %fusion.3), channel_id=1, source_target_pairs={{0,1},{1,0},{2,3},{3,2},{4,5},{5,4},{6,7},{7,6},{8,9},{9,8},{10,11... | collective-permute-start | bytes 6291464 | tf_op jit(solution)/shard_map/ppermute | solution.py:782
  82.6 14.2 %copy-start.23 = (bf16[2048,1664]{1,0:T(8,128)(2,1)S(1)}, bf16[2048,1664]{1,0:T(8,128)(2,1)}, u32[]{:S(2)}) copy-start(bf16[2048,1664]{1,0:T(8,128)(2,1)} %all-gather.4.cloned.1.call-done) | copy-start | bytes 20447236
  109.8 55.5 %copy-start.25 = (s32[2]{0:T(128)S(1)}, s32[2]{0:T(128)}, u32[]{:S(2)}) copy-start(s32[2]{0:T(128)} %param.34) | copy-start | bytes 28
  109.8 82.7 %copy-start.11 = (f32[1024]{0:T(1024)S(1)}, f32[1024]{0:T(1024)}, u32[]{:S(2)}) copy-start(f32[1024]{0:T(1024)} %param.37) | copy-start | bytes 12292
  163.8 28.7 %collective-permute-start.1 = (bf16[2,1024,256]{2,1,0:T(8,128)(2,1)}, bf16[2,1024,256]{2,1,0:T(8,128)(2,1)S(1)}, u32[]{:S(2)}, u32[]{:S(2)}) collective-permute-start(bf16[2,1024,256]{2,1,0:T(8,128)(2,1)} %slice.65), channel_id=1, source_target_pairs={{0,1},{1,0},{2,3},{3,2},{4,5},{5,4},{6,7},{7,6},{8,9},{9,8},{10,11... | collective-permute-start | bytes 3145736 | tf_op jit(solution)/shard_map/ppermute | solution.py:782
  165.3 205.5 %reduce-scatter.6.cloned.1.call-start = ((), (), s32[]{:S(2)}) async-start(), calls=%async_computation.8 | async-start | bytes 7864320 | tf_op jit(solution)/shard_map/reduce_scatter | solution.py:840
  166.7 36.4 %copy-start.12 = (s32[3]{0:T(128)}, s32[3]{0:T(128)S(1)}, u32[]{:S(2)}) copy-start(s32[3]{0:T(128)S(1)} %pad_add_fusion.scalars) | copy-start | bytes 40
  192.5 1.6 copy-start.4
  194.1 1.6 copy-start.8
  204.4 1.3 copy-start.14
  254.4 12.1 %collective-permute-start.2 = (bf16[4,512,1536]{2,1,0:T(8,128)(2,1)}, bf16[4,512,1536]{2,1,0:T(8,128)(2,1)}, u32[]{:S(2)}, u32[]{:S(2)}) collective-permute-start(bf16[4,512,1536]{2,1,0:T(8,128)(2,1)} %get-tuple-element.82), channel_id=1, source_target_pairs={{0,4},{4,0},{1,5},{5,1},{2,6},{6,2},{3,7},{7,3},{8,12},{12,8},{9,1... | collective-permute-start | bytes 18874376 | tf_op jit(solution)/shard_map/ppermute | solution.py:767
  275.6 29.8 %copy-start.13 = (s32[3]{0:T(128)S(1)}, s32[3]{0:T(128)}, u32[]{:S(2)}) copy-start(s32[3]{0:T(128)} %copy-done.12) | copy-start | bytes 40
  275.6 143.7 %reduce-scatter.8.cloned.1.call-start = ((), (), s32[]{:S(2)}) async-start(), calls=%async_computation.9 | async-start | bytes 4587520 | tf_op jit(solution)/shard_map/reduce_scatter | solution.py:840
  305.4 1.6 copy-start.10
  307.0 13.1 %copy-start.2 = (bf16[4,512,896]{2,1,0:T(8,128)(2,1)S(1)}, bf16[4,512,896]{2,1,0:T(8,128)(2,1)}, u32[]{:S(2)}) copy-start(bf16[4,512,896]{2,1,0:T(8,128)(2,1)} %get-tuple-element.98._) | copy-start | bytes 11010052
  307.0 13.1 %copy-start.3 = (bf16[4,512,896]{2,1,0:T(8,128)(2,1)S(1)}, bf16[4,512,896]{2,1,0:T(8,128)(2,1)}, u32[]{:S(2)}) copy-start(bf16[4,512,896]{2,1,0:T(8,128)(2,1)} %get-tuple-element.99.__) | copy-start | bytes 11010052
  307.0 13.1 %copy-start.5 = (bf16[2,2048,256]{2,1,0:T(8,128)(2,1)S(1)}, bf16[2,2048,256]{2,1,0:T(8,128)(2,1)}, u32[]{:S(2)}) copy-start(bf16[2,2048,256]{2,1,0:T(8,128)(2,1)} %get-tuple-element.75.refs_0_.mixed_ref) | copy-start | bytes 6291460
  320.1 2.3 copy-start.6
  324.7 43.3 %collective-permute-start.4 = (bf16[4,512,896]{2,1,0:T(8,128)(2,1)S(1)}, bf16[4,512,896]{2,1,0:T(8,128)(2,1)S(1)}, u32[]{:S(2)}, u32[]{:S(2)}) collective-permute-start(bf16[4,512,896]{2,1,0:T(8,128)(2,1)S(1)} %get-tuple-element.103), channel_id=1, source_target_pairs={{0,4},{4,0},{1,5},{5,1},{2,6},{6,2},{3,7},{7,3},{8,12},{12,8},{9,1... | collective-permute-start | bytes 11010056 | tf_op jit(solution)/shard_map/ppermute | solution.py:767
  324.8 41.7 %collective-permute-start.3 = (bf16[2,1024,256]{2,1,0:T(8,128)(2,1)S(1)}, bf16[2,1024,256]{2,1,0:T(8,128)(2,1)S(1)}, u32[]{:S(2)}, u32[]{:S(2)}) collective-permute-start(bf16[2,1024,256]{2,1,0:T(8,128)(2,1)S(1)} %get-tuple-element.96), channel_id=1, source_target_pairs={{0,1},{1,0},{2,3},{3,2},{4,5},{5,4},{6,7},{7,6},{8,9},{9,8},{10,11... | collective-permute-start | bytes 3145736 | tf_op jit(solution)/shard_map/ppermute | solution.py:782
  370.8 180.6 %reduce-scatter.12.cloned.1.call-start = ((), (), s32[]{:S(2)}) async-start(), calls=%async_computation.11 | async-start | bytes 1966080 | tf_op jit(solution)/shard_map/reduce_scatter | solution.py:843
  371.4 180.0 %reduce-scatter.14.cloned.1.call-start = ((), (), s32[]{:S(2)}) async-start(), calls=%async_computation.12 | async-start | bytes 1146880 | tf_op jit(solution)/shard_map/reduce_scatter | solution.py:843
  419.3 155.5 %reduce-scatter.10.cloned.1.call-start = ((), (), s32[]{:S(2)}) async-start(), calls=%async_computation.10 | async-start | bytes 7241728 | tf_op jit(solution)/shard_map/reduce_scatter | solution.py:886
  460.8 12.0 %copy-start.16 = (bf16[2048,1664]{1,0:T(8,128)(2,1)S(1)}, bf16[2048,1664]{1,0:T(8,128)(2,1)}, u32[]{:S(2)}) copy-start(bf16[2048,1664]{1,0:T(8,128)(2,1)} %get-tuple-element.115) | copy-start | bytes 20447236
  486.1 7.8 %slice-start = ((s8[6815744]{0:T(1024)(128)(4,1)}), s8[2621440]{0:T(1024)(128)(4,1)S(1)}, s32[]{:S(2)}) async-start(s8[6815744]{0:T(1024)(128)(4,1)} %bitcast.46), calls=%async_computation.13 | async-start | bytes 5242880
  486.7 7.2 %slice-start.1 = ((s8[6815744]{0:T(1024)(128)(4,1)}), s8[4194304]{0:T(1024)(128)(4,1)S(1)}, s32[]{:S(2)}) async-start(s8[6815744]{0:T(1024)(128)(4,1)} %bitcast.46), calls=%async_computation.14 | async-start | bytes 8388608
  486.7 16.5 %slice-start.2 = ((s8[6815744]{0:T(1024)(128)(4,1)}), s8[4194304]{0:T(1024)(128)(4,1)S(1)}, s32[]{:S(2)}) async-start(s8[6815744]{0:T(1024)(128)(4,1)} %bitcast.48), calls=%async_computation.15 | async-start | bytes 8388608
  486.7 16.5 %slice-start.4 = ((s8[6815744]{0:T(1024)(128)(4,1)}), s8[4194304]{0:T(1024)(128)(4,1)S(1)}, s32[]{:S(2)}) async-start(s8[6815744]{0:T(1024)(128)(4,1)} %bitcast.55), calls=%async_computation.17 | async-start | bytes 8388608
  493.9 9.3 %slice-start.3 = ((s8[6815744]{0:T(1024)(128)(4,1)}), s8[2621440]{0:T(1024)(128)(4,1)S(1)}, s32[]{:S(2)}) async-start(s8[6815744]{0:T(1024)(128)(4,1)} %bitcast.48), calls=%async_computation.16 | async-start | bytes 5242880
  493.9 9.3 %slice-start.5 = ((s8[6815744]{0:T(1024)(128)(4,1)}), s8[2621440]{0:T(1024)(128)(4,1)S(1)}, s32[]{:S(2)}) async-start(s8[6815744]{0:T(1024)(128)(4,1)} %bitcast.55), calls=%async_computation.18 | async-start | bytes 5242880
  502.0 55.4 %collective-permute-start.5 = (bf16[1024,1024]{1,0:T(8,128)(2,1)}, bf16[1024,1024]{1,0:T(8,128)(2,1)}, u32[]{:S(2)}, u32[]{:S(2)}) collective-permute-start(bf16[1024,1024]{1,0:T(8,128)(2,1)} %get-tuple-element.164), channel_id=1, source_target_pairs={{0,1},{1,0},{2,3},{3,2},{4,5},{5,4},{6,7},{7,6},{8,9},{9,8},{10,11... | collective-permute-start | bytes 6291464 | tf_op jit(solution)/shard_map/ppermute | solution.py:782
  514.9 1.5 copy-start.20
  515.6 41.8 %copy-start.1 = (bf16[1024,1024]{1,0:T(8,128)(2,1)S(1)}, bf16[1024,1024]{1,0:T(8,128)(2,1)}, u32[]{:S(2)}) copy-start(bf16[1024,1024]{1,0:T(8,128)(2,1)} %refs_2_.1) | copy-start | bytes 6291460
  515.6 41.8 %copy-start.18 = (f32[1024]{0:T(1024)S(1)}, f32[1024]{0:T(1024)}, u32[]{:S(2)}) copy-start(f32[1024]{0:T(1024)} %copy-done.17) | copy-start | bytes 12292
  517.2 1.2 collective-permute-start.6
  518.3 5.2 collective-permute-start.7
  523.6 6.1 %collective-permute-start.8 = (f32[2192]{0:T(1024)S(1)}, f32[2192]{0:T(1024)S(1)}, u32[]{:S(2)}, u32[]{:S(2)}) collective-permute-start(f32[2192]{0:T(1024)S(1)} %add.98), channel_id=1, source_target_pairs={{0,16},{8,24},{16,0},{24,8},{1,17},{9,25},{17,1},{25,9},{2,18},{10... | collective-permute-start | bytes 26312 | tf_op jit(solution)/shard_map/ppermute | solution.py:767
  529.7 3.9 collective-permute-start.9
  533.6 16.1 %collective-permute-start.10 = (f32[2192]{0:T(1024)S(1)}, f32[2192]{0:T(1024)S(1)}, u32[]{:S(2)}, u32[]{:S(2)}) collective-permute-start(f32[2192]{0:T(1024)S(1)} %add.100), channel_id=1, source_target_pairs={{0,1},{1,0},{2,3},{3,2},{4,5},{5,4},{6,7},{7,6},{8,9},{9,8},{10,11... | collective-permute-start | bytes 26312 | tf_op jit(solution)/shard_map/ppermute | solution.py:767
  557.4 4.2 copy-start.7
  557.4 5.3 copy-start.15
  (3 other events, 2.5 us)
Sparse Core Ops, SparseCore 0:
  14.8 67.6 all-gather.3
  85.4 106.3 all-gather.5
  195.3 69.1 all-gather.7
  275.7 86.6 reduce-scatter.5
  370.9 48.3 reduce-scatter.7
  421.5 35.2 reduce-scatter.11
  459.1 24.0 reduce-scatter.13
  487.2 87.5 reduce-scatter.9

commit v4 on v3

--- a/solution.py
+++ b/solution.py
@@ -394,7 +394,7 @@
     )(place, *pre, params, gain, jnp.asarray(square), jnp.asarray(thin), jnp.asarray(sums3, BF))
 
 
-def mixer_backward(place, parts, pre, params, gain, tinv, wks, states, deltas, outs, dmixed, heads, nb, at, earlier):
+def mixer_backward(place, parts, pre, params, gain, tinv, wks, states, deltas, outs, dmixed, heads, nb, skip, steps, earlier):
     nsq, (length, width) = len(pre), pre[0].shape
     lay = Layout(heads)
     square, thin, sums3 = mixer_tables()
@@ -402,7 +402,7 @@
     chains = nsq * heads
     span = nb * CT
     per_part = nchunk // nb // parts
-    last = nchunk // nb - 1 - at * per_part
+    last = nchunk // nb - 1 - skip
     big = lambda: pl.BlockSpec((nb, chains, ROWS, HEAD), lambda i, _: (last - i, 0, 0, 0))
     rows = lambda w: pl.BlockSpec(
         (nsq, span, w), lambda i, place: (0, part_chunk(last - i, place, per_part), 0)
@@ -416,7 +416,7 @@
         functools.partial(backward_kernel, lay, nsq, heads, nb),
         grid_spec=pltpu.PrefetchScalarGridSpec(
             num_scalar_prefetch=1,
-            grid=(per_part,),
+            grid=(steps,),
             in_specs=[wide() for _ in pre]
             + shared_specs(square, thin, sums3)
             + [big(), big(), big(), big(), rows(heads * HEAD), rows(heads * HEAD), held, sums]
@@ -429,8 +429,8 @@
         input_output_aliases={first_done + k: k for k in range(len(done))},
         compiler_params=pltpu.CompilerParams(vmem_limit_bytes=56 * 1024 * 1024),
         cost_estimate=pl.CostEstimate(
-            flops=nchunk // parts * chains * 26 * 2 * ROWS**3,
-            bytes_accessed=(nsq * length * (6 * width + 6 * heads * HEAD) + nchunk * chains * 8 * ROWS**2) // parts,
+            flops=steps * nb * chains * 26 * 2 * ROWS**3,
+            bytes_accessed=(nsq * length * (6 * width + 6 * heads * HEAD) + nchunk * chains * 8 * ROWS**2) * steps * nb // nchunk,
             transcendentals=0,
         ),
         name="mixer_backward",
@@ -500,12 +500,9 @@
     return jnp.where(core == 0, even, odd), jnp.where(core == 0, odd, even)
 
 
-def ff_kernel(
-    tile, block, lead, lead_out, units, scalars, sec_ref, grad_ref, w_ref, mlp_ref, sg_ref, keep_ref, send_ref, hid, both
-):
+def ff_tiles(tile, lead, units, sec_ref, grad_ref, w_ref, mlp_ref, sg_ref, store):
     tok, model = sec_ref.shape
     mid, end = lead + 2 * units, lead + 3 * units
-    mid_out, end_out = lead_out + 2 * units, lead_out + 3 * units
 
     @pl.when(pl.program_id(0) == 0)
     def _():
@@ -520,33 +517,46 @@
         sig = sigm(gate_pre)
         act = gate_pre * sig
         hidden = (act * up_pre).astype(BF)
-        hid[rows, :] = hidden
         gate_low = (hidden_grad * up_pre * (sig + act * (1.0 - sig))).astype(BF)
         up_low = (hidden_grad * act).astype(BF)
         both_low = jnp.concatenate([gate_low, up_low], axis=1)
-        both[rows, :] = both_low
+        store(rows, hidden, both_low)
         mlp_ref[rows, :] += dot_nt(hidden, w_ref[0, :, mid:end])
         sg_ref[rows, :] += dot_nt(both_low, w_ref[0, :, lead:mid])
+
+
+def weight_tiles(core, block, lead_out, sec_ref, grad_ref, hid, both, keep_ref, send_ref):
+    model, units = sec_ref.shape[1], hid.shape[1]
+    mid_out, end_out = lead_out + 2 * units, lead_out + 3 * units
     step = min(256, model)
     for k in range(model // step):
         cols = slice(k * step, (k + 1) * step)
         rows = slice(k * step // 2, (k + 1) * step // 2)
-        value = core_halves(scalars[2], block, dot_tn(sec_ref[:, cols], both[...]))
+        value = core_halves(core, block, dot_tn(sec_ref[:, cols], both[...]))
         keep_ref[0, rows, lead_out:mid_out] = value[0].astype(BF)
         send_ref[0, rows, lead_out:mid_out] = value[1].astype(BF)
-        value = core_halves(scalars[2], block, dot_tn(grad_ref[:, cols], hid[...]))
+        value = core_halves(core, block, dot_tn(grad_ref[:, cols], hid[...]))
         keep_ref[0, rows, mid_out:end_out] = value[0].astype(BF)
         send_ref[0, rows, mid_out:end_out] = value[1].astype(BF)
 
 
-def feed_forward(scalars, second, grad_low, wall, lead, lead_out, width_out, units, block):
+def ff_kernel(tile, block, lead, units, scalars, sec_ref, grad_ref, w_ref, mlp_ref, sg_ref, keep_ref, send_ref, hid, both):
+    def store(rows, hidden, both_low):
+        hid[rows, :] = hidden
+        both[rows, :] = both_low
+
+    ff_tiles(tile, lead, units, sec_ref, grad_ref, w_ref, mlp_ref, sg_ref, store)
+    weight_tiles(scalars[2], block, 0, sec_ref, grad_ref, hid, both, keep_ref, send_ref)
+
+
+def feed_forward(scalars, second, grad_low, wall, lead, width_out, units, block):
     tok, model = second.shape
     count, _, width = wall.shape
     whole = pl.BlockSpec((tok, model), lambda p, _: (0, 0))
     weight = pl.BlockSpec((1, model, width), lambda p, _: (p, 0, 0))
     half = pl.BlockSpec((1, model // 2, width_out), lambda p, _: (p, 0, 0))
     return pl.pallas_call(
-        functools.partial(ff_kernel, min(TILE, tok), block, lead, lead_out, units),
+        functools.partial(ff_kernel, min(TILE, tok), block, lead, units),
         grid_spec=pltpu.PrefetchScalarGridSpec(
             num_scalar_prefetch=1,
             grid=(count,),
@@ -568,6 +578,82 @@
         ),
         name="feed_forward",
     )(scalars, second, grad_low, wall)
+
+
+def ff_rest_kernel(tile, units, sec_ref, grad_ref, w_ref, mlp_ref, sg_ref, hid_ref, both_ref):
+    def store(rows, hidden, both_low):
+        hid_ref[0, rows, :] = hidden
+        both_ref[0, rows, :] = both_low
+
+    ff_tiles(tile, 0, units, sec_ref, grad_ref, w_ref, mlp_ref, sg_ref, store)
+
+
+def feed_forward_rest(second, grad_low, wall, units):
+    tok, model = second.shape
+    count, _, width = wall.shape
+    whole = pl.BlockSpec((tok, model), lambda p: (0, 0))
+    part = lambda w: pl.BlockSpec((1, tok, w), lambda p: (p, 0, 0))
+    return pl.pallas_call(
+        functools.partial(ff_rest_kernel, min(TILE, tok), units),
+        grid=(count,),
+        in_specs=[whole, whole, pl.BlockSpec((1, model, width), lambda p: (p, 0, 0))],
+        out_specs=[whole, whole, part(units), part(2 * units)],
+        out_shape=[
+            jax.ShapeDtypeStruct((tok, model), F32),
+            jax.ShapeDtypeStruct((tok, model), F32),
+            jax.ShapeDtypeStruct((count, tok, units), BF),
+            jax.ShapeDtypeStruct((count, tok, 2 * units), BF),
+        ],
+        compiler_params=pltpu.CompilerParams(vmem_limit_bytes=62 * 1024 * 1024),
+        cost_estimate=pl.CostEstimate(
+            flops=12 * tok * model * units * count,
+            bytes_accessed=count * model * width * 2 + 12 * tok * model,
+            transcendentals=0,
+        ),
+        name="feed_forward_rest",
+    )(second, grad_low, wall)
+
+
+def rest_grad_kernel(block, parts, hw, scalars, sec_ref, grad_ref, ml_ref, hid_ref, both_ref, *refs):
+    mixed_refs, (keep_ref, send_ref) = refs[:-2], refs[-2:]
+    model = sec_ref.shape[1]
+    weight_tiles(scalars[2], block, hw, sec_ref, grad_ref, hid_ref.at[0], both_ref.at[0], keep_ref, send_ref)
+    wanted = scalars[0] ^ (pl.program_id(0) % parts)
+    mixed = mixed_refs[0][0]
+    for r in range(1, parts):
+        mixed = jnp.where(wanted == r, mixed_refs[r][0], mixed)
+    step = min(256, model)
+    for k in range(model // step):
+        rows = slice(k * step // 2, (k + 1) * step // 2)
+        value = core_halves(scalars[2], block, dot_tn(ml_ref[:, k * step : (k + 1) * step], mixed))
+        keep_ref[0, rows, 0:hw] = value[0].astype(BF)
+        send_ref[0, rows, 0:hw] = value[1].astype(BF)
+
+
+def rest_grad(scalars, second, grad_low, middle_low, hidden, both, mixed_parts, width_out, parts, nsq, hw, block):
+    tok, model = second.shape
+    count, _, units = hidden.shape
+    whole = pl.BlockSpec((tok, model), lambda p, _: (0, 0))
+    part = lambda w: pl.BlockSpec((1, tok, w), lambda p, _: (p, 0, 0))
+    half = pl.BlockSpec((1, model // 2, width_out), lambda p, _: (p, 0, 0))
+    return pl.pallas_call(
+        functools.partial(rest_grad_kernel, block, parts, hw),
+        grid_spec=pltpu.PrefetchScalarGridSpec(
+            num_scalar_prefetch=1,
+            grid=(count,),
+            in_specs=[whole, whole, whole, part(units), part(2 * units)]
+            + [pl.BlockSpec((1, tok, hw), lambda p, _: (p // parts, 0, 0)) for _ in mixed_parts],
+            out_specs=[half, half],
+        ),
+        out_shape=[jax.ShapeDtypeStruct((count, model // 2, width_out), BF)] * 2,
+        compiler_params=pltpu.CompilerParams(vmem_limit_bytes=50 * 1024 * 1024),
+        cost_estimate=pl.CostEstimate(
+            flops=2 * tok * model * (3 * units + hw) * count,
+            bytes_accessed=count * model * width_out * 2 + 6 * tok * model,
+            transcendentals=0,
+        ),
+        name="rest_grad",
+    )(scalars, second, grad_low, middle_low, hidden, both, *mixed_parts)
 
 
 def split_kernel(parts, nsq, tok, scalars, *refs):
@@ -629,96 +715,99 @@
     )(scalars, middle, *mlps, *second_grads, grad_low, wall, gain)
 
 
-def out_grad_kernel(block, scalars, ml_ref, mixed_ref, _, __, keep_ref, send_ref):
-    model = ml_ref.shape[1]
-    step = min(256, model)
-    for k in range(model // step):
-        rows = slice(k * step // 2, (k + 1) * step // 2)
-        value = dot_tn(ml_ref[:, k * step : (k + 1) * step], mixed_ref[0])
-        value = core_halves(scalars[2], block, value)
-        keep_ref[0, rows, :] = value[0].astype(BF)
-        send_ref[0, rows, :] = value[1].astype(BF)
-
-
-def out_proj_grad(scalars, middle_low, mixed_part, halves, r, parts, nsq, hw, block):
-    tok, model = middle_low.shape
-    shape = halves[0].shape
-    half = pl.BlockSpec((1, model // 2, hw), lambda s, sc: (s * parts + (sc[0] ^ r), 0, 0))
-    return pl.pallas_call(
-        functools.partial(out_grad_kernel, block),
-        grid_spec=pltpu.PrefetchScalarGridSpec(
-            num_scalar_prefetch=1,
-            grid=(nsq,),
-            in_specs=[
-                pl.BlockSpec((tok, model), lambda s, _: (0, 0)),
-                pl.BlockSpec((1, tok, hw), lambda s, _: (s, 0, 0)),
-                pl.BlockSpec(memory_space=pl.ANY),
-                pl.BlockSpec(memory_space=pl.ANY),
-            ],
-            out_specs=[half, half],
-        ),
-        out_shape=[jax.ShapeDtypeStruct(shape, BF)] * 2,
-        input_output_aliases={3: 0, 4: 1},
-        compiler_params=pltpu.CompilerParams(vmem_limit_bytes=40 * 1024 * 1024),
-        cost_estimate=pl.CostEstimate(
-            flops=2 * tok * model * nsq * hw, bytes_accessed=2 * tok * model * 2, transcendentals=0
-        ),
-        name="out_proj_grad",
-    )(scalars, middle_low, mixed_part, *halves)
-
-
 def rounded(size):
     return size + -size % 128
 
 
 def unit_halves(units):
-    first = rounded(units * 7 // 10)
+    first = rounded((units + 1) // 2)
     return first, units - first
 
 
-def pack_kernel(lay, q_ref, k_ref, v_ref, r_ref, g_ref, out_ref, gate_ref, up_ref, down_ref, mix_ref, *all_refs):
+def turn(values):
+    return values.astype(F32).T.astype(BF)
+
+
+def pack_mix_kernel(lay, q_ref, k_ref, v_ref, r_ref, g_ref, mix_ref):
     mix_ref[:, lay.q : lay.k] = q_ref[...]
     mix_ref[:, lay.k : lay.v] = k_ref[...]
     mix_ref[:, lay.v : lay.g] = v_ref[...]
     mix_ref[:, lay.g : lay.r] = g_ref[...]
     mix_ref[:, lay.r : lay.width] = jnp.zeros((mix_ref.shape[0], 128), BF)
     mix_ref[:, lay.r : lay.r + r_ref.shape[1]] = r_ref[...]
-    hw, units = out_ref.shape[0], gate_ref.shape[1]
-    all_refs[0][:, 0:hw] = out_ref[...].astype(F32).T.astype(BF)
-    down = down_ref[...].astype(F32).T.astype(BF)
+
+
+def pack_mix(lay, w_query, w_key, w_value, w_rates, w_outgate):
+    return pl.pallas_call(
+        functools.partial(pack_mix_kernel, lay),
+        out_shape=jax.ShapeDtypeStruct((w_query.shape[0], lay.width), BF),
+        name="pack_mix",
+    )(w_query, w_key, w_value, w_rates, w_outgate)
+
+
+def pack_kernel(out_ref, gate_ref, up_ref, down_ref, *all_refs):
+    hw, units = out_ref.shape[0], gate_ref.shape[0]
+    all_refs[0][:, 0:hw] = turn(out_ref[...])
+    whole = [turn(ref[...]) for ref in (gate_ref, up_ref, down_ref)]
     start, lead = 0, hw
     for ref, size in zip(all_refs, unit_halves(units)):
-        cols = slice(start, start + size)
+        for k in range(3):
+            ref[:, lead + k * size : lead + (k + 1) * size] = whole[k][:, start : start + size]
         end = lead + 3 * size
-        ref[:, lead : lead + size] = gate_ref[:, cols]
-        ref[:, lead + size : lead + 2 * size] = up_ref[:, cols]
-        ref[:, lead + 2 * size : end] = down[:, cols]
         if end < ref.shape[1]:
             ref[:, end:] = jnp.zeros((ref.shape[0], ref.shape[1] - end), BF)
         start, lead = start + size, 0
 
 
-def pack(lay, w_query, w_key, w_value, w_rates, w_outgate, w_out, w_gate, w_up, w_down):
-    rows = w_query.shape[0]
-    one, two = unit_halves(w_gate.shape[1])
+def pack(w_out, w_gate, w_up, w_down):
+    rows = w_out.shape[1]
+    one, two = unit_halves(w_down.shape[0])
     return pl.pallas_call(
-        functools.partial(pack_kernel, lay),
+        pack_kernel,
         out_shape=[
-            jax.ShapeDtypeStruct((rows, lay.width), BF),
             jax.ShapeDtypeStruct((rows, rounded(w_out.shape[0] + 3 * one)), BF),
             jax.ShapeDtypeStruct((rows, rounded(3 * two)), BF),
         ],
         name="pack",
-    )(w_query, w_key, w_value, w_rates, w_outgate, w_out, w_gate, w_up, w_down)
+    )(w_out, w_gate.T, w_up.T, w_down)
+
+
+def project_kernel(x_ref, w_ref, *out_refs):
+    step = min(256, x_ref.shape[0])
+    for m in range(x_ref.shape[0] // step):
+        rows = slice(m * step, (m + 1) * step)
+        for s, out_ref in enumerate(out_refs):
+            out_ref[rows, :] = dot_nn(x_ref[rows, :], w_ref[s])
+
+
+def project(values, weights):
+    nsq, model, width = weights.shape
+    rows = values.shape[0]
+    tile = min(512, rows)
+    return pl.pallas_call(
+        project_kernel,
+        grid=(rows // tile,),
+        in_specs=[
+            pl.BlockSpec((tile, model), lambda i: (i, 0)),
+            pl.BlockSpec((nsq, model, width), lambda i: (0, 0, 0)),
+        ],
+        out_specs=[pl.BlockSpec((tile, width), lambda i: (i, 0))] * nsq,
+        out_shape=[jax.ShapeDtypeStruct((rows, width), F32)] * nsq,
+        compiler_params=pltpu.CompilerParams(vmem_limit_bytes=50 * 1024 * 1024),
+        cost_estimate=pl.CostEstimate(
+            flops=2 * rows * model * width * nsq, bytes_accessed=4 * rows * width * nsq, transcendentals=0
+        ),
+        name="project",
+    )(values, weights)
 
 
 def unpack_kernel(hw, one, two, a_ref, b_ref, out_ref, gate_ref, up_ref, down_ref):
     a, b = a_ref[...].astype(F32), b_ref[...].astype(F32)
     out_ref[...] = b[:, :hw].T
-    gate_ref[:, 0:one] = a[:, :one]
-    gate_ref[:, one:] = b[:, hw : hw + two]
-    up_ref[:, 0:one] = a[:, one : 2 * one]
-    up_ref[:, one:] = b[:, hw + two : hw + 2 * two]
+    gate_ref[0:one, :] = a[:, :one].T
+    gate_ref[one:, :] = b[:, hw : hw + two].T
+    up_ref[0:one, :] = a[:, one : 2 * one].T
+    up_ref[one:, :] = b[:, hw + two : hw + 2 * two].T
     down_ref[0:one, :] = a[:, 2 * one : 3 * one].T
     down_ref[one:, :] = b[:, hw + 2 * two : hw + 3 * two].T
 
@@ -726,12 +815,13 @@
 def unpack(own_a, own_b, hw, units):
     one, two = unit_halves(units)
     rows = own_a.shape[0]
-    shapes = [(hw, rows), (rows, units), (rows, units), (units, rows)]
-    return pl.pallas_call(
+    shapes = [(hw, rows), (units, rows), (units, rows), (units, rows)]
+    out, gate, up, down = pl.pallas_call(
         functools.partial(unpack_kernel, hw, one, two),
         out_shape=[jax.ShapeDtypeStruct(shape, F32) for shape in shapes],
         name="unpack",
     )(own_a, own_b)
+    return out, gate.T, up.T, down
 
 
 def unpack_mix_kernel(lay, nrates, own_ref, q_ref, k_ref, v_ref, r_ref, g_ref):
@@ -776,6 +866,14 @@
 
 def plus(left, right):
     return (left.astype(F32) + right.astype(F32)).astype(BF)
+
+
+def column_step(values, k):
+    rows, width = values.shape
+    mine = (lax.axis_index("dz") >> k) & 1
+    blocks = values.reshape(-1, 2, rows // (lax.axis_size("dz") >> k), width)
+    part = lambda i: lax.dynamic_index_in_dim(blocks, i, 1, keepdims=False).reshape(-1, width)
+    return plus(part(mine), trade(part(1 - mine), "dz", 1 << k))
 
 
 def swap(values, which, parts):
@@ -796,9 +894,8 @@
     hw = heads * HEAD
     place_arr = place.astype(jnp.int32).reshape(1)
 
-    mix_shard, *ff_shards = pack(
-        lay, w_query, w_key, w_value, w_rates, w_outgate, w_out, w_gate, w_up, w_down
-    )
+    mix_shard = pack_mix(lay, w_query, w_key, w_value, w_rates, w_outgate)
+    ff_shards = pack(w_out, w_gate, w_up, w_down)
     w_mix = lax.all_gather(mix_shard, ("sq", "dz", "core"), axis=0, tiled=True)
     w_mix = w_mix.reshape(nsq, model, lay.width)
     walls = [
@@ -812,7 +909,7 @@
     first = (normed_one * ln1_gain).astype(BF)
     first_seq = jnp.concatenate([first] + [swap(first, r, parts) for r in range(1, parts)], axis=0)
 
-    pre = [dot_nn(first_seq, w_mix[s]) for s in range(nsq)]
+    pre = project(first_seq, w_mix)
     hpos = [(s * parts + place) * heads for s in range(nsq)]
     lanes = np.stack([8 * (c * nsq + s) + 3 * np.arange(heads) + 2 for c in range(STEP) for s in range(nsq)])
 
@@ -839,40 +936,33 @@
     def plane(values):
         return lax.psum_scatter(values, ("sq", "sub"), scatter_dimension=0, tiled=True)
 
-    def column(values):
-        return lax.psum_scatter(values, "dz", scatter_dimension=0, tiled=True)
-
     mlp_a, sg_a, *grads_a = feed_forward(
-        scalars, second, grad_low, walls[0], hw, 0, rounded(3 * one), one, block
+        scalars, second, grad_low, walls[0], hw, rounded(3 * one), one, block
     )
     grads_a, wall_b = lax.optimization_barrier((chips(grads_a), walls[1]))
     grads_a = plane(grads_a)
-    mlp_b, sg_b, *grads_b = feed_forward(
-        scalars, second, grad_low, wall_b, 0, hw, hw + rounded(3 * two), two, block
-    )
+    mlp_b, sg_b, *acts_b = feed_forward_rest(second, grad_low, wall_b, two)
     block_out, middle_grad, middle_low, ln2_grad, *back = split(
         scalars, middle, (mlp_a, mlp_b), (sg_a, sg_b), grad_low, walls[0],
         ln2_gain.reshape(1, model), parts, nsq, hw,
     )
-    for r in range(parts):
-        grads_b = out_proj_grad(scalars, middle_low, got[r], grads_b, r, parts, nsq, hw, block)
-
-    dmixed = jnp.concatenate([back[0]] + [swap(back[r], r, parts) for r in range(1, parts)], axis=1)
-    dmixed, grads_b, grads_a = lax.optimization_barrier((dmixed, chips(grads_b), grads_a))
-    own_a = column(grads_a)
+    arrived = [swap(back[r], r, parts) for r in range(1, parts)]
+    grads_b = rest_grad(
+        scalars, second, grad_low, middle_low, *acts_b, got, hw + rounded(3 * two), parts, nsq, hw, block
+    )
+    arrived, grads_b = lax.optimization_barrier((arrived, grads_b))
+    dmixed = jnp.concatenate([back[0], *arrived], axis=1)
+    dmixed, grads_b = lax.optimization_barrier((dmixed, chips(grads_b)))
     grads_b = plane(grads_b)
-    chains = nsq * heads
-    dpre = (jnp.zeros((chains, HEAD, HEAD), F32), jnp.zeros((8, 128), F32))
-    for at in range(parts):
-        *dpre, carry, small = mixer_backward(
-            place_arr, parts, pre, params, gain, *kept, dmixed, heads, STEP, at, dpre
-        )
-        if at == 0:
-            carry, grads_b = lax.optimization_barrier((carry, grads_b))
-            own_b = column(grads_b)
-        if at < parts - 1:
-            dpre = (carry, small, *dpre)
-    own_out, own_gate, own_up, own_down = unpack(own_a, own_b, hw, units)
+    steps = dmixed.shape[1] // CT // STEP
+    head_steps = steps * 3 // 4
+    dpre = (jnp.zeros((nsq * heads, HEAD, HEAD), F32), jnp.zeros((8, 128), F32))
+    back_args = (place_arr, parts, pre, params, gain, *kept, dmixed, heads, STEP)
+    *dpre, carry, small = mixer_backward(*back_args, 0, head_steps, dpre)
+    carry, grads_b, grads_a = lax.optimization_barrier((carry, grads_b, grads_a))
+    own_a = lax.psum_scatter(grads_a, "dz", scatter_dimension=0, tiled=True)
+    grads_b = column_step(grads_b, 0)
+    *dpre, carry, small = mixer_backward(*back_args, head_steps, steps - head_steps, (carry, small, *dpre))
 
     def back_rows(values, r):
         rows = slice(r * tok_dev, (r + 1) * tok_dev)
@@ -882,7 +972,11 @@
         return total, jnp.sum(total * first_seq[rows].astype(F32), axis=0)
 
     mix_grads = jnp.concatenate([dot_tn(first_seq, dpre[s]).astype(BF) for s in range(nsq)], axis=0)
-    dpre, mix_grads = lax.optimization_barrier((dpre, mix_grads))
+    dpre, mix_grads, grads_b = lax.optimization_barrier((dpre, mix_grads, grads_b))
+    own_b = grads_b
+    for k in range(1, len(bits("dz"))):
+        own_b = column_step(own_b, k)
+    own_out, own_gate, own_up, own_down = unpack(own_a, own_b, hw, units)
     mix_own = lax.psum_scatter(mix_grads, ("sq", "dz", "core"), scatter_dimension=0, tiled=True)
     leaving = [back_rows(dpre, r) for r in range(1, parts)]
     arriving = [swap(leaving[r - 1][0].astype(BF), r, parts) for r in range(1, parts)]

time: 596 us -> 580 us (0.973)
  waiting for transfers between devices: 181 us -> 149 us
  Pallas kernels: 244 us -> 275 us
  matrix products: 75.3 us -> 52.5 us
  other arithmetic: 30.6 us -> 37.7 us
    pallas_call x3 -> x5, Pallas kernels: 6.97 us -> 77.1 us  [the longest x1 31.9 us: feed_forward_rest(): pl.pallas_call(functools.partial(ff_rest_kernel, min(TILE, tok), units),...]
    pallas_call x2 -> x1, Pallas kernels: 78.4 us -> 39.8 us  [feed_forward(): pl.pallas_call(functools.partial(ff_kernel, min(TILE, tok), block, lead,...]
    ppermute x4, waiting for transfers between devices: 111 us -> 73.9 us  [swap(): return lax.ppermute(values, 'sub', [(i, i ^ which) for i in range(parts)])]
    dot_general x2 -> x0, matrix products: 27.3 us -> none  [dot_nn(): return jnp.dot(left, right, preferred_element_type=F32)]
    ppermute x7 -> x9, waiting for transfers between devices: 42 us -> 52.2 us  [trade(): lax.ppermute(values, axis, [(i, i ^ bit) for i in range(lax.axis_size(axi...]
    all_gather x1, waiting for transfers between devices: 13.6 us -> 6.88 us  [per_device(): w_mix = lax.all_gather(mix_shard, ('sq', 'dz', 'core'), axis=0, tiled=True)]
    all_gather x2, waiting for transfers between devices: 0.01 us -> 6.2 us  [per_device(): lax.all_gather(shard, ('sq', 'sub', 'dz', 'core'), axis=0, tiled=True)]
    unnamed x70 -> x62, local copies, waits for them, and re-layouts: 20.2 us -> 15.7 us
  transfers between devices with their start and end apart: 19 -> 20, of which waited for: 12 -> 15; matrix products, arithmetic and copies ran while one was open for 20% -> 18% of each run, Pallas kernels for 41% -> 48%
where the time goes in v4:
time: 580 us; the launch traced here: 571 us
  Pallas kernels  275 us (47%)
  waiting for transfers between devices  149 us (26%)
  matrix products  52.5 us (9%)
  other arithmetic  37.7 us (7%)
  local copies, waits for them, and re-layouts  28.1 us (5%)
  between operations  14.9 us (3%)
  starting transfers between devices  13.3 us (2%)
    pallas_call x2, Pallas kernels, mixer_backward(): pl.pallas_call(functools.partial(backward_kernel, lay, nsq, heads, nb), g...  82.2 us
    ppermute x4, waiting for transfers between devices, swap(): return lax.ppermute(values, 'sub', [(i, i ^ which) for i in range(parts)])  73.9 us
    ppermute x9, waiting for transfers between devices, trade(): lax.ppermute(values, axis, [(i, i ^ bit) for i in range(lax.axis_size(axi...  52.2 us
    pallas_call x1, Pallas kernels, mixer_forward(): pl.pallas_call(functools.partial(forward_kernel, lay, nsq, heads, nb), gr...  51.4 us
    pallas_call x1, Pallas kernels, feed_forward(): pl.pallas_call(functools.partial(ff_kernel, min(TILE, tok), block, lead,...  39.8 us
    pallas_call x1, Pallas kernels, feed_forward_rest(): pl.pallas_call(functools.partial(ff_rest_kernel, min(TILE, tok), units),...  31.9 us
    dot_general x4, matrix products, dot_nt(): lax.dot_general(left, right, (((1,), (1,)), ((), ())), preferred_element_...  30.6 us
    dot_general x2, matrix products, dot_tn(): lax.dot_general(left, right, (((0,), (0,)), ((), ())), preferred_element_...  21.9 us
  transfers between devices with their start and end apart: 20, of which 15 were waited for; matrix products, arithmetic and copies ran while one was open for 18% of the time, Pallas kernels for 48%

profile of v4, /device:TPU:0, one launch (start us, length us, event | category | flops | bytes accessed | tf_op | source)
XLA Modules:
  0.0 571.1 jit_solution(16846968682190247803)
XLA Ops:
  8.8 1.8 pack_mix.1
  10.7 2.2 pack.1
  13.7 2.1 fusion.9
  16.4 1.9 fusion.3
  18.2 2.9 collective-permute-start
  23.7 43.4 %collective-permute-done = bf16[1024,1024]{1,0:T(8,128)(2,1)} collective-permute-done((bf16[1024,1024]{1,0:T(8,128)(2,1)}, bf16[1024,1024]{1,0:T(8,128)(2,1)}, u32[]{:S(2)}, u32[]{:S(2)}) %collective-permute-start) | collective-permute-done | bytes 2097184 | tf_op jit(solution)/shard_map/ppermute | solution.py:880
  67.1 4.6 pad_maximum_fusion.1.x_ref
  71.8 6.9 %all-gather.4.cloned.1.call-done = bf16[2048,1664]{1,0:T(8,128)(2,1)} async-done(((bf16[128,1664]{1,0:T(8,128)(2,1)}), bf16[2048,1664]{1,0:T(8,128)(2,1)}) %all-gather.4.cloned.1.call-update) | async-done | bytes 6815760 | tf_op jit(solution)/shard_map/all_gather | solution.py:899
  78.6 21.1 %project.1 = (f32[2048,1664]{1,0:T(8,128)}, f32[2048,1664]{1,0:T(8,128)}) custom-call(bf16[2048,1024]{1,0:T(8,128)(2,1)} %pad_maximum_fusion.1.x_ref, bf16[2,1024,1664]{2,1,0:T(8,128)(2,1)} %bitcast.81), custom_call_target="tpu_custom_call" | custom-call | flops 13958643712 | bytes 27262976 | tf_op jit(solution)/shard_map/project/pallas_call | solution.py:787
  99.8 51.4 %mixer_forward.1 = (bf16[2,2048,256]{2,1,0:T(8,128)(2,1)}, bf16[32,4,128,128]{3,2,1,0:T(8,128)(2,1)}, bf16[32,4,128,128]{3,2,1,0:T(8,128)(2,1)}, bf16[32,4,128,1...) custom-call(s32[1]{0:T(128)} %bitcast._, f32[2048,1664]{1,0:T(8,128)} %get-tuple-element.77.refs_0_, ...), custom_call_target="tpu_custom_call" | custom-call | flops 10737418240 | bytes 46137344 | tf_op jit(solution)/shard_map/mixer_forward/pallas_call | solution.py:370
  151.1 2.3 slice.61
  156.2 22.7 %collective-permute-done.1.refs_1_ = bf16[2,1024,256]{2,1,0:T(8,128)(2,1)S(1)} collective-permute-done((bf16[2,1024,256]{2,1,0:T(8,128)(2,1)}, bf16[2,1024,256]{2,1,0:T(8,128)(2,1)S(1)}, u32[]{:S(2)}, u32[]{:S(2)}) %collective-permute-start.1) | collective-permute-done | bytes 1048608 | tf_op jit(solution)/shard_map/ppermute | solution.py:880
  179.0 1.6 copy-done.2
  180.6 1.6 copy-done.5
  182.1 7.5 %join.1 = (f32[1024,1024]{1,0:T(8,128)}, bf16[1024,1024]{1,0:T(8,128)(2,1)S(1)}, bf16[1024,1024]{1,0:T(8,128)(2,1)S(1)}) custom-call(s32[3]{0:T(128)S(1)} %pad_add_fusion.scalars, bf16[2,2048,256]{2,1,0:T(8,128)(2,1)S(1)} %copy-done.2, bf16[2,1024,256]{2,1,0:T(8,128)(2,1)S(1)} %collective-permute-done.1.refs_1_, bf16[1024,1024]{1,0:T(8,128)(2,1)S(1)} %copy-done, ...), custom_call_target="tpu_custom_call" | custom-call | flops 2147483648 | bytes 14680064 | tf_op jit(solution)/shard_map/join/pallas_call | solution.py:472
  192.3 39.8 %feed_forward.1 = (f32[1024,1024]{1,0:T(8,128)}, f32[1024,1024]{1,0:T(8,128)}, bf16[4,512,1152]{2,1,0:T(8,128)(2,1)}, bf16[4,512,1152]{2,1,0:T(8,128)(2,1)}) custom-call(s32[3]{0:T(128)} %copy-done.9, bf16[1024,1024]{1,0:T(8,128)(2,1)} %copy-done.11, bf16[1024,1024]{1,0:T(8,128)(2,1)} %copy-done.6, bf16[4,1024,1408]{2,1,0:T(8,128)(2,1)} %bitcast.62), custom_call_target="tpu_custom_call" | custom-call | flops 28991029248 | bytes 35651584 | tf_op jit(solution)/shard_map/feed_forward/pallas_call | solution.py:558
  232.2 8.2 %collective-permute-done.2 = bf16[4,512,1152]{2,1,0:T(8,128)(2,1)S(1)} collective-permute-done((bf16[4,512,1152]{2,1,0:T(8,128)(2,1)}, bf16[4,512,1152]{2,1,0:T(8,128)(2,1)S(1)}, u32[]{:S(2)}, u32[]{:S(2)}) %collective-permute-start.2) | collective-permute-done | bytes 4718624 | tf_op jit(solution)/shard_map/ppermute | solution.py:857
  240.4 6.0 %add_convert_fusion.1 = bf16[4,512,1152]{2,1,0:T(8,128)(2,1)} fusion(bf16[4,512,1152]{2,1,0:T(8,128)(2,1)S(1)} %collective-permute-done.2, bf16[4,512,1152]{2,1,0:T(8,128)(2,1)} %get-tuple-element.85), kind=kLoop, calls=%fused_computation.5 | loop fusion | flops 9437184 | bytes 14155776 | tf_op jit(solution)/shard_map/convert_element_type | solution.py:868
  246.4 6.2 %all-gather.8.cloned.1.call-done = bf16[4096,1024]{1,0:T(8,128)(2,1)} async-done(((bf16[128,1024]{1,0:T(8,128)(2,1)}), bf16[4096,1024]{1,0:T(8,128)(2,1)}) %all-gather.8.cloned.1.call-update) | async-done | bytes 8388624 | tf_op jit(solution)/shard_map/all_gather | solution.py:902
  252.7 31.9 %feed_forward_rest.1 = (f32[1024,1024]{1,0:T(8,128)}, f32[1024,1024]{1,0:T(8,128)}, bf16[4,1024,320]{2,1,0:T(8,128)(2,1)}, bf16[4,1024,640]{2,1,0:T(8,128)(2,1)}) custom-call(bf16[1024,1024]{1,0:T(8,128)(2,1)} %copy-done.11, bf16[1024,1024]{1,0:T(8,128)(2,1)} %copy-done.6, bf16[4,1024,1024]{2,1,0:T(8,128)(2,1)} %bitcast.80), custom_call_target="tpu_custom_call" | custom-call | flops 16106127360 | bytes 20971520 | tf_op jit(solution)/shard_map/feed_forward_rest/pallas_call | solution.py:596
  284.6 1.6 copy-done.7
  286.1 13.1 %split.1 = (bf16[1024,1024]{1,0:T(8,128)(2,1)}, f32[1024,1024]{1,0:T(8,128)S(1)}, bf16[1024,1024]{1,0:T(8,128)(2,1)S(1)}, f32[1,1024]{1,0:T(1,128)S(1)}, bf16[2,...) custom-call(s32[3]{0:T(128)S(1)} %copy-done.10, f32[1024,1024]{1,0:T(8,128)} %get-tuple-element.81.refs_0_, ...), custom_call_target="tpu_custom_call" | custom-call | flops 2147483648 | bytes 27262976 | tf_op jit(solution)/shard_map/split/pallas_call | solution.py:694
  299.3 2.1 copy-done.3
  304.1 20.1 %rest_grad.1 = (bf16[4,512,1280]{2,1,0:T(8,128)(2,1)}, bf16[4,512,1280]{2,1,0:T(8,128)(2,1)}) custom-call(s32[3]{0:T(128)S(1)} %copy-done.10, bf16[1024,1024]{1,0:T(8,128)(2,1)S(1)} %copy-done.12, bf16[1024,1024]{1,0:T(8,128)(2,1)} %copy-done.6, bf16[1024,1024]{1,0:T(8,128)(2,1)} %copy-done.13, bf16[4,1024,320]{2,1,0:T(8,128)(2,1)} %get-tuple-element.102.hid_ref, ...), custom_call_target="tpu_custom_call" | custom-call | flops 10200547328 | bytes 16777216 | tf_op jit(solution)/shard_map/rest_grad/pallas_call | solution.py:639
  324.2 7.8 %collective-permute-done.3 = bf16[2,1024,256]{2,1,0:T(8,128)(2,1)S(1)} collective-permute-done((bf16[2,1024,256]{2,1,0:T(8,128)(2,1)S(1)}, bf16[2,1024,256]{2,1,0:T(8,128)(2,1)S(1)}, u32[]{:S(2)}, u32[]{:S(2)}) %collective-permute-start.3) | collective-permute-done | bytes 1048608 | tf_op jit(solution)/shard_map/ppermute | solution.py:880
  333.4 7.4 %collective-permute-done.4 = bf16[4,512,1280]{2,1,0:T(8,128)(2,1)S(1)} collective-permute-done((bf16[4,512,1280]{2,1,0:T(8,128)(2,1)}, bf16[4,512,1280]{2,1,0:T(8,128)(2,1)S(1)}, u32[]{:S(2)}, u32[]{:S(2)}) %collective-permute-start.4) | collective-permute-done | bytes 5242912 | tf_op jit(solution)/shard_map/ppermute | solution.py:857
  340.9 6.0 %add_convert_fusion = bf16[4,512,1280]{2,1,0:T(8,128)(2,1)} fusion(bf16[4,512,1280]{2,1,0:T(8,128)(2,1)S(1)} %collective-permute-done.4, bf16[4,512,1280]{2,1,0:T(8,128)(2,1)} %get-tuple-element.107), kind=kLoop, calls=%fused_computation.4 | loop fusion | flops 10485760 | bytes 15728640 | tf_op jit(solution)/shard_map/convert_element_type | solution.py:868
  348.3 59.4 %mixer_backward.2 = (bf16[2048,1664]{1,0:T(8,128)(2,1)}, bf16[2048,1664]{1,0:T(8,128)(2,1)}, f32[4,128,128]{2,1,0:T(8,128)}, f32[8,128]{1,0:T(8,128)}) custom-call(s32[1]{0:T(128)} %bitcast._, f32[2048,1664]{1,0:T(8,128)} %get-tuple-element.77.refs_0_, f32[2048,1664]{1,0:T(8,128)} %get-tuple-element.78.refs_1_, f32[2,128]{1,0:T(2,128)} %pad_maximum_fusion.5.refs_2_, ...), custom_call_target="tpu_custom_call" | custom-call | flops 10468982784 | bytes 47972352 | tf_op jit(solution)/shard_map/mixer_backward/pallas_call | solution.py:415
  408.6 2.4 constant_dynamic-slice_fusion.1
  412.5 22.8 %mixer_backward.3 = (bf16[2048,1664]{1,0:T(8,128)(2,1)}, bf16[2048,1664]{1,0:T(8,128)(2,1)}, f32[4,128,128]{2,1,0:T(8,128)}, f32[8,128]{1,0:T(8,128)}) custom-call(s32[1]{0:T(128)} %bitcast._, f32[2048,1664]{1,0:T(8,128)} %get-tuple-element.77.refs_0_, f32[2048,1664]{1,0:T(8,128)} %get-tuple-element.78.refs_1_, ...), custom_call_target="tpu_custom_call", output_to_operand_aliasing={{0}: (16, {}), {1}: (17, {})} | custom-call | flops 3489660928 | bytes 15990784 | tf_op jit(solution)/shard_map/mixer_backward/pallas_call | solution.py:415
  435.3 11.8 %convolution_convert_fusion.1 = bf16[1024,1664]{1,0:T(8,128)(2,1)S(1)} fusion(bf16[2048,1664]{1,0:T(8,128)(2,1)} %get-tuple-element.120, bf16[1024,1024]{1,0:T(8,128)(2,1)} %collective-permute-done, bf16[1024,1024]{1,0:T(8,128)(2,1)} %fusion.3), kind=kOutput, calls=%fused_computation.24 | convolution fusion | flops 6989414400 | bytes 14417920 | tf_op jit(solution)/shard_map/dot_general | solution.py:30
  447.1 10.0 %convolution_convert_fusion = bf16[1024,1664]{1,0:T(8,128)(2,1)S(1)} fusion(bf16[2048,1664]{1,0:T(8,128)(2,1)S(1)} %copy-done.15, bf16[1024,1024]{1,0:T(8,128)(2,1)} %collective-permute-done, bf16[1024,1024]{1,0:T(8,128)(2,1)} %fusion.3), kind=kOutput, calls=%fused_computation.23 | convolution fusion | flops 6989414400 | bytes 14417920 | tf_op jit(solution)/shard_map/dot_general | solution.py:30
  457.1 3.3 pad_maximum_fusion
  464.7 7.4 %fusion.10 = f32[1024,1024]{1,0:T(8,128)S(1)} fusion(bf16[2048,1664]{1,0:T(8,128)(2,1)} %get-tuple-element.121, bf16[2048,1664]{1,0:T(8,128)(2,1)} %all-gather.4.cloned.1.call-done), kind=kOutput, calls=%fused_computation.25 | convolution fusion | flops 3489660928 | bytes 11010048 | tf_op jit(solution)/shard_map/dot_general | solution.py:26
  472.1 9.8 %fusion.39 = (bf16[1024,1024]{1,0:T(8,128)(2,1)}, f32[1024]{0:T(1024)S(1)}) fusion(bf16[1024,1024]{1,0:T(8,128)(2,1)} %collective-permute-done, f32[1024,1024]{1,0:T(8,128)S(1)} %fusion.10, bf16[2048,1664]{1,0:T(8,128)(2,1)} %all-gather.4.cloned.1.call-done, bf16[2048,1664]{1,0:T(8,128)(2,1)} %get-tuple-element.120), kind=kOutput, calls=%fused_computation.73 | convolution fusion | flops 3494902784 | bytes 15208448 | tf_op jit(solution)/shard_map/dot_general | solution.py:26
  483.2 5.8 %fusion.14 = f32[1024,1024]{1,0:T(8,128)} fusion(bf16[2048,1664]{1,0:T(8,128)(2,1)S(1)} %bitcast.69, bf16[2048,1664]{1,0:T(8,128)(2,1)S(1)} %bitcast.83), kind=kOutput, calls=%fused_computation.29 | convolution fusion | flops 3489660928 | bytes 11010048 | tf_op jit(solution)/shard_map/dot_general | solution.py:26
  489.1 7.6 %multiply_reduce_fusion.1 = (f32[1024]{0:T(1024)S(1)}, f32[1024,1024]{1,0:T(8,128)}) fusion(bf16[1024,1024]{1,0:T(8,128)(2,1)} %fusion.3, f32[1024,1024]{1,0:T(8,128)} %fusion.14, bf16[2048,1664]{1,0:T(8,128)(2,1)S(1)} %bitcast.83, bf16[2048,1664]{1,0:T(8,128)(2,1)S(1)} %bitcast.67), kind=kOutput, calls=%fused_computation.22 | convolution fusion | flops 3493854208 | bytes 17305600 | tf_op jit(solution)/shard_map/dot_general | solution.py:26
  498.3 4.8 collective-permute-done.8
  504.3 3.4 collective-permute-done.9
  508.4 3.2 collective-permute-done.10
  512.2 1.6 collective-permute-start.12
  513.8 15.7 %collective-permute-done.11 = f32[2192]{0:T(1024)S(1)} collective-permute-done((f32[2192]{0:T(1024)S(1)}, f32[2192]{0:T(1024)S(1)}, u32[]{:S(2)}, u32[]{:S(2)}) %collective-permute-start.11) | collective-permute-done | bytes 8800 | tf_op jit(solution)/shard_map/ppermute | solution.py:857
  531.2 8.3 %collective-permute-done.12 = bf16[128,1280]{1,0:T(8,128)(2,1)S(1)} collective-permute-done((bf16[128,1280]{1,0:T(8,128)(2,1)S(1)}, bf16[128,1280]{1,0:T(8,128)(2,1)S(1)}, u32[]{:S(2)}, u32[]{:S(2)}) %collective-permute-start.12) | collective-permute-done | bytes 327712 | tf_op jit(solution)/shard_map/ppermute | solution.py:857
  540.3 2.2 unpack.1
  542.5 4.2 fusion.4
  547.9 3.9 fusion.8
  551.8 8.5 %reduce-scatter.9.cloned.1.call-done.own_ref = bf16[128,1664]{1,0:T(8,128)(2,1)} async-done(((bf16[2048,1664]{1,0:T(8,128)(2,1)}), bf16[128,1664]{1,0:T(8,128)(2,1)}) %reduce-scatter.9.cloned.1.call-update) | async-done | bytes 426000 | tf_op jit(solution)/shard_map/reduce_scatter | solution.py:980
  560.4 1.9 unpack_mix.1
  (140 shorter events, 33.8 us)
Async XLA Ops:
  7.2 9.2 %copy-start = (bf16[1024,1024]{1,0:T(8,128)(2,1)S(1)}, bf16[1024,1024]{1,0:T(8,128)(2,1)}, u32[]{:S(2)}) copy-start(bf16[1024,1024]{1,0:T(8,128)(2,1)} %refs_2_.1) | copy-start | bytes 6291460
  7.2 9.2 %copy-start.18 = (f32[1024]{0:T(1024)S(1)}, f32[1024]{0:T(1024)}, u32[]{:S(2)}) copy-start(f32[1024]{0:T(1024)} %param.36) | copy-start | bytes 12292
  7.2 71.4 %all-gather.4.cloned.1.call-start = ((), (), s32[]{:S(2)}) async-start(), calls=%async_computation.4 | async-start | bytes 7241728 | tf_op jit(solution)/shard_map/all_gather | solution.py:899
  10.6 10.6 %copy-start.22 = (f32[8]{0:T(128)S(1)}, f32[8]{0:T(128)}, u32[]{:S(2)}) copy-start(f32[8]{0:T(128)} %param.39) | copy-start | bytes 100
  10.6 10.6 %copy-start.20 = (f32[8]{0:T(128)S(1)}, f32[8]{0:T(128)}, u32[]{:S(2)}) copy-start(f32[8]{0:T(128)} %param.40) | copy-start | bytes 100
  10.6 168.3 %all-gather.6.cloned.1.call-start = ((), (), s32[]{:S(2)}) async-start(), calls=%async_computation.5 | async-start | bytes 11894784 | tf_op jit(solution)/shard_map/all_gather | solution.py:902
  12.9 239.7 %all-gather.8.cloned.1.call-start = ((), (), s32[]{:S(2)}) async-start(), calls=%async_computation.6 | async-start | bytes 8650752 | tf_op jit(solution)/shard_map/all_gather | solution.py:902
  13.6 394.0 %reduce-scatter.7.cloned.1.call-start = ((), (), s32[]{:S(2)}) async-start(), calls=%async_computation.8 | async-start | bytes 5898240 | tf_op jit(solution)/shard_map/reduce_scatter | solution.py:937
  18.2 48.9 %collective-permute-start = (bf16[1024,1024]{1,0:T(8,128)(2,1)}, bf16[1024,1024]{1,0:T(8,128)(2,1)}, u32[]{:S(2)}, u32[]{:S(2)}) collective-permute-start(bf16[1024,1024]{1,0:T(8,128)(2,1)} %fusion.3), channel_id=1, source_target_pairs={{0,1},{1,0},{2,3},{3,2},{4,5},{5,4},{6,7},{7,6},{8,9},{9,8},{10,11... | collective-permute-start | bytes 6291464 | tf_op jit(solution)/shard_map/ppermute | solution.py:880
  99.8 55.1 %copy-start.23 = (s32[2]{0:T(128)S(1)}, s32[2]{0:T(128)}, u32[]{:S(2)}) copy-start(s32[2]{0:T(128)} %param.34) | copy-start | bytes 28
  99.8 79.2 %copy-start.8 = (f32[1024]{0:T(1024)S(1)}, f32[1024]{0:T(1024)}, u32[]{:S(2)}) copy-start(f32[1024]{0:T(1024)} %param.37) | copy-start | bytes 12292
  153.4 25.5 %collective-permute-start.1 = (bf16[2,1024,256]{2,1,0:T(8,128)(2,1)}, bf16[2,1024,256]{2,1,0:T(8,128)(2,1)S(1)}, u32[]{:S(2)}, u32[]{:S(2)}) collective-permute-start(bf16[2,1024,256]{2,1,0:T(8,128)(2,1)} %slice.61), channel_id=1, source_target_pairs={{0,1},{1,0},{2,3},{3,2},{4,5},{5,4},{6,7},{7,6},{8,9},{9,8},{10,11... | collective-permute-start | bytes 3145736 | tf_op jit(solution)/shard_map/ppermute | solution.py:880
  156.2 33.4 %copy-start.9 = (s32[3]{0:T(128)}, s32[3]{0:T(128)S(1)}, u32[]{:S(2)}) copy-start(s32[3]{0:T(128)S(1)} %pad_add_fusion.scalars) | copy-start | bytes 40
  179.0 1.6 copy-start.2
  180.6 1.6 copy-start.5
  189.7 1.3 copy-start.6
  191.0 1.3 copy-start.11
  232.2 8.2 %collective-permute-start.2 = (bf16[4,512,1152]{2,1,0:T(8,128)(2,1)}, bf16[4,512,1152]{2,1,0:T(8,128)(2,1)S(1)}, u32[]{:S(2)}, u32[]{:S(2)}) collective-permute-start(bf16[4,512,1152]{2,1,0:T(8,128)(2,1)} %get-tuple-element.86), channel_id=1, source_target_pairs={{0,4},{4,0},{1,5},{5,1},{2,6},{6,2},{3,7},{7,3},{8,12},{12,8},{9,1... | collective-permute-start | bytes 14155784 | tf_op jit(solution)/shard_map/ppermute | solution.py:857
  252.6 31.9 %copy-start.10 = (s32[3]{0:T(128)S(1)}, s32[3]{0:T(128)}, u32[]{:S(2)}) copy-start(s32[3]{0:T(128)} %copy-done.9) | copy-start | bytes 40
  252.6 155.9 %reduce-scatter.5.cloned.1.call-start = ((), (), s32[]{:S(2)}) async-start(), calls=%async_computation.7 | async-start | bytes 6553600 | tf_op jit(solution)/shard_map/reduce_scatter | solution.py:937
  284.6 1.6 copy-start.7
  286.1 17.9 %copy-start.12 = (bf16[1024,1024]{1,0:T(8,128)(2,1)S(1)}, bf16[1024,1024]{1,0:T(8,128)(2,1)}, u32[]{:S(2)}) copy-start(bf16[1024,1024]{1,0:T(8,128)(2,1)} %copy-done.11) | copy-start | bytes 6291460
  299.3 2.1 copy-start.3
  302.7 29.3 %collective-permute-start.3 = (bf16[2,1024,256]{2,1,0:T(8,128)(2,1)S(1)}, bf16[2,1024,256]{2,1,0:T(8,128)(2,1)S(1)}, u32[]{:S(2)}, u32[]{:S(2)}) collective-permute-start(bf16[2,1024,256]{2,1,0:T(8,128)(2,1)S(1)} %get-tuple-element.100), channel_id=1, source_target_pairs={{0,1},{1,0},{2,3},{3,2},{4,5},{5,4},{6,7},{7,6},{8,9},{9,8},{10,11... | collective-permute-start | bytes 3145736 | tf_op jit(solution)/shard_map/ppermute | solution.py:880
  332.0 8.9 %collective-permute-start.4 = (bf16[4,512,1280]{2,1,0:T(8,128)(2,1)}, bf16[4,512,1280]{2,1,0:T(8,128)(2,1)S(1)}, u32[]{:S(2)}, u32[]{:S(2)}) collective-permute-start(bf16[4,512,1280]{2,1,0:T(8,128)(2,1)} %get-tuple-element.108), channel_id=1, source_target_pairs={{0,4},{4,0},{1,5},{5,1},{2,6},{6,2},{3,7},{7,3},{8,12},{12,8},{9,1... | collective-permute-start | bytes 15728648 | tf_op jit(solution)/shard_map/ppermute | solution.py:857
  346.9 193.4 %reduce-scatter.11.cloned.1.call-start = ((), (), s32[]{:S(2)}) async-start(), calls=%async_computation.10 | async-start | bytes 1474560 | tf_op jit(solution)/shard_map/reduce_scatter | solution.py:963
  408.5 151.9 %reduce-scatter.9.cloned.1.call-start = ((), (), s32[]{:S(2)}) async-start(), calls=%async_computation.9 | async-start | bytes 7241728 | tf_op jit(solution)/shard_map/reduce_scatter | solution.py:980
  411.0 49.4 %collective-permute-start.5 = (bf16[256,1280]{1,0:T(8,128)(2,1)}, bf16[256,1280]{1,0:T(8,128)(2,1)}, u32[]{:S(2)}, u32[]{:S(2)}) collective-permute-start(bf16[256,1280]{1,0:T(8,128)(2,1)} %bitcast.20), channel_id=1, source_target_pairs={{0,8},{8,0},{16,24},{24,16},{1,9},{9,1},{17,25},{25,17},{2,10},{10... | collective-permute-start | bytes 1966088 | tf_op jit(solution)/shard_map/ppermute | solution.py:857
  435.2 11.9 %copy-start.15 = (bf16[2048,1664]{1,0:T(8,128)(2,1)S(1)}, bf16[2048,1664]{1,0:T(8,128)(2,1)}, u32[]{:S(2)}) copy-start(bf16[2048,1664]{1,0:T(8,128)(2,1)} %get-tuple-element.121) | copy-start | bytes 20447236
  460.4 1.5 copy-start.21
  464.7 18.5 %slice-start.2 = ((s8[6815744]{0:T(1024)(128)(4,1)}), s8[4194304]{0:T(1024)(128)(4,1)S(1)}, s32[]{:S(2)}) async-start(s8[6815744]{0:T(1024)(128)(4,1)} %bitcast.68), calls=%async_computation.13 | async-start | bytes 8388608
  464.7 18.5 %slice-start.4 = ((s8[6815744]{0:T(1024)(128)(4,1)}), s8[4194304]{0:T(1024)(128)(4,1)S(1)}, s32[]{:S(2)}) async-start(s8[6815744]{0:T(1024)(128)(4,1)} %bitcast.82), calls=%async_computation.15 | async-start | bytes 8388608
  472.1 11.1 %slice-start.3 = ((s8[6815744]{0:T(1024)(128)(4,1)}), s8[2621440]{0:T(1024)(128)(4,1)S(1)}, s32[]{:S(2)}) async-start(s8[6815744]{0:T(1024)(128)(4,1)} %bitcast.68), calls=%async_computation.14 | async-start | bytes 5242880
  472.1 11.1 %slice-start.5 = ((s8[6815744]{0:T(1024)(128)(4,1)}), s8[2621440]{0:T(1024)(128)(4,1)S(1)}, s32[]{:S(2)}) async-start(s8[6815744]{0:T(1024)(128)(4,1)} %bitcast.82), calls=%async_computation.16 | async-start | bytes 5242880
  481.9 7.2 %slice-start = ((s8[6815744]{0:T(1024)(128)(4,1)}), s8[4194304]{0:T(1024)(128)(4,1)S(1)}, s32[]{:S(2)}) async-start(s8[6815744]{0:T(1024)(128)(4,1)} %bitcast.66), calls=%async_computation.11 | async-start | bytes 8388608
  481.9 7.2 %slice-start.1 = ((s8[6815744]{0:T(1024)(128)(4,1)}), s8[2621440]{0:T(1024)(128)(4,1)S(1)}, s32[]{:S(2)}) async-start(s8[6815744]{0:T(1024)(128)(4,1)} %bitcast.66), calls=%async_computation.12 | async-start | bytes 5242880
  481.9 60.6 %collective-permute-start.6 = (bf16[1024,1024]{1,0:T(8,128)(2,1)}, bf16[1024,1024]{1,0:T(8,128)(2,1)}, u32[]{:S(2)}, u32[]{:S(2)}) collective-permute-start(bf16[1024,1024]{1,0:T(8,128)(2,1)} %get-tuple-element.170), channel_id=1, source_target_pairs={{0,1},{1,0},{2,3},{3,2},{4,5},{5,4},{6,7},{7,6},{8,9},{9,8},{10,11... | collective-permute-start | bytes 6291464 | tf_op jit(solution)/shard_map/ppermute | solution.py:880
  489.1 7.7 %copy-start.19 = (f32[1024]{0:T(1024)S(1)}, f32[1024]{0:T(1024)}, u32[]{:S(2)}) copy-start(f32[1024]{0:T(1024)} %param.36) | copy-start | bytes 12292
  489.1 53.4 %copy-start.1 = (bf16[1024,1024]{1,0:T(8,128)(2,1)S(1)}, bf16[1024,1024]{1,0:T(8,128)(2,1)}, u32[]{:S(2)}) copy-start(bf16[1024,1024]{1,0:T(8,128)(2,1)} %refs_2_.1) | copy-start | bytes 6291460
  489.1 53.4 %copy-start.17 = (f32[1024]{0:T(1024)S(1)}, f32[1024]{0:T(1024)}, u32[]{:S(2)}) copy-start(f32[1024]{0:T(1024)} %copy-done.16) | copy-start | bytes 12292
  496.8 1.2 collective-permute-start.7
  498.0 5.1 collective-permute-start.8
  503.1 4.6 collective-permute-start.9
  507.7 3.9 collective-permute-start.10
  511.6 17.8 %collective-permute-start.11 = (f32[2192]{0:T(1024)S(1)}, f32[2192]{0:T(1024)S(1)}, u32[]{:S(2)}, u32[]{:S(2)}) collective-permute-start(f32[2192]{0:T(1024)S(1)} %add.123), channel_id=1, source_target_pairs={{0,1},{1,0},{2,3},{3,2},{4,5},{5,4},{6,7},{7,6},{8,9},{9,8},{10,11... | collective-permute-start | bytes 26312 | tf_op jit(solution)/shard_map/ppermute | solution.py:857
  512.2 27.3 %collective-permute-start.12 = (bf16[128,1280]{1,0:T(8,128)(2,1)S(1)}, bf16[128,1280]{1,0:T(8,128)(2,1)S(1)}, u32[]{:S(2)}, u32[]{:S(2)}) collective-permute-start(bf16[128,1280]{1,0:T(8,128)(2,1)S(1)} %dynamic-slice_bitcast_fusion), channel_id=1, source_target_pairs={{0,16},{8,24},{16,0},{24,8},{1,17},{9,25},{17,1},{25,9},{2,18},{10... | collective-permute-start | bytes 983048 | tf_op jit(solution)/shard_map/ppermute | solution.py:857
  542.5 4.3 copy-start.4
  542.5 5.4 copy-start.14
  (2 other events, 1.9 us)
Sparse Core Ops, SparseCore 0:
  10.9 67.6 all-gather.3
  82.1 89.6 all-gather.5
  175.3 77.2 all-gather.7
  255.4 59.5 reduce-scatter.6
  347.0 61.4 reduce-scatter.4
  410.7 37.9 reduce-scatter.10
  462.0 98.2 reduce-scatter.8

commit v5 on v4

--- a/solution.py
+++ b/solution.py
@@ -734,7 +734,7 @@
     mix_ref[:, lay.v : lay.g] = v_ref[...]
     mix_ref[:, lay.g : lay.r] = g_ref[...]
     mix_ref[:, lay.r : lay.width] = jnp.zeros((mix_ref.shape[0], 128), BF)
-    mix_ref[:, lay.r : lay.r + r_ref.shape[1]] = r_ref[...]
+    mix_ref[:, lay.r : lay.r + r_ref.shape[0]] = turn(r_ref[...])
 
 
 def pack_mix(lay, w_query, w_key, w_value, w_rates, w_outgate):
@@ -742,7 +742,7 @@
         functools.partial(pack_mix_kernel, lay),
         out_shape=jax.ShapeDtypeStruct((w_query.shape[0], lay.width), BF),
         name="pack_mix",
-    )(w_query, w_key, w_value, w_rates, w_outgate)
+    )(w_query, w_key, w_value, w_rates.T, w_outgate)
 
 
 def pack_kernel(out_ref, gate_ref, up_ref, down_ref, *all_refs):
@@ -829,18 +829,20 @@
     q_ref[...] = own[:, lay.q : lay.k]
     k_ref[...] = own[:, lay.k : lay.v]
     v_ref[...] = own[:, lay.v : lay.g]
-    r_ref[...] = own[:, lay.r : lay.r + nrates]
+    r_ref[...] = own[:, lay.r : lay.width].T[:nrates]
     g_ref[...] = own[:, lay.g : lay.r]
 
 
 def unpack_mix(own, lay, nrates):
     rows = own.shape[0]
     widths = (lay.k - lay.q, lay.v - lay.k, lay.g - lay.v, nrates, lay.r - lay.g)
-    return pl.pallas_call(
+    shapes = [(nrates, rows) if k == 3 else (rows, width) for k, width in enumerate(widths)]
+    query, key, value, rates, outgate = pl.pallas_call(
         functools.partial(unpack_mix_kernel, lay, nrates),
-        out_shape=[jax.ShapeDtypeStruct((rows, width), F32) for width in widths],
+        out_shape=[jax.ShapeDtypeStruct(shape, F32) for shape in shapes],
         name="unpack_mix",
     )(own)
+    return query, key, value, rates.T, outgate
 STEP = 4
 
 
@@ -959,9 +961,12 @@
     dpre = (jnp.zeros((nsq * heads, HEAD, HEAD), F32), jnp.zeros((8, 128), F32))
     back_args = (place_arr, parts, pre, params, gain, *kept, dmixed, heads, STEP)
     *dpre, carry, small = mixer_backward(*back_args, 0, head_steps, dpre)
+    grads_a = column_step(grads_a, 0)
     carry, grads_b, grads_a = lax.optimization_barrier((carry, grads_b, grads_a))
-    own_a = lax.psum_scatter(grads_a, "dz", scatter_dimension=0, tiled=True)
-    grads_b = column_step(grads_b, 0)
+    own_b = lax.psum_scatter(grads_b, "dz", scatter_dimension=0, tiled=True)
+    own_a = column_step(grads_a, 1)
+    for k in range(2, len(bits("dz"))):
+        own_a = column_step(own_a, k)
     *dpre, carry, small = mixer_backward(*back_args, head_steps, steps - head_steps, (carry, small, *dpre))
 
     def back_rows(values, r):
@@ -972,10 +977,7 @@
         return total, jnp.sum(total * first_seq[rows].astype(F32), axis=0)
 
     mix_grads = jnp.concatenate([dot_tn(first_seq, dpre[s]).astype(BF) for s in range(nsq)], axis=0)
-    dpre, mix_grads, grads_b = lax.optimization_barrier((dpre, mix_grads, grads_b))
-    own_b = grads_b
-    for k in range(1, len(bits("dz"))):
-        own_b = column_step(own_b, k)
+    dpre, mix_grads, own_a = lax.optimization_barrier((dpre, mix_grads, own_a))
     own_out, own_gate, own_up, own_down = unpack(own_a, own_b, hw, units)
     mix_own = lax.psum_scatter(mix_grads, ("sq", "dz", "core"), scatter_dimension=0, tiled=True)
     leaving = [back_rows(dpre, r) for r in range(1, parts)]

time: 580 us -> 569 us (0.981)
  waiting for transfers between devices: 149 us -> 140 us
    ppermute x9, waiting for transfers between devices: 52.2 us -> 45.2 us  [trade(): lax.ppermute(values, axis, [(i, i ^ bit) for i in range(lax.axis_size(axi...]
  transfers between devices with their start and end apart: 20 -> 20, of which waited for: 15 -> 13; matrix products, arithmetic and copies ran while one was open for 18% -> 18% of each run, Pallas kernels for 48% -> 49%
where the time goes in v5:
time: 569 us; the launch traced here: 560 us
  Pallas kernels  276 us (49%)
  waiting for transfers between devices  140 us (25%)
  matrix products  52.7 us (9%)
  other arithmetic  37.5 us (7%)
  local copies, waits for them, and re-layouts  24.8 us (4%)
  between operations  14.9 us (3%)
  starting transfers between devices  13.8 us (2%)
    pallas_call x2, Pallas kernels, mixer_backward(): pl.pallas_call(functools.partial(backward_kernel, lay, nsq, heads, nb), g...  82.9 us
    ppermute x4, waiting for transfers between devices, swap(): return lax.ppermute(values, 'sub', [(i, i ^ which) for i in range(parts)])  73.9 us
    pallas_call x1, Pallas kernels, mixer_forward(): pl.pallas_call(functools.partial(forward_kernel, lay, nsq, heads, nb), gr...  51.4 us
    ppermute x9, waiting for transfers between devices, trade(): lax.ppermute(values, axis, [(i, i ^ bit) for i in range(lax.axis_size(axi...  45.2 us
    pallas_call x1, Pallas kernels, feed_forward(): pl.pallas_call(functools.partial(ff_kernel, min(TILE, tok), block, lead,...  39.8 us
    pallas_call x1, Pallas kernels, feed_forward_rest(): pl.pallas_call(functools.partial(ff_rest_kernel, min(TILE, tok), units),...  31.9 us
    dot_general x4, matrix products, dot_nt(): lax.dot_general(left, right, (((1,), (1,)), ((), ())), preferred_element_...  30.9 us
    dot_general x2, matrix products, dot_tn(): lax.dot_general(left, right, (((0,), (0,)), ((), ())), preferred_element_...  21.8 us
  transfers between devices with their start and end apart: 20, of which 13 were waited for; matrix products, arithmetic and copies ran while one was open for 18% of the time, Pallas kernels for 49%

profile of v5, /device:TPU:0, one launch (start us, length us, event | category | flops | bytes accessed | tf_op | source)
XLA Modules:
  0.0 559.7 jit_solution(18162444365887002155)
XLA Ops:
  7.3 2.0 pack_mix.1
  9.3 2.2 pack.1
  12.3 2.1 fusion.9
  15.0 1.9 fusion.3
  16.9 2.9 collective-permute-start
  22.4 43.4 %collective-permute-done = bf16[1024,1024]{1,0:T(8,128)(2,1)} collective-permute-done((bf16[1024,1024]{1,0:T(8,128)(2,1)}, bf16[1024,1024]{1,0:T(8,128)(2,1)}, u32[]{:S(2)}, u32[]{:S(2)}) %collective-permute-start) | collective-permute-done | bytes 2097184 | tf_op jit(solution)/shard_map/ppermute | solution.py:882
  65.8 4.7 pad_maximum_fusion.1.x_ref
  70.5 8.2 %all-gather.4.cloned.1.call-done = bf16[2048,1664]{1,0:T(8,128)(2,1)} async-done(((bf16[128,1664]{1,0:T(8,128)(2,1)}), bf16[2048,1664]{1,0:T(8,128)(2,1)}) %all-gather.4.cloned.1.call-update) | async-done | bytes 6815760 | tf_op jit(solution)/shard_map/all_gather | solution.py:901
  78.6 21.1 %project.1 = (f32[2048,1664]{1,0:T(8,128)}, f32[2048,1664]{1,0:T(8,128)}) custom-call(bf16[2048,1024]{1,0:T(8,128)(2,1)} %pad_maximum_fusion.1.x_ref, bf16[2,1024,1664]{2,1,0:T(8,128)(2,1)} %bitcast.83), custom_call_target="tpu_custom_call" | custom-call | flops 13958643712 | bytes 27262976 | tf_op jit(solution)/shard_map/project/pallas_call | solution.py:787
  99.8 51.4 %mixer_forward.1 = (bf16[2,2048,256]{2,1,0:T(8,128)(2,1)}, bf16[32,4,128,128]{3,2,1,0:T(8,128)(2,1)}, bf16[32,4,128,128]{3,2,1,0:T(8,128)(2,1)}, bf16[32,4,128,1...) custom-call(s32[1]{0:T(128)} %bitcast._, f32[2048,1664]{1,0:T(8,128)} %get-tuple-element.77.refs_0_, ...), custom_call_target="tpu_custom_call" | custom-call | flops 10737418240 | bytes 46137344 | tf_op jit(solution)/shard_map/mixer_forward/pallas_call | solution.py:370
  151.2 2.3 slice.61
  156.2 22.7 %collective-permute-done.1.refs_1_ = bf16[2,1024,256]{2,1,0:T(8,128)(2,1)S(1)} collective-permute-done((bf16[2,1024,256]{2,1,0:T(8,128)(2,1)}, bf16[2,1024,256]{2,1,0:T(8,128)(2,1)S(1)}, u32[]{:S(2)}, u32[]{:S(2)}) %collective-permute-start.1) | collective-permute-done | bytes 1048608 | tf_op jit(solution)/shard_map/ppermute | solution.py:882
  179.0 1.6 copy-done.2
  180.6 1.6 copy-done.5
  182.2 7.5 %join.1 = (f32[1024,1024]{1,0:T(8,128)}, bf16[1024,1024]{1,0:T(8,128)(2,1)S(1)}, bf16[1024,1024]{1,0:T(8,128)(2,1)S(1)}) custom-call(s32[3]{0:T(128)S(1)} %pad_add_fusion.scalars, bf16[2,2048,256]{2,1,0:T(8,128)(2,1)S(1)} %copy-done.2, bf16[2,1024,256]{2,1,0:T(8,128)(2,1)S(1)} %collective-permute-done.1.refs_1_, bf16[1024,1024]{1,0:T(8,128)(2,1)S(1)} %copy-done, ...), custom_call_target="tpu_custom_call" | custom-call | flops 2147483648 | bytes 14680064 | tf_op jit(solution)/shard_map/join/pallas_call | solution.py:472
  192.3 39.8 %feed_forward.1 = (f32[1024,1024]{1,0:T(8,128)}, f32[1024,1024]{1,0:T(8,128)}, bf16[4,512,1152]{2,1,0:T(8,128)(2,1)}, bf16[4,512,1152]{2,1,0:T(8,128)(2,1)}) custom-call(s32[3]{0:T(128)} %copy-done.9, bf16[1024,1024]{1,0:T(8,128)(2,1)} %copy-done.11, bf16[1024,1024]{1,0:T(8,128)(2,1)} %copy-done.6, bf16[4,1024,1408]{2,1,0:T(8,128)(2,1)} %bitcast.62), custom_call_target="tpu_custom_call" | custom-call | flops 28991029248 | bytes 35651584 | tf_op jit(solution)/shard_map/feed_forward/pallas_call | solution.py:558
  232.2 8.2 %collective-permute-done.2 = bf16[4,512,1152]{2,1,0:T(8,128)(2,1)S(1)} collective-permute-done((bf16[4,512,1152]{2,1,0:T(8,128)(2,1)}, bf16[4,512,1152]{2,1,0:T(8,128)(2,1)S(1)}, u32[]{:S(2)}, u32[]{:S(2)}) %collective-permute-start.2) | collective-permute-done | bytes 4718624 | tf_op jit(solution)/shard_map/ppermute | solution.py:859
  240.4 6.0 %add_convert_fusion.1 = bf16[4,512,1152]{2,1,0:T(8,128)(2,1)} fusion(bf16[4,512,1152]{2,1,0:T(8,128)(2,1)S(1)} %collective-permute-done.2, bf16[4,512,1152]{2,1,0:T(8,128)(2,1)} %get-tuple-element.85), kind=kLoop, calls=%fused_computation.5 | loop fusion | flops 9437184 | bytes 14155776 | tf_op jit(solution)/shard_map/convert_element_type | solution.py:870
  246.4 6.2 %all-gather.8.cloned.1.call-done = bf16[4096,1024]{1,0:T(8,128)(2,1)} async-done(((bf16[128,1024]{1,0:T(8,128)(2,1)}), bf16[4096,1024]{1,0:T(8,128)(2,1)}) %all-gather.8.cloned.1.call-update) | async-done | bytes 8388624 | tf_op jit(solution)/shard_map/all_gather | solution.py:904
  252.7 31.9 %feed_forward_rest.1 = (f32[1024,1024]{1,0:T(8,128)}, f32[1024,1024]{1,0:T(8,128)}, bf16[4,1024,320]{2,1,0:T(8,128)(2,1)}, bf16[4,1024,640]{2,1,0:T(8,128)(2,1)}) custom-call(bf16[1024,1024]{1,0:T(8,128)(2,1)} %copy-done.11, bf16[1024,1024]{1,0:T(8,128)(2,1)} %copy-done.6, bf16[4,1024,1024]{2,1,0:T(8,128)(2,1)} %bitcast.82), custom_call_target="tpu_custom_call" | custom-call | flops 16106127360 | bytes 20971520 | tf_op jit(solution)/shard_map/feed_forward_rest/pallas_call | solution.py:596
  284.6 1.6 copy-done.7
  286.2 13.1 %split.1 = (bf16[1024,1024]{1,0:T(8,128)(2,1)}, f32[1024,1024]{1,0:T(8,128)S(1)}, bf16[1024,1024]{1,0:T(8,128)(2,1)S(1)}, f32[1,1024]{1,0:T(1,128)S(1)}, bf16[2,...) custom-call(s32[3]{0:T(128)S(1)} %copy-done.10, f32[1024,1024]{1,0:T(8,128)} %get-tuple-element.81.refs_0_, ...), custom_call_target="tpu_custom_call" | custom-call | flops 2147483648 | bytes 27262976 | tf_op jit(solution)/shard_map/split/pallas_call | solution.py:694
  299.3 2.1 copy-done.3
  304.1 20.1 %rest_grad.1 = (bf16[4,512,1280]{2,1,0:T(8,128)(2,1)}, bf16[4,512,1280]{2,1,0:T(8,128)(2,1)}) custom-call(s32[3]{0:T(128)S(1)} %copy-done.10, bf16[1024,1024]{1,0:T(8,128)(2,1)S(1)} %copy-done.12, bf16[1024,1024]{1,0:T(8,128)(2,1)} %copy-done.6, bf16[1024,1024]{1,0:T(8,128)(2,1)} %copy-done.13, bf16[4,1024,320]{2,1,0:T(8,128)(2,1)} %get-tuple-element.102.hid_ref, ...), custom_call_target="tpu_custom_call" | custom-call | flops 10200547328 | bytes 16777216 | tf_op jit(solution)/shard_map/rest_grad/pallas_call | solution.py:639
  324.2 7.8 %collective-permute-done.3 = bf16[2,1024,256]{2,1,0:T(8,128)(2,1)S(1)} collective-permute-done((bf16[2,1024,256]{2,1,0:T(8,128)(2,1)S(1)}, bf16[2,1024,256]{2,1,0:T(8,128)(2,1)S(1)}, u32[]{:S(2)}, u32[]{:S(2)}) %collective-permute-start.3) | collective-permute-done | bytes 1048608 | tf_op jit(solution)/shard_map/ppermute | solution.py:882
  333.4 7.4 %collective-permute-done.4 = bf16[4,512,1280]{2,1,0:T(8,128)(2,1)S(1)} collective-permute-done((bf16[4,512,1280]{2,1,0:T(8,128)(2,1)}, bf16[4,512,1280]{2,1,0:T(8,128)(2,1)S(1)}, u32[]{:S(2)}, u32[]{:S(2)}) %collective-permute-start.4) | collective-permute-done | bytes 5242912 | tf_op jit(solution)/shard_map/ppermute | solution.py:859
  340.9 6.0 %add_convert_fusion = bf16[4,512,1280]{2,1,0:T(8,128)(2,1)} fusion(bf16[4,512,1280]{2,1,0:T(8,128)(2,1)S(1)} %collective-permute-done.4, bf16[4,512,1280]{2,1,0:T(8,128)(2,1)} %get-tuple-element.107), kind=kLoop, calls=%fused_computation.4 | loop fusion | flops 10485760 | bytes 15728640 | tf_op jit(solution)/shard_map/convert_element_type | solution.py:870
  351.2 60.2 %mixer_backward.2 = (bf16[2048,1664]{1,0:T(8,128)(2,1)}, bf16[2048,1664]{1,0:T(8,128)(2,1)}, f32[4,128,128]{2,1,0:T(8,128)}, f32[8,128]{1,0:T(8,128)}) custom-call(s32[1]{0:T(128)} %bitcast._, f32[2048,1664]{1,0:T(8,128)} %get-tuple-element.77.refs_0_, f32[2048,1664]{1,0:T(8,128)} %get-tuple-element.78.refs_1_, f32[2,128]{1,0:T(2,128)} %pad_maximum_fusion.5.refs_2_, ...), custom_call_target="tpu_custom_call" | custom-call | flops 10468982784 | bytes 47972352 | tf_op jit(solution)/shard_map/mixer_backward/pallas_call | solution.py:415
  412.4 2.0 collective-permute-start.6
  414.5 22.8 %mixer_backward.3 = (bf16[2048,1664]{1,0:T(8,128)(2,1)}, bf16[2048,1664]{1,0:T(8,128)(2,1)}, f32[4,128,128]{2,1,0:T(8,128)}, f32[8,128]{1,0:T(8,128)}) custom-call(s32[1]{0:T(128)} %bitcast._, f32[2048,1664]{1,0:T(8,128)} %get-tuple-element.77.refs_0_, f32[2048,1664]{1,0:T(8,128)} %get-tuple-element.78.refs_1_, ...), custom_call_target="tpu_custom_call", output_to_operand_aliasing={{0}: (16, {}), {1}: (17, {})} | custom-call | flops 3489660928 | bytes 15990784 | tf_op jit(solution)/shard_map/mixer_backward/pallas_call | solution.py:415
  437.3 11.8 %convolution_convert_fusion.1 = bf16[1024,1664]{1,0:T(8,128)(2,1)S(1)} fusion(bf16[2048,1664]{1,0:T(8,128)(2,1)} %get-tuple-element.120, bf16[1024,1024]{1,0:T(8,128)(2,1)} %collective-permute-done, bf16[1024,1024]{1,0:T(8,128)(2,1)} %fusion.3), kind=kOutput, calls=%fused_computation.24 | convolution fusion | flops 6989414400 | bytes 14417920 | tf_op jit(solution)/shard_map/dot_general | solution.py:30
  449.2 10.0 %convolution_convert_fusion = bf16[1024,1664]{1,0:T(8,128)(2,1)S(1)} fusion(bf16[2048,1664]{1,0:T(8,128)(2,1)S(1)} %copy-done.15, bf16[1024,1024]{1,0:T(8,128)(2,1)} %collective-permute-done, bf16[1024,1024]{1,0:T(8,128)(2,1)} %fusion.3), kind=kOutput, calls=%fused_computation.23 | convolution fusion | flops 6989414400 | bytes 14417920 | tf_op jit(solution)/shard_map/dot_general | solution.py:30
  459.2 3.3 pad_maximum_fusion
  462.5 1.8 fusion.33.a_ref
  467.1 7.6 %fusion.10 = f32[1024,1024]{1,0:T(8,128)S(1)} fusion(bf16[2048,1664]{1,0:T(8,128)(2,1)} %get-tuple-element.121, bf16[2048,1664]{1,0:T(8,128)(2,1)} %all-gather.4.cloned.1.call-done), kind=kOutput, calls=%fused_computation.25 | convolution fusion | flops 3489660928 | bytes 11010048 | tf_op jit(solution)/shard_map/dot_general | solution.py:26
  474.7 9.8 %fusion.39 = (bf16[1024,1024]{1,0:T(8,128)(2,1)}, f32[1024]{0:T(1024)S(1)}) fusion(bf16[1024,1024]{1,0:T(8,128)(2,1)} %collective-permute-done, f32[1024,1024]{1,0:T(8,128)S(1)} %fusion.10, bf16[2048,1664]{1,0:T(8,128)(2,1)} %all-gather.4.cloned.1.call-done, bf16[2048,1664]{1,0:T(8,128)(2,1)} %get-tuple-element.120), kind=kOutput, calls=%fused_computation.73 | convolution fusion | flops 3494902784 | bytes 15208448 | tf_op jit(solution)/shard_map/dot_general | solution.py:26
  484.6 5.8 %fusion.14 = f32[1024,1024]{1,0:T(8,128)} fusion(bf16[2048,1664]{1,0:T(8,128)(2,1)S(1)} %bitcast.69, bf16[2048,1664]{1,0:T(8,128)(2,1)S(1)} %bitcast.85), kind=kOutput, calls=%fused_computation.29 | convolution fusion | flops 3489660928 | bytes 11010048 | tf_op jit(solution)/shard_map/dot_general | solution.py:26
  490.5 7.7 %multiply_reduce_fusion.1 = (f32[1024]{0:T(1024)S(1)}, f32[1024,1024]{1,0:T(8,128)}) fusion(bf16[1024,1024]{1,0:T(8,128)(2,1)} %fusion.3, f32[1024,1024]{1,0:T(8,128)} %fusion.14, bf16[2048,1664]{1,0:T(8,128)(2,1)S(1)} %bitcast.85, bf16[2048,1664]{1,0:T(8,128)(2,1)S(1)} %bitcast.67), kind=kOutput, calls=%fused_computation.22 | convolution fusion | flops 3493854208 | bytes 17305600 | tf_op jit(solution)/shard_map/dot_general | solution.py:26
  499.9 4.2 collective-permute-done.9
  504.1 5.0 collective-permute-done.10
  509.1 2.0 collective-permute-start.11
  511.2 1.8 collective-permute-done.11
  514.4 17.4 %collective-permute-done.12 = f32[2192]{0:T(1024)S(1)} collective-permute-done((f32[2192]{0:T(1024)S(1)}, f32[2192]{0:T(1024)S(1)}, u32[]{:S(2)}, u32[]{:S(2)}) %collective-permute-start.12) | collective-permute-done | bytes 8800 | tf_op jit(solution)/shard_map/ppermute | solution.py:859
  533.5 4.2 fusion.4
  538.9 3.9 fusion.8
  542.8 2.2 unpack.1
  545.0 5.4 reduce-scatter.9.cloned.1.call-done.own_ref
  550.5 1.9 unpack_mix.1
  (140 shorter events, 28.1 us)
Async XLA Ops:
  7.2 7.8 %copy-start = (bf16[1024,1024]{1,0:T(8,128)(2,1)S(1)}, bf16[1024,1024]{1,0:T(8,128)(2,1)}, u32[]{:S(2)}) copy-start(bf16[1024,1024]{1,0:T(8,128)(2,1)} %refs_2_.1) | copy-start | bytes 6291460
  7.2 7.8 %copy-start.19 = (f32[1024]{0:T(1024)S(1)}, f32[1024]{0:T(1024)}, u32[]{:S(2)}) copy-start(f32[1024]{0:T(1024)} %param.36) | copy-start | bytes 12292
  7.2 71.4 %all-gather.4.cloned.1.call-start = ((), (), s32[]{:S(2)}) async-start(), calls=%async_computation.4 | async-start | bytes 7241728 | tf_op jit(solution)/shard_map/all_gather | solution.py:901
  9.3 10.6 %copy-start.23 = (f32[8]{0:T(128)S(1)}, f32[8]{0:T(128)}, u32[]{:S(2)}) copy-start(f32[8]{0:T(128)} %param.39) | copy-start | bytes 100
  9.3 10.6 %copy-start.21 = (f32[8]{0:T(128)S(1)}, f32[8]{0:T(128)}, u32[]{:S(2)}) copy-start(f32[8]{0:T(128)} %param.40) | copy-start | bytes 100
  9.3 169.7 %all-gather.6.cloned.1.call-start = ((), (), s32[]{:S(2)}) async-start(), calls=%async_computation.5 | async-start | bytes 11894784 | tf_op jit(solution)/shard_map/all_gather | solution.py:904
  11.6 241.0 %all-gather.8.cloned.1.call-start = ((), (), s32[]{:S(2)}) async-start(), calls=%async_computation.6 | async-start | bytes 8650752 | tf_op jit(solution)/shard_map/all_gather | solution.py:904
  12.3 334.7 %reduce-scatter.7.cloned.1.call-start = ((), (), s32[]{:S(2)}) async-start(), calls=%async_computation.8 | async-start | bytes 5898240 | tf_op jit(solution)/shard_map/reduce_scatter | solution.py:939
  16.9 48.9 %collective-permute-start = (bf16[1024,1024]{1,0:T(8,128)(2,1)}, bf16[1024,1024]{1,0:T(8,128)(2,1)}, u32[]{:S(2)}, u32[]{:S(2)}) collective-permute-start(bf16[1024,1024]{1,0:T(8,128)(2,1)} %fusion.3), channel_id=1, source_target_pairs={{0,1},{1,0},{2,3},{3,2},{4,5},{5,4},{6,7},{7,6},{8,9},{9,8},{10,11... | collective-permute-start | bytes 6291464 | tf_op jit(solution)/shard_map/ppermute | solution.py:882
  99.8 55.1 %copy-start.24 = (s32[2]{0:T(128)S(1)}, s32[2]{0:T(128)}, u32[]{:S(2)}) copy-start(s32[2]{0:T(128)} %param.34) | copy-start | bytes 28
  99.8 79.2 %copy-start.8 = (f32[1024]{0:T(1024)S(1)}, f32[1024]{0:T(1024)}, u32[]{:S(2)}) copy-start(f32[1024]{0:T(1024)} %param.37) | copy-start | bytes 12292
  153.4 25.5 %collective-permute-start.1 = (bf16[2,1024,256]{2,1,0:T(8,128)(2,1)}, bf16[2,1024,256]{2,1,0:T(8,128)(2,1)S(1)}, u32[]{:S(2)}, u32[]{:S(2)}) collective-permute-start(bf16[2,1024,256]{2,1,0:T(8,128)(2,1)} %slice.61), channel_id=1, source_target_pairs={{0,1},{1,0},{2,3},{3,2},{4,5},{5,4},{6,7},{7,6},{8,9},{9,8},{10,11... | collective-permute-start | bytes 3145736 | tf_op jit(solution)/shard_map/ppermute | solution.py:882
  156.2 33.4 %copy-start.9 = (s32[3]{0:T(128)}, s32[3]{0:T(128)S(1)}, u32[]{:S(2)}) copy-start(s32[3]{0:T(128)S(1)} %pad_add_fusion.scalars) | copy-start | bytes 40
  179.0 1.6 copy-start.2
  180.6 1.6 copy-start.5
  189.7 1.3 copy-start.6
  232.2 8.2 %collective-permute-start.2 = (bf16[4,512,1152]{2,1,0:T(8,128)(2,1)}, bf16[4,512,1152]{2,1,0:T(8,128)(2,1)S(1)}, u32[]{:S(2)}, u32[]{:S(2)}) collective-permute-start(bf16[4,512,1152]{2,1,0:T(8,128)(2,1)} %get-tuple-element.86), channel_id=1, source_target_pairs={{0,4},{4,0},{1,5},{5,1},{2,6},{6,2},{3,7},{7,3},{8,12},{12,8},{9,1... | collective-permute-start | bytes 14155784 | tf_op jit(solution)/shard_map/ppermute | solution.py:859
  252.6 31.9 %copy-start.10 = (s32[3]{0:T(128)S(1)}, s32[3]{0:T(128)}, u32[]{:S(2)}) copy-start(s32[3]{0:T(128)} %copy-done.9) | copy-start | bytes 40
  252.6 159.0 %reduce-scatter.5.cloned.1.call-start = ((), (), s32[]{:S(2)}) async-start(), calls=%async_computation.7 | async-start | bytes 6553600 | tf_op jit(solution)/shard_map/reduce_scatter | solution.py:939
  284.6 1.6 copy-start.7
  286.1 18.0 %copy-start.12 = (bf16[1024,1024]{1,0:T(8,128)(2,1)S(1)}, bf16[1024,1024]{1,0:T(8,128)(2,1)}, u32[]{:S(2)}) copy-start(bf16[1024,1024]{1,0:T(8,128)(2,1)} %copy-done.11) | copy-start | bytes 6291460
  299.3 2.1 copy-start.3
  302.7 29.3 %collective-permute-start.3 = (bf16[2,1024,256]{2,1,0:T(8,128)(2,1)S(1)}, bf16[2,1024,256]{2,1,0:T(8,128)(2,1)S(1)}, u32[]{:S(2)}, u32[]{:S(2)}) collective-permute-start(bf16[2,1024,256]{2,1,0:T(8,128)(2,1)S(1)} %get-tuple-element.100), channel_id=1, source_target_pairs={{0,1},{1,0},{2,3},{3,2},{4,5},{5,4},{6,7},{7,6},{8,9},{9,8},{10,11... | collective-permute-start | bytes 3145736 | tf_op jit(solution)/shard_map/ppermute | solution.py:882
  332.0 8.9 %collective-permute-start.4 = (bf16[4,512,1280]{2,1,0:T(8,128)(2,1)}, bf16[4,512,1280]{2,1,0:T(8,128)(2,1)S(1)}, u32[]{:S(2)}, u32[]{:S(2)}) collective-permute-start(bf16[4,512,1280]{2,1,0:T(8,128)(2,1)} %get-tuple-element.108), channel_id=1, source_target_pairs={{0,4},{4,0},{1,5},{5,1},{2,6},{6,2},{3,7},{7,3},{8,12},{12,8},{9,1... | collective-permute-start | bytes 15728648 | tf_op jit(solution)/shard_map/ppermute | solution.py:859
  346.9 195.9 %reduce-scatter.11.cloned.1.call-start = ((), (), s32[]{:S(2)}) async-start(), calls=%async_computation.10 | async-start | bytes 1638400 | tf_op jit(solution)/shard_map/reduce_scatter | solution.py:966
  348.3 63.0 %collective-permute-start.5 = (bf16[256,1152]{1,0:T(8,128)(2,1)S(1)}, bf16[256,1152]{1,0:T(8,128)(2,1)S(1)}, u32[]{:S(2)}, u32[]{:S(2)}) collective-permute-start(bf16[256,1152]{1,0:T(8,128)(2,1)S(1)} %bitcast.73), channel_id=1, source_target_pairs={{0,8},{8,0},{16,24},{24,16},{1,9},{9,1},{17,25},{25,17},{2,10},{10... | collective-permute-start | bytes 1769480 | tf_op jit(solution)/shard_map/ppermute | solution.py:859
  411.5 25.8 %copy-start.16 = (bf16[256,1152]{1,0:T(8,128)(2,1)}, bf16[256,1152]{1,0:T(8,128)(2,1)S(1)}, u32[]{:S(2)}) copy-start(bf16[256,1152]{1,0:T(8,128)(2,1)S(1)} %fusion.32) | copy-start | bytes 1769476
  412.4 50.1 %collective-permute-start.6 = (bf16[128,1152]{1,0:T(8,128)(2,1)}, bf16[128,1152]{1,0:T(8,128)(2,1)}, u32[]{:S(2)}, u32[]{:S(2)}) collective-permute-start(bf16[128,1152]{1,0:T(8,128)(2,1)} %dynamic-slice_bitcast_fusion), channel_id=1, source_target_pairs={{0,16},{8,24},{16,0},{24,8},{1,17},{9,25},{17,1},{25,9},{2,18},{10... | collective-permute-start | bytes 884744 | tf_op jit(solution)/shard_map/ppermute | solution.py:859
  414.5 136.0 %reduce-scatter.9.cloned.1.call-start = ((), (), s32[]{:S(2)}) async-start(), calls=%async_computation.9 | async-start | bytes 7241728 | tf_op jit(solution)/shard_map/reduce_scatter | solution.py:982
  437.3 11.9 %copy-start.15 = (bf16[2048,1664]{1,0:T(8,128)(2,1)S(1)}, bf16[2048,1664]{1,0:T(8,128)(2,1)}, u32[]{:S(2)}) copy-start(bf16[2048,1664]{1,0:T(8,128)(2,1)} %get-tuple-element.121) | copy-start | bytes 20447236
  462.5 1.9 copy-start.22
  467.1 17.5 %slice-start.2 = ((s8[6815744]{0:T(1024)(128)(4,1)}), s8[4194304]{0:T(1024)(128)(4,1)S(1)}, s32[]{:S(2)}) async-start(s8[6815744]{0:T(1024)(128)(4,1)} %bitcast.68), calls=%async_computation.13 | async-start | bytes 8388608
  467.1 17.5 %slice-start.4 = ((s8[6815744]{0:T(1024)(128)(4,1)}), s8[4194304]{0:T(1024)(128)(4,1)S(1)}, s32[]{:S(2)}) async-start(s8[6815744]{0:T(1024)(128)(4,1)} %bitcast.84), calls=%async_computation.15 | async-start | bytes 8388608
  474.7 9.9 %slice-start.3 = ((s8[6815744]{0:T(1024)(128)(4,1)}), s8[2621440]{0:T(1024)(128)(4,1)S(1)}, s32[]{:S(2)}) async-start(s8[6815744]{0:T(1024)(128)(4,1)} %bitcast.68), calls=%async_computation.14 | async-start | bytes 5242880
  474.7 9.9 %slice-start.5 = ((s8[6815744]{0:T(1024)(128)(4,1)}), s8[2621440]{0:T(1024)(128)(4,1)S(1)}, s32[]{:S(2)}) async-start(s8[6815744]{0:T(1024)(128)(4,1)} %bitcast.84), calls=%async_computation.16 | async-start | bytes 5242880
  484.5 5.9 %slice-start = ((s8[6815744]{0:T(1024)(128)(4,1)}), s8[4194304]{0:T(1024)(128)(4,1)S(1)}, s32[]{:S(2)}) async-start(s8[6815744]{0:T(1024)(128)(4,1)} %bitcast.66), calls=%async_computation.11 | async-start | bytes 8388608
  484.5 5.9 %slice-start.1 = ((s8[6815744]{0:T(1024)(128)(4,1)}), s8[2621440]{0:T(1024)(128)(4,1)S(1)}, s32[]{:S(2)}) async-start(s8[6815744]{0:T(1024)(128)(4,1)} %bitcast.66), calls=%async_computation.12 | async-start | bytes 5242880
  484.5 49.0 %collective-permute-start.7 = (bf16[1024,1024]{1,0:T(8,128)(2,1)}, bf16[1024,1024]{1,0:T(8,128)(2,1)}, u32[]{:S(2)}, u32[]{:S(2)}) collective-permute-start(bf16[1024,1024]{1,0:T(8,128)(2,1)} %get-tuple-element.138), channel_id=1, source_target_pairs={{0,1},{1,0},{2,3},{3,2},{4,5},{5,4},{6,7},{7,6},{8,9},{9,8},{10,11... | collective-permute-start | bytes 6291464 | tf_op jit(solution)/shard_map/ppermute | solution.py:882
  490.4 7.8 %copy-start.20 = (f32[1024]{0:T(1024)S(1)}, f32[1024]{0:T(1024)}, u32[]{:S(2)}) copy-start(f32[1024]{0:T(1024)} %param.36) | copy-start | bytes 12292
  490.5 43.1 %copy-start.1 = (bf16[1024,1024]{1,0:T(8,128)(2,1)S(1)}, bf16[1024,1024]{1,0:T(8,128)(2,1)}, u32[]{:S(2)}) copy-start(bf16[1024,1024]{1,0:T(8,128)(2,1)} %refs_2_.1) | copy-start | bytes 6291460
  490.5 43.1 %copy-start.18 = (f32[1024]{0:T(1024)S(1)}, f32[1024]{0:T(1024)}, u32[]{:S(2)}) copy-start(f32[1024]{0:T(1024)} %copy-done.17) | copy-start | bytes 12292
  498.3 1.2 collective-permute-start.8
  499.5 4.6 collective-permute-start.9
  504.1 5.0 collective-permute-start.10
  509.1 3.8 collective-permute-start.11
  513.0 18.8 %collective-permute-start.12 = (f32[2192]{0:T(1024)S(1)}, f32[2192]{0:T(1024)S(1)}, u32[]{:S(2)}, u32[]{:S(2)}) collective-permute-start(f32[2192]{0:T(1024)S(1)} %add.126), channel_id=1, source_target_pairs={{0,1},{1,0},{2,3},{3,2},{4,5},{5,4},{6,7},{7,6},{8,9},{9,8},{10,11... | collective-permute-start | bytes 26312 | tf_op jit(solution)/shard_map/ppermute | solution.py:859
  533.5 4.2 copy-start.4
  533.5 5.3 copy-start.14
  (3 other events, 3.2 us)
Sparse Core Ops, SparseCore 0:
  10.9 67.6 all-gather.3
  82.1 89.5 all-gather.5
  175.2 77.3 all-gather.7
  255.4 59.5 reduce-scatter.6
  347.0 61.4 reduce-scatter.4
  414.6 34.4 reduce-scatter.10
  464.5 85.9 reduce-scatter.8
